TPU v7x, 32 devices: a whole 2x2x4 slice. The times are simulated.
32 devices in a mesh: row: 1, col: 16 (over z, y, core), seg: 2 (over x).
Axes of the slice: x: 2, y: 2, z: 4, core: 2. Of those that a mesh axis runs over, the one named last changes fastest.
Arguments:
- traces: bfloat16 [8, 128, 1024], P('seg', ('row', 'col')), may hold values from -600 to 600, as said below
- valid: int32 [8, 128], P('seg', ('row', 'col')), may hold values 0 or 1
Outputs:
- correlation: float32 [33, 1, 128, 128], P(None, None, ('col', 'seg'), 'row')
Inputs may be any that keep to these rules, and one draw needn't show every extreme that they name: `traces`: samples of a common wavefield delayed by up to 32 samples per station plus noise, scaled per station.
All inputs are finite; a program needn't handle non-finite values. No bound on the sum of `valid` on one device may be relied on, other than what follows from the above.
Results may differ from a plain program's by a relative error of at most 0.002.
Values may be sent and summed in bfloat16 or wider, within the bound.
No kernel may reach another device: no remote copies, remote signals or barrier semaphores. Data moves between devices by JAX's collectives and lax.ppermute only.
A program may use at most 64 MiB of HBM per device.

v0:
```python
import functools
import math

import jax
import jax.numpy as jnp
import numpy as np
from jax import lax
from jax.experimental import pallas as pl
from jax.experimental.pallas import tpu as pltpu
from jax.sharding import PartitionSpec as P

MAXLAG = 16
LAGSET = 3
VMEM = pl.BlockSpec(memory_space=pltpu.VMEM)
SMEM = pl.BlockSpec(memory_space=pltpu.SMEM)
HBM = pl.BlockSpec(memory_space=pltpu.HBM)


def grant(mib):
    return pltpu.CompilerParams(vmem_limit_bytes=mib * 2**20)


def make_tables(length, max_shift):
    bins = jnp.arange(length // 2, dtype=jnp.int32)
    samples = jnp.arange(length, dtype=jnp.int32)
    product = samples[:, None] * bins[None, :] % length
    angle = 2.0 * math.pi / length * product.astype(jnp.float32)
    dft_table = jnp.concatenate([jnp.cos(angle), -jnp.sin(angle)], axis=1).astype(jnp.bfloat16)
    shifts = jnp.arange(2 * max_shift + 1, dtype=jnp.int32) - max_shift
    lag_prod = shifts[:, None] * bins[None, :] % length
    lag_angle = 2.0 * math.pi / length * lag_prod.astype(jnp.float32)
    return (dft_table, jnp.cos(lag_angle), jnp.sin(lag_angle))


def whiten(traces, valid, dft_table):
    length = traces.shape[2]
    half = length // 2
    flat = traces.reshape(-1, length)
    spectrum = jnp.dot(flat, dft_table, preferred_element_type=jnp.float32)
    spectrum = spectrum.reshape(traces.shape[0], traces.shape[1], length)
    real_part = spectrum[..., :half]
    imag_part = spectrum[..., half:]
    power = real_part * real_part + imag_part * imag_part
    level = jnp.mean(power, axis=-1, keepdims=True)
    factor = lax.rsqrt(power + 0.1 * level + 1e-05) * valid[..., None].astype(jnp.float32)
    return jnp.concatenate([real_part * factor, imag_part * factor], axis=-1).astype(jnp.bfloat16)


def lag_sums(first_set, second_set, cosines, sines, group_size):
    half = first_set.shape[2] // 2
    lag_count = cosines.shape[0]
    real_part = second_set[..., :half].astype(jnp.float32)
    imag_part = second_set[..., half:].astype(jnp.float32)

    def one_group(group):
        cosine = lax.dynamic_slice_in_dim(cosines, group * group_size, group_size, 0)[
            :, None, None, :
        ]
        sine = lax.dynamic_slice_in_dim(sines, group * group_size, group_size, 0)[:, None, None, :]
        first = real_part[None] * cosine + imag_part[None] * sine
        second = imag_part[None] * cosine - real_part[None] * sine
        rotated = jnp.concatenate([first, second], axis=-1).astype(jnp.bfloat16)
        return jnp.einsum("gsbk,sak->gba", rotated, first_set, preferred_element_type=jnp.float32)

    result = lax.map(one_group, jnp.arange(lag_count // group_size, dtype=jnp.int32))
    return result.reshape(lag_count, second_set.shape[1], first_set.shape[1])


def general_device(traces, valid):
    length = traces.shape[2]
    dft_table, cosines, sines = make_tables(length, MAXLAG)
    whitened = whiten(traces, valid, dft_table)
    first_set = lax.all_gather(whitened, "col", axis=1, tiled=True)
    second_set = lax.all_gather(whitened, "row", axis=1, tiled=True)
    groups_row = lax.axis_size("row")
    seg_count = lax.axis_size("seg")
    segments_all = whitened.shape[0] * seg_count
    scale = 1.0 / math.sqrt(segments_all * (length // 2))
    own_count = whitened.shape[1]
    partial_value = lag_sums(first_set, second_set, cosines, sines, LAGSET)
    partial_value = partial_value.reshape(
        partial_value.shape[0], groups_row, own_count, partial_value.shape[2]
    )
    summed = lax.psum_scatter(partial_value, "seg", scatter_dimension=2, tiled=True)
    return summed * scale


def bin_order(length):
    return np.concatenate([np.arange(r, length // 2, 4) for r in range(4)])


def quarter_table(length):
    product = np.arange(length // 4)[:, None] * bin_order(length)[None, :] % length
    angle = 2.0 * np.pi / length * product
    return np.concatenate([np.cos(angle), -np.sin(angle)], axis=1).astype(jnp.bfloat16)


def lag_tables(length, max_shift, copies, rows):
    shifts = np.arange(2 * max_shift + 1) - max_shift
    product = shifts[:, None] * bin_order(length)[None, :] % length
    angle = 2.0 * np.pi / length * product
    out = []
    for table in (np.cos(angle), np.sin(angle)):
        full = np.zeros((rows, length // 2), np.float32)
        full[: copies * len(shifts)] = np.repeat(table, copies, axis=0)
        out.append(full)
    return out


def whiten_kernel(
    x_in, v_in, t_in, c_in, s_in, w_ref, c_out, s_out, x_ref, v_ref, t_ref, sems
):
    pairs = ((x_in, x_ref), (t_in, t_ref), (v_in, v_ref), (c_in, c_out), (s_in, s_out))
    copies = [pltpu.make_async_copy(a, b, sems.at[i]) for i, (a, b) in enumerate(pairs)]
    for copy in copies:
        copy.start()
    segs, own, length = x_ref.shape
    for copy in copies[:3]:
        copy.wait()
    quarter, half = length // 4, length // 2
    rows, group = segs * own, half // 4
    stacked = jnp.concatenate(
        [x_ref[:, :, q * quarter : (q + 1) * quarter].reshape(rows, quarter) for q in range(4)],
        axis=0,
    )
    z = jnp.dot(stacked, t_ref[...], preferred_element_type=jnp.float32)

    def piece(q, r, imag):
        start = r * group + (half if imag else 0)
        return z[q * rows : (q + 1) * rows, start : start + group]

    real, imag = [], []
    for r in range(4):
        re, im = piece(0, r, False), piece(0, r, True)
        for q in range(1, 4):
            a, b = piece(q, r, False), piece(q, r, True)
            turn = (q * r) % 4
            if turn == 0:
                re, im = re + a, im + b
            elif turn == 1:
                re, im = re + b, im - a
            elif turn == 2:
                re, im = re - a, im - b
            else:
                re, im = re - b, im + a
        real.append(re)
        imag.append(im)
    power = [re * re + im * im for re, im in zip(real, imag)]
    level = jnp.sum(power[0] + power[1] + power[2] + power[3], axis=-1, keepdims=True) / half
    flags = v_ref[...].astype(jnp.float32)
    eye = lax.broadcasted_iota(jnp.int32, (own, own), 0) == lax.broadcasted_iota(
        jnp.int32, (own, own), 1
    )
    column = jnp.concatenate(
        [
            jnp.sum(
                jnp.where(eye, jnp.broadcast_to(flags[s : s + 1], (own, own)), 0.0),
                axis=-1,
                keepdims=True,
            )
            for s in range(segs)
        ],
        axis=0,
    )
    for r in range(4):
        factor = lax.rsqrt(power[r] + 0.1 * level + 1e-05) * column
        for base, part in ((0, real[r]), (half, imag[r])):
            value = (part * factor).astype(jnp.bfloat16).reshape(segs, own, group)
            w_ref[:, :, base + r * group : base + (r + 1) * group] = value
    for copy in copies[3:]:
        copy.wait()


def rotate_kernel(seg_ref, w_ref, c_ref, s_ref, r_ref):
    segs, own, length = w_ref.shape
    half, part = length // 2, own // 2
    rows = c_ref.shape[0]
    first_half = seg_ref[0] == 0
    for seg in range(segs):
        w = w_ref[seg].astype(jnp.float32)
        low, high = w[:part], w[part:]
        keep = jnp.where(first_half, low, high)
        send = jnp.where(first_half, high, low)
        keep2 = jnp.concatenate([keep, keep], axis=0)
        send2 = jnp.concatenate([send, send], axis=0)
        for start in range(0, 2 * rows, 2 * own):
            pieces = []
            for row in (start, start + own):
                w2 = keep2 if row < rows else send2
                at = row % rows
                pieces.append((w2[:, :half], w2[:, half:], at))
            top, bottom = [], []
            for re, im, at in pieces:
                c, s = c_ref[at : at + own], s_ref[at : at + own]
                top.append(re * c + im * s)
                bottom.append(im * c - re * s)
            stop = start + 2 * own
            r_ref[seg, start:stop, :half] = jnp.concatenate(top, axis=0).astype(jnp.bfloat16)
            r_ref[seg, start:stop, half:] = jnp.concatenate(bottom, axis=0).astype(jnp.bfloat16)


def correlate_kernel(*refs):
    r_ref, keep_ref, send_ref = refs[0], refs[-2], refs[-1]
    blocks = refs[1:-2]
    rows = keep_ref.shape[0]
    total = None
    for seg in range(r_ref.shape[0]):
        first = jnp.concatenate([b[seg] for b in blocks], axis=0)
        term = lax.dot_general(
            r_ref[seg], first, (((1,), (1,)), ((), ())), preferred_element_type=jnp.float32
        )
        total = term if total is None else total + term
    keep_ref[...] = total[:rows]
    send_ref[...] = total[rows:]


def finish_kernel(scale, own, me_ref, keep_ref, got_ref, out_ref):
    lags, part, lanes = out_ref.shape
    value = (keep_ref[: lags * part] + got_ref[: lags * part]) * scale
    lane = lax.broadcasted_iota(jnp.int32, value.shape, 1)
    width = own
    bit = 1
    while width < lanes:
        up = pltpu.roll(value, width, 1)
        down = pltpu.roll(value, lanes - width, 1)
        swapped = jnp.where((lane & width) != 0, up, down)
        value = jnp.where((me_ref[0] & bit) != 0, swapped, value)
        width, bit = 2 * width, 2 * bit
    for lag in range(lags):
        out_ref[lag] = value[lag * part : (lag + 1) * part]


def gather_plan(col):
    bits = [1 << i for i in reversed(range(col.bit_length() - 1))]
    far, close, last = bits[:-3], bits[-3:-1], bits[-1:]
    held, steps = [0], []
    for bit in far:
        steps += [(m | bit, m, bit) for m in held]
        held += [m | bit for m in held]
    near = [sum(close)] * (len(close) > 1) + close
    for m in list(held):
        steps += [(m | d, m, d) for d in near]
        held += [m | d for d in near]
    for bit in last:
        steps += [(m | bit, m, bit) for m in held]
    return steps


def fast_device(traces, valid):
    return fast_body(traces, valid)


def fast_body(traces, valid):
    segs, own, length = traces.shape
    col = lax.axis_size("col")
    lags, part, lanes = 2 * MAXLAG + 1, own // 2, own * col
    half = length // 2
    rows = -(-lags * part // own) * own
    me = lax.axis_index("col").astype(jnp.int32).reshape(1)
    seg_index = lax.axis_index("seg").astype(jnp.int32).reshape(1)
    scale = 1.0 / math.sqrt(segs * lax.axis_size("seg") * half)

    table = quarter_table(length)
    lag_cos, lag_sin = lag_tables(length, MAXLAG, part, rows)
    whitened, cosines, sines = pl.pallas_call(
        whiten_kernel,
        out_shape=[
            jax.ShapeDtypeStruct(traces.shape, jnp.bfloat16),
            jax.ShapeDtypeStruct(lag_cos.shape, jnp.float32),
            jax.ShapeDtypeStruct(lag_sin.shape, jnp.float32),
        ],
        in_specs=[HBM] * 5,
        out_specs=[VMEM] * 3,
        scratch_shapes=[
            pltpu.VMEM(traces.shape, traces.dtype),
            pltpu.VMEM(valid.shape, valid.dtype),
            pltpu.VMEM(table.shape, table.dtype),
            pltpu.SemaphoreType.DMA((5,)),
        ],
        compiler_params=grant(4),
    )(
        *[
            pltpu.with_memory_space_constraint(jnp.asarray(t), pltpu.HBM)
            for t in (traces, valid, table, lag_cos, lag_sin)
        ]
    )

    blocks = {0: whitened}
    for block, held, distance in gather_plan(col):
        blocks[block] = lax.ppermute(blocks[held], "col", [(i, i ^ distance) for i in range(col)])

    rotated = pl.pallas_call(
        rotate_kernel,
        out_shape=jax.ShapeDtypeStruct((segs, 2 * rows, length), jnp.bfloat16),
        in_specs=[SMEM, VMEM, VMEM, VMEM],
        out_specs=VMEM,
        compiler_params=grant(8),
        cost_estimate=pl.CostEstimate(
            flops=12 * segs * rows * length,
            bytes_accessed=4 * segs * rows * length,
            transcendentals=0,
        ),
    )(seg_index, whitened, cosines, sines)

    keep, send = pl.pallas_call(
        correlate_kernel,
        out_shape=[jax.ShapeDtypeStruct((rows, lanes), jnp.float32)] * 2,
        in_specs=[VMEM] * (1 + col),
        out_specs=[VMEM] * 2,
        compiler_params=grant(12),
    )(rotated, *[blocks[m] for m in range(col)])
    got = lax.ppermute(send, "seg", [(0, 1), (1, 0)])
    out = pl.pallas_call(
        functools.partial(finish_kernel, scale, own),
        out_shape=jax.ShapeDtypeStruct((lags, part, lanes), jnp.float32),
        in_specs=[SMEM, VMEM, VMEM],
        out_specs=VMEM,
        compiler_params=grant(2),
    )(me, keep, got)
    return out[:, None]


def on_device(traces, valid):
    fast = (
        fast_mesh(lax.axis_size("row"), lax.axis_size("col"), lax.axis_size("seg"))
        and traces.shape[1] == 8
        and traces.shape[1] * lax.axis_size("col") == 128
        and traces.shape[2] % 1024 == 0
    )
    return (fast_device if fast else general_device)(traces, valid)


def fast_mesh(row, col, seg):
    return row == 1 and seg == 2 and col >= 8 and col & (col - 1) == 0


def solution(mesh):
    placed = (P("seg", ("row", "col"), None), P("seg", ("row", "col")))
    return jax.shard_map(
        on_device,
        mesh=mesh,
        in_specs=placed,
        out_specs=P(None, None, ("col", "seg"), "row"),
        check_vma=False,
    )
```

profile of v0, /device:TPU:0, one launch (start us, length us, event | category | flops | bytes accessed | tf_op | source)
XLA Modules:
  0.0 25.3 jit_solution(14282901746056268697)
XLA Ops:
  0.0 1.5 %shard_map.55 = (bf16[4,8,1024]{2,1,0:T(8,128)(2,1)S(1)}, f32[136,512]{1,0:T(8,128)S(1)}, f32[136,512]{1,0:T(8,128)S(1)}) custom-call(bf16[4,8,1024]{2,1,0:T(8,128)(2,1)} %x_in.1, s32[4,8]{1,0:T(4,128)} %v_in.1, bf16[256,1024]{1,0:T(8,128)(2,1)} %constant.14.clone.t_in, f32[136,512]{1,0:T(8,128)} %constant.15.clone.c_in, f32[136,512]{1,0:T(8,128)} %constant.16.clone.s_in), custom_call_target="tpu_custom_call" | custom-call | tf_op jit(solution)/shard_map/pallas_call | solution.py:265
  1.5 4.1 %collective-permute-start.7 = (bf16[4,8,1024]{2,1,0:T(8,128)(2,1)S(1)}, bf16[4,8,1024]{2,1,0:T(8,128)(2,1)S(1)}, u32[]{:S(2)}, u32[]{:S(2)}) collective-permute-start(bf16[4,8,1024]{2,1,0:T(8,128)(2,1)S(1)} %get-tuple-element.10.w_ref.refs_1_), channel_id=1, source_target_pairs={{0,16},{2,18},{4,20},{6,22},{8,24},{10,26},{12,28},{14,30},{16,0},... | collective-permute-start | bytes 196616 | tf_op jit(solution)/shard_map/ppermute | solution.py:290
  5.6 1.5 %collective-permute-start.1 = (bf16[4,8,1024]{2,1,0:T(8,128)(2,1)S(1)}, bf16[4,8,1024]{2,1,0:T(8,128)(2,1)S(1)}, u32[]{:S(2)}, u32[]{:S(2)}) collective-permute-start(bf16[4,8,1024]{2,1,0:T(8,128)(2,1)S(1)} %get-tuple-element.10.w_ref.refs_1_), channel_id=1, source_target_pairs={{0,4},{2,6},{4,0},{6,2},{8,12},{10,14},{12,8},{14,10},{16,20},{18,... | collective-permute-start | bytes 196616 | tf_op jit(solution)/shard_map/ppermute | solution.py:290
  7.2 1.6 %collective-permute-start.3 = (bf16[4,8,1024]{2,1,0:T(8,128)(2,1)S(1)}, bf16[4,8,1024]{2,1,0:T(8,128)(2,1)S(1)}, u32[]{:S(2)}, u32[]{:S(2)}) collective-permute-start(bf16[4,8,1024]{2,1,0:T(8,128)(2,1)S(1)} %get-tuple-element.10.w_ref.refs_1_), channel_id=1, source_target_pairs={{0,8},{2,10},{4,12},{6,14},{8,0},{10,2},{12,4},{14,6},{16,24},{18,... | collective-permute-start | bytes 196616 | tf_op jit(solution)/shard_map/ppermute | solution.py:290
  8.7 0.4 %collective-permute-start.5 = (bf16[4,8,1024]{2,1,0:T(8,128)(2,1)S(1)}, bf16[4,8,1024]{2,1,0:T(8,128)(2,1)S(1)}, u32[]{:S(2)}, u32[]{:S(2)}) collective-permute-start(bf16[4,8,1024]{2,1,0:T(8,128)(2,1)S(1)} %get-tuple-element.10.w_ref.refs_1_), channel_id=1, source_target_pairs={{0,12},{2,14},{4,8},{6,10},{8,4},{10,6},{12,0},{14,2},{16,28},{18,... | collective-permute-start | bytes 196616 | tf_op jit(solution)/shard_map/ppermute | solution.py:290
  9.1 0.0 collective-permute-start
  9.1 0.0 collective-permute-done.7.refs_9_
  9.1 1.5 %collective-permute-start.9 = (bf16[4,8,1024]{2,1,0:T(8,128)(2,1)S(1)}, bf16[4,8,1024]{2,1,0:T(8,128)(2,1)S(1)}, u32[]{:S(2)}, u32[]{:S(2)}) collective-permute-start(bf16[4,8,1024]{2,1,0:T(8,128)(2,1)S(1)} %collective-permute-done.7.refs_9_), channel_id=1, source_target_pairs={{0,4},{2,6},{4,0},{6,2},{8,12},{10,14},{12,8},{14,10},{16,20},{18,... | collective-permute-start | bytes 196616 | tf_op jit(solution)/shard_map/ppermute | solution.py:290
  10.7 0.0 collective-permute-done.1.refs_3_
  10.7 1.6 %collective-permute-start.11 = (bf16[4,8,1024]{2,1,0:T(8,128)(2,1)S(1)}, bf16[4,8,1024]{2,1,0:T(8,128)(2,1)S(1)}, u32[]{:S(2)}, u32[]{:S(2)}) collective-permute-start(bf16[4,8,1024]{2,1,0:T(8,128)(2,1)S(1)} %collective-permute-done.7.refs_9_), channel_id=1, source_target_pairs={{0,8},{2,10},{4,12},{6,14},{8,0},{10,2},{12,4},{14,6},{16,24},{18,... | collective-permute-start | bytes 196616 | tf_op jit(solution)/shard_map/ppermute | solution.py:290
  12.2 0.0 collective-permute-done.3.refs_5_
  12.2 0.9 %collective-permute-start.13 = (bf16[4,8,1024]{2,1,0:T(8,128)(2,1)S(1)}, bf16[4,8,1024]{2,1,0:T(8,128)(2,1)S(1)}, u32[]{:S(2)}, u32[]{:S(2)}) collective-permute-start(bf16[4,8,1024]{2,1,0:T(8,128)(2,1)S(1)} %collective-permute-done.7.refs_9_), channel_id=1, source_target_pairs={{0,12},{2,14},{4,8},{6,10},{8,4},{10,6},{12,0},{14,2},{16,28},{18,... | collective-permute-start | bytes 196616 | tf_op jit(solution)/shard_map/ppermute | solution.py:290
  13.2 1.2 %collective-permute-done.5.refs_7_ = bf16[4,8,1024]{2,1,0:T(8,128)(2,1)S(1)} collective-permute-done((bf16[4,8,1024]{2,1,0:T(8,128)(2,1)S(1)}, bf16[4,8,1024]{2,1,0:T(8,128)(2,1)S(1)}, u32[]{:S(2)}, u32[]{:S(2)}) %collective-permute-start.5) | collective-permute-done | bytes 65568 | tf_op jit(solution)/shard_map/ppermute | solution.py:290
  14.4 0.0 collective-permute-start.8
  14.4 0.0 collective-permute-done.refs_2_
  14.4 0.5 %collective-permute-start.2 = (bf16[4,8,1024]{2,1,0:T(8,128)(2,1)S(1)}, bf16[4,8,1024]{2,1,0:T(8,128)(2,1)S(1)}, u32[]{:S(2)}, u32[]{:S(2)}) collective-permute-start(bf16[4,8,1024]{2,1,0:T(8,128)(2,1)S(1)} %collective-permute-done.1.refs_3_), channel_id=1, source_target_pairs={{0,2},{2,0},{4,6},{6,4},{8,10},{10,8},{12,14},{14,12},{16,18},{18,... | collective-permute-start | bytes 196616 | tf_op jit(solution)/shard_map/ppermute | solution.py:290
  14.9 0.0 collective-permute-done.9.refs_11_
  14.9 0.1 collective-permute-start.4
  15.0 0.2 collective-permute-done.11.refs_13_
  15.1 0.3 %collective-permute-start.6 = (bf16[4,8,1024]{2,1,0:T(8,128)(2,1)S(1)}, bf16[4,8,1024]{2,1,0:T(8,128)(2,1)S(1)}, u32[]{:S(2)}, u32[]{:S(2)}) collective-permute-start(bf16[4,8,1024]{2,1,0:T(8,128)(2,1)S(1)} %collective-permute-done.5.refs_7_), channel_id=1, source_target_pairs={{0,2},{2,0},{4,6},{6,4},{8,10},{10,8},{12,14},{14,12},{16,18},{18,... | collective-permute-start | bytes 196616 | tf_op jit(solution)/shard_map/ppermute | solution.py:290
  15.4 2.0 %collective-permute-done.13.refs_15_ = bf16[4,8,1024]{2,1,0:T(8,128)(2,1)S(1)} collective-permute-done((bf16[4,8,1024]{2,1,0:T(8,128)(2,1)S(1)}, bf16[4,8,1024]{2,1,0:T(8,128)(2,1)S(1)}, u32[]{:S(2)}, u32[]{:S(2)}) %collective-permute-start.13) | collective-permute-done | bytes 65568 | tf_op jit(solution)/shard_map/ppermute | solution.py:290
  17.4 0.0 collective-permute-start.10
  17.4 0.0 collective-permute-done.8.refs_10_
  17.4 0.5 %collective-permute-start.12 = (bf16[4,8,1024]{2,1,0:T(8,128)(2,1)S(1)}, bf16[4,8,1024]{2,1,0:T(8,128)(2,1)S(1)}, u32[]{:S(2)}, u32[]{:S(2)}) collective-permute-start(bf16[4,8,1024]{2,1,0:T(8,128)(2,1)S(1)} %collective-permute-done.11.refs_13_), channel_id=1, source_target_pairs={{0,2},{2,0},{4,6},{6,4},{8,10},{10,8},{12,14},{14,12},{16,18},{18,... | collective-permute-start | bytes 196616 | tf_op jit(solution)/shard_map/ppermute | solution.py:290
  17.9 0.0 collective-permute-done.2.refs_4_
  17.9 0.1 collective-permute-start.14
  18.0 0.5 %shard_map.56.refs_0_ = bf16[4,272,1024]{2,1,0:T(8,128)(2,1)S(1)} custom-call(s32[1]{0:T(128)} %bitcast.1.seg_ref, bf16[4,8,1024]{2,1,0:T(8,128)(2,1)S(1)} %get-tuple-element.10.w_ref.refs_1_, f32[136,512]{1,0:T(8,128)S(1)} %get-tuple-element.11.c_ref, f32[136,512]{1,0:T(8,128)S(1)} %get-tuple-element.12.s_ref), custom_call_target="tpu_custom_call" | custom-call | flops 6684672 | bytes 2228224 | tf_op jit(solution)/shard_map/pallas_call | solution.py:292
  18.5 0.0 collective-permute-done.4.refs_6_
  18.5 0.0 collective-permute-done.6.refs_8_
  18.6 0.1 collective-permute-done.10.refs_12_
  18.7 0.2 collective-permute-done.12.refs_14_
  18.8 0.4 %collective-permute-done.14.refs_16_ = bf16[4,8,1024]{2,1,0:T(8,128)(2,1)S(1)} collective-permute-done((bf16[4,8,1024]{2,1,0:T(8,128)(2,1)S(1)}, bf16[4,8,1024]{2,1,0:T(8,128)(2,1)S(1)}, u32[]{:S(2)}, u32[]{:S(2)}) %collective-permute-start.14) | collective-permute-done | bytes 65568 | tf_op jit(solution)/shard_map/ppermute | solution.py:290
  19.2 0.7 %shard_map.57 = (f32[136,128]{1,0:T(8,128)S(1)}, f32[136,128]{1,0:T(8,128)S(1)}) custom-call(bf16[4,272,1024]{2,1,0:T(8,128)(2,1)S(1)} %shard_map.56.refs_0_, bf16[4,8,1024]{2,1,0:T(8,128)(2,1)S(1)} %get-tuple-element.10.w_ref.refs_1_, bf16[4,8,1024]{2,1,0:T(8,128)(2,1)S(1)} %collective-permute-done.refs_2_, ...), custom_call_target="tpu_custom_call" | custom-call | tf_op jit(solution)/shard_map/pallas_call | solution.py:305
  19.9 1.6 %collective-permute-start.15 = (f32[136,128]{1,0:T(8,128)S(1)}, f32[136,128]{1,0:T(8,128)S(1)}, u32[]{:S(2)}, u32[]{:S(2)}) collective-permute-start(f32[136,128]{1,0:T(8,128)S(1)} %get-tuple-element.14), channel_id=1, source_target_pairs={{0,1},{1,0},{2,3},{3,2},{4,5},{5,4},{6,7},{7,6},{8,9},{9,8},{10,11... | collective-permute-start | bytes 208904 | tf_op jit(solution)/shard_map/ppermute | solution.py:312
  21.5 2.8 %collective-permute-done.15.got_ref = f32[136,128]{1,0:T(8,128)S(1)} collective-permute-done((f32[136,128]{1,0:T(8,128)S(1)}, f32[136,128]{1,0:T(8,128)S(1)}, u32[]{:S(2)}, u32[]{:S(2)}) %collective-permute-start.15) | collective-permute-done | bytes 69664 | tf_op jit(solution)/shard_map/ppermute | solution.py:312
  24.3 1.0 %shard_map.58 = f32[33,4,128]{2,1,0:T(4,128)} custom-call(s32[1]{0:T(128)} %bitcast.me_ref, f32[136,128]{1,0:T(8,128)S(1)} %get-tuple-element.13.keep_ref, f32[136,128]{1,0:T(8,128)S(1)} %collective-permute-done.15.got_ref), custom_call_target="tpu_custom_call" | custom-call | tf_op jit(solution)/shard_map/pallas_call | solution.py:313
Async XLA Ops:
  1.5 7.6 %collective-permute-start.7 = (bf16[4,8,1024]{2,1,0:T(8,128)(2,1)S(1)}, bf16[4,8,1024]{2,1,0:T(8,128)(2,1)S(1)}, u32[]{:S(2)}, u32[]{:S(2)}) collective-permute-start(bf16[4,8,1024]{2,1,0:T(8,128)(2,1)S(1)} %get-tuple-element.10.w_ref.refs_1_), channel_id=1, source_target_pairs={{0,16},{2,18},{4,20},{6,22},{8,24},{10,26},{12,28},{14,30},{16,0},... | collective-permute-start | bytes 196616 | tf_op jit(solution)/shard_map/ppermute | solution.py:290
  5.6 5.0 %collective-permute-start.1 = (bf16[4,8,1024]{2,1,0:T(8,128)(2,1)S(1)}, bf16[4,8,1024]{2,1,0:T(8,128)(2,1)S(1)}, u32[]{:S(2)}, u32[]{:S(2)}) collective-permute-start(bf16[4,8,1024]{2,1,0:T(8,128)(2,1)S(1)} %get-tuple-element.10.w_ref.refs_1_), channel_id=1, source_target_pairs={{0,4},{2,6},{4,0},{6,2},{8,12},{10,14},{12,8},{14,10},{16,20},{18,... | collective-permute-start | bytes 196616 | tf_op jit(solution)/shard_map/ppermute | solution.py:290
  7.2 5.1 %collective-permute-start.3 = (bf16[4,8,1024]{2,1,0:T(8,128)(2,1)S(1)}, bf16[4,8,1024]{2,1,0:T(8,128)(2,1)S(1)}, u32[]{:S(2)}, u32[]{:S(2)}) collective-permute-start(bf16[4,8,1024]{2,1,0:T(8,128)(2,1)S(1)} %get-tuple-element.10.w_ref.refs_1_), channel_id=1, source_target_pairs={{0,8},{2,10},{4,12},{6,14},{8,0},{10,2},{12,4},{14,6},{16,24},{18,... | collective-permute-start | bytes 196616 | tf_op jit(solution)/shard_map/ppermute | solution.py:290
  8.7 5.6 %collective-permute-start.5 = (bf16[4,8,1024]{2,1,0:T(8,128)(2,1)S(1)}, bf16[4,8,1024]{2,1,0:T(8,128)(2,1)S(1)}, u32[]{:S(2)}, u32[]{:S(2)}) collective-permute-start(bf16[4,8,1024]{2,1,0:T(8,128)(2,1)S(1)} %get-tuple-element.10.w_ref.refs_1_), channel_id=1, source_target_pairs={{0,12},{2,14},{4,8},{6,10},{8,4},{10,6},{12,0},{14,2},{16,28},{18,... | collective-permute-start | bytes 196616 | tf_op jit(solution)/shard_map/ppermute | solution.py:290
  9.1 5.3 %collective-permute-start = (bf16[4,8,1024]{2,1,0:T(8,128)(2,1)S(1)}, bf16[4,8,1024]{2,1,0:T(8,128)(2,1)S(1)}, u32[]{:S(2)}, u32[]{:S(2)}) collective-permute-start(bf16[4,8,1024]{2,1,0:T(8,128)(2,1)S(1)} %get-tuple-element.10.w_ref.refs_1_), channel_id=1, source_target_pairs={{0,2},{2,0},{4,6},{6,4},{8,10},{10,8},{12,14},{14,12},{16,18},{18,... | collective-permute-start | bytes 196616 | tf_op jit(solution)/shard_map/ppermute | solution.py:290
  9.1 5.8 %collective-permute-start.9 = (bf16[4,8,1024]{2,1,0:T(8,128)(2,1)S(1)}, bf16[4,8,1024]{2,1,0:T(8,128)(2,1)S(1)}, u32[]{:S(2)}, u32[]{:S(2)}) collective-permute-start(bf16[4,8,1024]{2,1,0:T(8,128)(2,1)S(1)} %collective-permute-done.7.refs_9_), channel_id=1, source_target_pairs={{0,4},{2,6},{4,0},{6,2},{8,12},{10,14},{12,8},{14,10},{16,20},{18,... | collective-permute-start | bytes 196616 | tf_op jit(solution)/shard_map/ppermute | solution.py:290
  10.7 4.5 %collective-permute-start.11 = (bf16[4,8,1024]{2,1,0:T(8,128)(2,1)S(1)}, bf16[4,8,1024]{2,1,0:T(8,128)(2,1)S(1)}, u32[]{:S(2)}, u32[]{:S(2)}) collective-permute-start(bf16[4,8,1024]{2,1,0:T(8,128)(2,1)S(1)} %collective-permute-done.7.refs_9_), channel_id=1, source_target_pairs={{0,8},{2,10},{4,12},{6,14},{8,0},{10,2},{12,4},{14,6},{16,24},{18,... | collective-permute-start | bytes 196616 | tf_op jit(solution)/shard_map/ppermute | solution.py:290
  12.2 5.2 %collective-permute-start.13 = (bf16[4,8,1024]{2,1,0:T(8,128)(2,1)S(1)}, bf16[4,8,1024]{2,1,0:T(8,128)(2,1)S(1)}, u32[]{:S(2)}, u32[]{:S(2)}) collective-permute-start(bf16[4,8,1024]{2,1,0:T(8,128)(2,1)S(1)} %collective-permute-done.7.refs_9_), channel_id=1, source_target_pairs={{0,12},{2,14},{4,8},{6,10},{8,4},{10,6},{12,0},{14,2},{16,28},{18,... | collective-permute-start | bytes 196616 | tf_op jit(solution)/shard_map/ppermute | solution.py:290
  14.4 3.0 %collective-permute-start.8 = (bf16[4,8,1024]{2,1,0:T(8,128)(2,1)S(1)}, bf16[4,8,1024]{2,1,0:T(8,128)(2,1)S(1)}, u32[]{:S(2)}, u32[]{:S(2)}) collective-permute-start(bf16[4,8,1024]{2,1,0:T(8,128)(2,1)S(1)} %collective-permute-done.7.refs_9_), channel_id=1, source_target_pairs={{0,2},{2,0},{4,6},{6,4},{8,10},{10,8},{12,14},{14,12},{16,18},{18,... | collective-permute-start | bytes 196616 | tf_op jit(solution)/shard_map/ppermute | solution.py:290
  14.4 3.5 %collective-permute-start.2 = (bf16[4,8,1024]{2,1,0:T(8,128)(2,1)S(1)}, bf16[4,8,1024]{2,1,0:T(8,128)(2,1)S(1)}, u32[]{:S(2)}, u32[]{:S(2)}) collective-permute-start(bf16[4,8,1024]{2,1,0:T(8,128)(2,1)S(1)} %collective-permute-done.1.refs_3_), channel_id=1, source_target_pairs={{0,2},{2,0},{4,6},{6,4},{8,10},{10,8},{12,14},{14,12},{16,18},{18,... | collective-permute-start | bytes 196616 | tf_op jit(solution)/shard_map/ppermute | solution.py:290
  14.9 3.6 %collective-permute-start.4 = (bf16[4,8,1024]{2,1,0:T(8,128)(2,1)S(1)}, bf16[4,8,1024]{2,1,0:T(8,128)(2,1)S(1)}, u32[]{:S(2)}, u32[]{:S(2)}) collective-permute-start(bf16[4,8,1024]{2,1,0:T(8,128)(2,1)S(1)} %collective-permute-done.3.refs_5_), channel_id=1, source_target_pairs={{0,2},{2,0},{4,6},{6,4},{8,10},{10,8},{12,14},{14,12},{16,18},{18,... | collective-permute-start | bytes 196616 | tf_op jit(solution)/shard_map/ppermute | solution.py:290
  15.1 3.4 %collective-permute-start.6 = (bf16[4,8,1024]{2,1,0:T(8,128)(2,1)S(1)}, bf16[4,8,1024]{2,1,0:T(8,128)(2,1)S(1)}, u32[]{:S(2)}, u32[]{:S(2)}) collective-permute-start(bf16[4,8,1024]{2,1,0:T(8,128)(2,1)S(1)} %collective-permute-done.5.refs_7_), channel_id=1, source_target_pairs={{0,2},{2,0},{4,6},{6,4},{8,10},{10,8},{12,14},{14,12},{16,18},{18,... | collective-permute-start | bytes 196616 | tf_op jit(solution)/shard_map/ppermute | solution.py:290
  17.4 1.3 %collective-permute-start.10 = (bf16[4,8,1024]{2,1,0:T(8,128)(2,1)S(1)}, bf16[4,8,1024]{2,1,0:T(8,128)(2,1)S(1)}, u32[]{:S(2)}, u32[]{:S(2)}) collective-permute-start(bf16[4,8,1024]{2,1,0:T(8,128)(2,1)S(1)} %collective-permute-done.9.refs_11_), channel_id=1, source_target_pairs={{0,2},{2,0},{4,6},{6,4},{8,10},{10,8},{12,14},{14,12},{16,18},{18,... | collective-permute-start | bytes 196616 | tf_op jit(solution)/shard_map/ppermute | solution.py:290
  17.4 1.4 %collective-permute-start.12 = (bf16[4,8,1024]{2,1,0:T(8,128)(2,1)S(1)}, bf16[4,8,1024]{2,1,0:T(8,128)(2,1)S(1)}, u32[]{:S(2)}, u32[]{:S(2)}) collective-permute-start(bf16[4,8,1024]{2,1,0:T(8,128)(2,1)S(1)} %collective-permute-done.11.refs_13_), channel_id=1, source_target_pairs={{0,2},{2,0},{4,6},{6,4},{8,10},{10,8},{12,14},{14,12},{16,18},{18,... | collective-permute-start | bytes 196616 | tf_op jit(solution)/shard_map/ppermute | solution.py:290
  17.9 1.3 %collective-permute-start.14 = (bf16[4,8,1024]{2,1,0:T(8,128)(2,1)S(1)}, bf16[4,8,1024]{2,1,0:T(8,128)(2,1)S(1)}, u32[]{:S(2)}, u32[]{:S(2)}) collective-permute-start(bf16[4,8,1024]{2,1,0:T(8,128)(2,1)S(1)} %collective-permute-done.13.refs_15_), channel_id=1, source_target_pairs={{0,2},{2,0},{4,6},{6,4},{8,10},{10,8},{12,14},{14,12},{16,18},{18,... | collective-permute-start | bytes 196616 | tf_op jit(solution)/shard_map/ppermute | solution.py:290
  19.9 4.4 %collective-permute-start.15 = (f32[136,128]{1,0:T(8,128)S(1)}, f32[136,128]{1,0:T(8,128)S(1)}, u32[]{:S(2)}, u32[]{:S(2)}) collective-permute-start(f32[136,128]{1,0:T(8,128)S(1)} %get-tuple-element.14), channel_id=1, source_target_pairs={{0,1},{1,0},{2,3},{3,2},{4,5},{5,4},{6,7},{7,6},{8,9},{9,8},{10,11... | collective-permute-start | bytes 208904 | tf_op jit(solution)/shard_map/ppermute | solution.py:312
where the time goes:
time: 25.4 us; the launch traced here: 25.3 us
  starting transfers between devices  14.6 us (57%)
  waiting for transfers between devices  6.85 us (27%)
  Pallas kernels  3.76 us (15%)
    ppermute x15, starting transfers between devices, fast_body(): lax.ppermute(blocks[held], 'col', [(i, i ^ distance) for i in range(col)])  13.1 us
    ppermute x15, waiting for transfers between devices, fast_body(): lax.ppermute(blocks[held], 'col', [(i, i ^ distance) for i in range(col)])  4.04 us
    ppermute x1, waiting for transfers between devices, fast_body(): got = lax.ppermute(send, 'seg', [(0, 1), (1, 0)])  2.81 us
    ppermute x1, starting transfers between devices, fast_body(): got = lax.ppermute(send, 'seg', [(0, 1), (1, 0)])  1.56 us
    pallas_call x1, Pallas kernels, fast_body(): pl.pallas_call(whiten_kernel, out_shape=[jax.ShapeDtypeStruct(traces.shap...  1.51 us
    pallas_call x1, Pallas kernels, fast_body(): pl.pallas_call(functools.partial(finish_kernel, scale, own), out_shape=ja...  0.98 us
    pallas_call x1, Pallas kernels, fast_body(): pl.pallas_call(correlate_kernel, out_shape=[jax.ShapeDtypeStruct((rows, l...  0.74 us
    pallas_call x1, Pallas kernels, fast_body(): pl.pallas_call(rotate_kernel, out_shape=jax.ShapeDtypeStruct((segs, 2 * r...  0.53 us
  transfers between devices with their start and end apart: 16, of which 7 were waited for; matrix products, arithmetic and copies ran while one was open for 0% of the time, Pallas kernels for 2%

commit v1 on v0

--- a/solution.py
+++ b/solution.py
@@ -205,7 +205,12 @@
     rows = keep_ref.shape[0]
     total = None
     for seg in range(r_ref.shape[0]):
-        first = jnp.concatenate([b[seg] for b in blocks], axis=0)
+        first = []
+        for at in range(0, len(blocks), 6):
+            block, mate, pair_mate, pair, cross, cross_mate = blocks[at : at + 6]
+            first += [block[seg], mate[seg], pair_mate[1, seg], pair_mate[0, seg]]
+            first += [pair[0, seg], pair[1, seg], cross[seg], cross_mate[seg]]
+        first = jnp.concatenate(first, axis=0)
         term = lax.dot_general(
             r_ref[seg], first, (((1,), (1,)), ((), ())), preferred_element_type=jnp.float32
         )
@@ -214,10 +219,19 @@
     send_ref[...] = total[rows:]
 
 
+def pair_kernel(a_ref, b_ref, out_ref):
+    out_ref[0] = a_ref[...]
+    out_ref[1] = b_ref[...]
+
+
 def finish_kernel(scale, own, me_ref, keep_ref, got_ref, out_ref):
     lags, part, lanes = out_ref.shape
     value = (keep_ref[: lags * part] + got_ref[: lags * part]) * scale
     lane = lax.broadcasted_iota(jnp.int32, value.shape, 1)
+    low, high = (lane & (2 * own)) != 0, (lane & (4 * own)) != 0
+    after, before = pltpu.roll(value, lanes - 2 * own, 1), pltpu.roll(value, 2 * own, 1)
+    crossed = jnp.where(low & ~high, after, jnp.where(high & ~low, before, value))
+    value = jnp.where((me_ref[0] & 1) != 0, crossed, value)
     width = own
     bit = 1
     while width < lanes:
@@ -230,20 +244,47 @@
         out_ref[lag] = value[lag * part : (lag + 1) * part]
 
 
-def gather_plan(col):
-    bits = [1 << i for i in reversed(range(col.bit_length() - 1))]
-    far, close, last = bits[:-3], bits[-3:-1], bits[-1:]
+CORE, SIDE, NEAR = 1, 2, 4
+
+
+def far_blocks(col):
     held, steps = [0], []
-    for bit in far:
+    bit = col // 2
+    while bit > NEAR:
         steps += [(m | bit, m, bit) for m in held]
         held += [m | bit for m in held]
-    near = [sum(close)] * (len(close) > 1) + close
-    for m in list(held):
-        steps += [(m | d, m, d) for d in near]
-        held += [m | d for d in near]
-    for bit in last:
-        steps += [(m | bit, m, bit) for m in held]
-    return steps
+        bit //= 2
+    return held, steps
+
+
+def hop(array, col, distance, other=None):
+    other = distance if other is None else other
+    return lax.ppermute(array, "col", [(i, i ^ (other if i & 1 else distance)) for i in range(col)])
+
+
+def gather(own_block, col):
+    def swap(array):
+        return hop(array, col, CORE)
+
+    blocks = {0: own_block}
+    held, steps = far_blocks(col)
+    for block, source, distance in steps:
+        blocks[block] = hop(blocks[source], col, distance)
+    out = []
+    for m in held:
+        block = blocks[m]
+        mate = swap(block)
+        cross = hop(block, col, NEAR | SIDE)
+        pair = pl.pallas_call(
+            pair_kernel,
+            out_shape=jax.ShapeDtypeStruct((2, *block.shape), block.dtype),
+            in_specs=[VMEM] * 2,
+            out_specs=VMEM,
+            compiler_params=grant(2),
+        )(block, mate)
+        pair = hop(pair, col, NEAR, SIDE)
+        out += [block, mate, swap(pair), pair, cross, swap(cross)]
+    return out
 
 
 def fast_device(traces, valid):
@@ -285,9 +326,7 @@
         ]
     )
 
-    blocks = {0: whitened}
-    for block, held, distance in gather_plan(col):
-        blocks[block] = lax.ppermute(blocks[held], "col", [(i, i ^ distance) for i in range(col)])
+    blocks = gather(whitened, col)
 
     rotated = pl.pallas_call(
         rotate_kernel,
@@ -305,10 +344,10 @@
     keep, send = pl.pallas_call(
         correlate_kernel,
         out_shape=[jax.ShapeDtypeStruct((rows, lanes), jnp.float32)] * 2,
-        in_specs=[VMEM] * (1 + col),
+        in_specs=[VMEM] * (1 + len(blocks)),
         out_specs=[VMEM] * 2,
         compiler_params=grant(12),
-    )(rotated, *[blocks[m] for m in range(col)])
+    )(rotated, *blocks)
     got = lax.ppermute(send, "seg", [(0, 1), (1, 0)])
     out = pl.pallas_call(
         functools.partial(finish_kernel, scale, own),

time: 25.4 us -> 27.3 us (1.075)
  waiting for transfers between devices: 6.85 us -> 12.9 us
  starting transfers between devices: 14.6 us -> 10.4 us
    ppermute x15 -> x11, waiting for transfers between devices: 4.04 us -> 10.1 us  [hop(): lax.ppermute(array, 'col', [(i, i ^ (other if i & 1 else distance)) for i...]
    ppermute x15 -> x11, starting transfers between devices: 13.1 us -> 8.81 us  [hop(): lax.ppermute(array, 'col', [(i, i ^ (other if i & 1 else distance)) for i...]
  transfers between devices with their start and end apart: 16 -> 12, of which waited for: 7 -> 7; matrix products, arithmetic and copies ran while one was open for 0% -> 0% of each run, Pallas kernels for 2% -> 2%
where the time goes in v1:
time: 27.3 us; the launch traced here: 27.2 us
  waiting for transfers between devices  12.9 us (47%)
  starting transfers between devices  10.4 us (38%)
  Pallas kernels  3.86 us (14%)
    ppermute x11, waiting for transfers between devices, hop(): lax.ppermute(array, 'col', [(i, i ^ (other if i & 1 else distance)) for i...  10.1 us
    ppermute x11, starting transfers between devices, hop(): lax.ppermute(array, 'col', [(i, i ^ (other if i & 1 else distance)) for i...  8.81 us
    ppermute x1, waiting for transfers between devices, fast_body(): got = lax.ppermute(send, 'seg', [(0, 1), (1, 0)])  2.82 us
    ppermute x1, starting transfers between devices, fast_body(): got = lax.ppermute(send, 'seg', [(0, 1), (1, 0)])  1.56 us
    pallas_call x1, Pallas kernels, fast_body(): pl.pallas_call(whiten_kernel, out_shape=[jax.ShapeDtypeStruct(traces.shap...  1.51 us
    pallas_call x1, Pallas kernels, fast_body(): pl.pallas_call(functools.partial(finish_kernel, scale, own), out_shape=ja...  1.06 us
    pallas_call x1, Pallas kernels, fast_body(): pl.pallas_call(correlate_kernel, out_shape=[jax.ShapeDtypeStruct((rows, l...  0.74 us
  transfers between devices with their start and end apart: 12, of which 7 were waited for; matrix products, arithmetic and copies ran while one was open for 0% of the time, Pallas kernels for 2%

profile of v1, /device:TPU:0, one launch (start us, length us, event | category | flops | bytes accessed | tf_op | source)
XLA Modules:
  0.0 27.2 jit_solution(6182411838758033226)
XLA Ops:
  0.0 1.5 %shard_map.55 = (bf16[4,8,1024]{2,1,0:T(8,128)(2,1)S(1)}, f32[136,512]{1,0:T(8,128)S(1)}, f32[136,512]{1,0:T(8,128)S(1)}) custom-call(bf16[4,8,1024]{2,1,0:T(8,128)(2,1)} %x_in.1, s32[4,8]{1,0:T(4,128)} %v_in.1, bf16[256,1024]{1,0:T(8,128)(2,1)} %constant.14.clone.t_in, f32[136,512]{1,0:T(8,128)} %constant.15.clone.c_in, f32[136,512]{1,0:T(8,128)} %constant.16.clone.s_in), custom_call_target="tpu_custom_call" | custom-call | tf_op jit(solution)/shard_map/pallas_call | solution.py:306
  1.5 4.1 %collective-permute-start.5 = (bf16[4,8,1024]{2,1,0:T(8,128)(2,1)S(1)}, bf16[4,8,1024]{2,1,0:T(8,128)(2,1)S(1)}, u32[]{:S(2)}, u32[]{:S(2)}) collective-permute-start(bf16[4,8,1024]{2,1,0:T(8,128)(2,1)S(1)} %get-tuple-element.10.w_ref.a_ref.refs_1_), channel_id=1, source_target_pairs={{0,16},{2,18},{4,20},{6,22},{8,24},{10,26},{12,28},{14,30},{16,0},... | collective-permute-start | bytes 196616 | tf_op jit(solution)/shard_map/ppermute | solution.py:262
  5.6 0.0 collective-permute-start
  5.6 3.6 %collective-permute-done.5.a_ref.refs_7_ = bf16[4,8,1024]{2,1,0:T(8,128)(2,1)S(1)} collective-permute-done((bf16[4,8,1024]{2,1,0:T(8,128)(2,1)S(1)}, bf16[4,8,1024]{2,1,0:T(8,128)(2,1)S(1)}, u32[]{:S(2)}, u32[]{:S(2)}) %collective-permute-start.5) | collective-permute-done | bytes 65568 | tf_op jit(solution)/shard_map/ppermute | solution.py:262
  9.3 0.0 collective-permute-start.6
  9.3 0.0 collective-permute-done.b_ref.refs_2_
  9.3 0.6 %collective-permute-start.1 = (bf16[2,4,8,1024]{3,2,1,0:T(8,128)(2,1)S(1)}, bf16[2,4,8,1024]{3,2,1,0:T(8,128)(2,1)S(1)}, u32[]{:S(2)}, u32[]{:S(2)}) collective-permute-start(bf16[2,4,8,1024]{3,2,1,0:T(8,128)(2,1)S(1)} %shard_map.57), channel_id=1, source_target_pairs={{0,8},{2,6},{4,12},{6,2},{8,0},{10,14},{12,4},{14,10},{16,24},{18,... | collective-permute-start | bytes 393224 | tf_op jit(solution)/shard_map/ppermute | solution.py:262
  10.0 0.6 %collective-permute-done.6.b_ref.refs_8_ = bf16[4,8,1024]{2,1,0:T(8,128)(2,1)S(1)} collective-permute-done((bf16[4,8,1024]{2,1,0:T(8,128)(2,1)S(1)}, bf16[4,8,1024]{2,1,0:T(8,128)(2,1)S(1)}, u32[]{:S(2)}, u32[]{:S(2)}) %collective-permute-start.6) | collective-permute-done | bytes 65568 | tf_op jit(solution)/shard_map/ppermute | solution.py:262
  10.6 0.9 %collective-permute-start.7 = (bf16[2,4,8,1024]{3,2,1,0:T(8,128)(2,1)S(1)}, bf16[2,4,8,1024]{3,2,1,0:T(8,128)(2,1)S(1)}, u32[]{:S(2)}, u32[]{:S(2)}) collective-permute-start(bf16[2,4,8,1024]{3,2,1,0:T(8,128)(2,1)S(1)} %shard_map.58), channel_id=1, source_target_pairs={{0,8},{2,6},{4,12},{6,2},{8,0},{10,14},{12,4},{14,10},{16,24},{18,... | collective-permute-start | bytes 393224 | tf_op jit(solution)/shard_map/ppermute | solution.py:262
  11.5 2.3 %collective-permute-start.3 = (bf16[4,8,1024]{2,1,0:T(8,128)(2,1)S(1)}, bf16[4,8,1024]{2,1,0:T(8,128)(2,1)S(1)}, u32[]{:S(2)}, u32[]{:S(2)}) collective-permute-start(bf16[4,8,1024]{2,1,0:T(8,128)(2,1)S(1)} %get-tuple-element.10.w_ref.a_ref.refs_1_), channel_id=1, source_target_pairs={{0,12},{2,14},{4,8},{6,10},{8,4},{10,6},{12,0},{14,2},{16,28},{18,... | collective-permute-start | bytes 196616 | tf_op jit(solution)/shard_map/ppermute | solution.py:262
  13.8 0.6 %collective-permute-start.9 = (bf16[4,8,1024]{2,1,0:T(8,128)(2,1)S(1)}, bf16[4,8,1024]{2,1,0:T(8,128)(2,1)S(1)}, u32[]{:S(2)}, u32[]{:S(2)}) collective-permute-start(bf16[4,8,1024]{2,1,0:T(8,128)(2,1)S(1)} %collective-permute-done.5.a_ref.refs_7_), channel_id=1, source_target_pairs={{0,12},{2,14},{4,8},{6,10},{8,4},{10,6},{12,0},{14,2},{16,28},{18,... | collective-permute-start | bytes 196616 | tf_op jit(solution)/shard_map/ppermute | solution.py:262
  14.4 0.0 collective-permute-done.1.refs_4_
  14.4 0.2 collective-permute-start.2
  14.6 1.7 %collective-permute-done.7.refs_10_ = bf16[2,4,8,1024]{3,2,1,0:T(8,128)(2,1)S(1)} collective-permute-done((bf16[2,4,8,1024]{3,2,1,0:T(8,128)(2,1)S(1)}, bf16[2,4,8,1024]{3,2,1,0:T(8,128)(2,1)S(1)}, u32[]{:S(2)}, u32[]{:S(2)}) %collective-permute-start.7) | collective-permute-done | bytes 131104 | tf_op jit(solution)/shard_map/ppermute | solution.py:262
  16.3 0.0 collective-permute-start.8
  16.3 2.7 %collective-permute-done.3.refs_5_ = bf16[4,8,1024]{2,1,0:T(8,128)(2,1)S(1)} collective-permute-done((bf16[4,8,1024]{2,1,0:T(8,128)(2,1)S(1)}, bf16[4,8,1024]{2,1,0:T(8,128)(2,1)S(1)}, u32[]{:S(2)}, u32[]{:S(2)}) %collective-permute-start.3) | collective-permute-done | bytes 65568 | tf_op jit(solution)/shard_map/ppermute | solution.py:262
  19.0 0.0 collective-permute-start.4
  19.0 0.7 %collective-permute-done.9.refs_11_ = bf16[4,8,1024]{2,1,0:T(8,128)(2,1)S(1)} collective-permute-done((bf16[4,8,1024]{2,1,0:T(8,128)(2,1)S(1)}, bf16[4,8,1024]{2,1,0:T(8,128)(2,1)S(1)}, u32[]{:S(2)}, u32[]{:S(2)}) %collective-permute-start.9) | collective-permute-done | bytes 65568 | tf_op jit(solution)/shard_map/ppermute | solution.py:262
  19.7 0.0 collective-permute-start.10
  19.7 0.5 %shard_map.56.refs_0_ = bf16[4,272,1024]{2,1,0:T(8,128)(2,1)S(1)} custom-call(s32[1]{0:T(128)} %bitcast.1.seg_ref, bf16[4,8,1024]{2,1,0:T(8,128)(2,1)S(1)} %get-tuple-element.10.w_ref.a_ref.refs_1_, f32[136,512]{1,0:T(8,128)S(1)} %get-tuple-element.11.c_ref, f32[136,512]{1,0:T(8,128)S(1)} %get-tuple-element.12.s_ref), custom_call_target="tpu_custom_call" | custom-call | flops 6684672 | bytes 2228224 | tf_op jit(solution)/shard_map/pallas_call | solution.py:331
  20.3 0.0 collective-permute-done.4.refs_6_
  20.3 0.7 %collective-permute-done.10.refs_12_ = bf16[4,8,1024]{2,1,0:T(8,128)(2,1)S(1)} collective-permute-done((bf16[4,8,1024]{2,1,0:T(8,128)(2,1)S(1)}, bf16[4,8,1024]{2,1,0:T(8,128)(2,1)S(1)}, u32[]{:S(2)}, u32[]{:S(2)}) %collective-permute-start.10) | collective-permute-done | bytes 65568 | tf_op jit(solution)/shard_map/ppermute | solution.py:262
  21.0 0.0 collective-permute-done.2.refs_3_
  21.0 0.0 collective-permute-done.8.refs_9_
  21.0 0.7 %shard_map.59 = (f32[136,128]{1,0:T(8,128)S(1)}, f32[136,128]{1,0:T(8,128)S(1)}) custom-call(bf16[4,272,1024]{2,1,0:T(8,128)(2,1)S(1)} %shard_map.56.refs_0_, bf16[4,8,1024]{2,1,0:T(8,128)(2,1)S(1)} %get-tuple-element.10.w_ref.a_ref.refs_1_, bf16[4,8,1024]{2,1,0:T(8,128)(2,1)S(1)} %collective-permute-done.b_ref.refs_2_, ...), custom_call_target="tpu_custom_call" | custom-call | tf_op jit(solution)/shard_map/pallas_call | solution.py:344
  21.7 1.6 %collective-permute-start.11 = (f32[136,128]{1,0:T(8,128)S(1)}, f32[136,128]{1,0:T(8,128)S(1)}, u32[]{:S(2)}, u32[]{:S(2)}) collective-permute-start(f32[136,128]{1,0:T(8,128)S(1)} %get-tuple-element.14), channel_id=1, source_target_pairs={{0,1},{1,0},{2,3},{3,2},{4,5},{5,4},{6,7},{7,6},{8,9},{9,8},{10,11... | collective-permute-start | bytes 208904 | tf_op jit(solution)/shard_map/ppermute | solution.py:351
  23.3 2.8 %collective-permute-done.11.got_ref = f32[136,128]{1,0:T(8,128)S(1)} collective-permute-done((f32[136,128]{1,0:T(8,128)S(1)}, f32[136,128]{1,0:T(8,128)S(1)}, u32[]{:S(2)}, u32[]{:S(2)}) %collective-permute-start.11) | collective-permute-done | bytes 69664 | tf_op jit(solution)/shard_map/ppermute | solution.py:351
  26.1 1.1 %shard_map.60 = f32[33,4,128]{2,1,0:T(4,128)} custom-call(s32[1]{0:T(128)} %bitcast.me_ref, f32[136,128]{1,0:T(8,128)S(1)} %get-tuple-element.13.keep_ref, f32[136,128]{1,0:T(8,128)S(1)} %collective-permute-done.11.got_ref), custom_call_target="tpu_custom_call" | custom-call | tf_op jit(solution)/shard_map/pallas_call | solution.py:352
  (2 shorter events, 0.0 us)
Async XLA Ops:
  1.5 7.8 %collective-permute-start.5 = (bf16[4,8,1024]{2,1,0:T(8,128)(2,1)S(1)}, bf16[4,8,1024]{2,1,0:T(8,128)(2,1)S(1)}, u32[]{:S(2)}, u32[]{:S(2)}) collective-permute-start(bf16[4,8,1024]{2,1,0:T(8,128)(2,1)S(1)} %get-tuple-element.10.w_ref.a_ref.refs_1_), channel_id=1, source_target_pairs={{0,16},{2,18},{4,20},{6,22},{8,24},{10,26},{12,28},{14,30},{16,0},... | collective-permute-start | bytes 196616 | tf_op jit(solution)/shard_map/ppermute | solution.py:262
  5.6 3.7 %collective-permute-start = (bf16[4,8,1024]{2,1,0:T(8,128)(2,1)S(1)}, bf16[4,8,1024]{2,1,0:T(8,128)(2,1)S(1)}, u32[]{:S(2)}, u32[]{:S(2)}) collective-permute-start(bf16[4,8,1024]{2,1,0:T(8,128)(2,1)S(1)} %get-tuple-element.10.w_ref.a_ref.refs_1_), channel_id=1, source_target_pairs={{0,2},{2,0},{4,6},{6,4},{8,10},{10,8},{12,14},{14,12},{16,18},{18,... | collective-permute-start | bytes 196616 | tf_op jit(solution)/shard_map/ppermute | solution.py:262
  9.3 1.3 %collective-permute-start.6 = (bf16[4,8,1024]{2,1,0:T(8,128)(2,1)S(1)}, bf16[4,8,1024]{2,1,0:T(8,128)(2,1)S(1)}, u32[]{:S(2)}, u32[]{:S(2)}) collective-permute-start(bf16[4,8,1024]{2,1,0:T(8,128)(2,1)S(1)} %collective-permute-done.5.a_ref.refs_7_), channel_id=1, source_target_pairs={{0,2},{2,0},{4,6},{6,4},{8,10},{10,8},{12,14},{14,12},{16,18},{18,... | collective-permute-start | bytes 196616 | tf_op jit(solution)/shard_map/ppermute | solution.py:262
  9.3 5.1 %collective-permute-start.1 = (bf16[2,4,8,1024]{3,2,1,0:T(8,128)(2,1)S(1)}, bf16[2,4,8,1024]{3,2,1,0:T(8,128)(2,1)S(1)}, u32[]{:S(2)}, u32[]{:S(2)}) collective-permute-start(bf16[2,4,8,1024]{3,2,1,0:T(8,128)(2,1)S(1)} %shard_map.57), channel_id=1, source_target_pairs={{0,8},{2,6},{4,12},{6,2},{8,0},{10,14},{12,4},{14,10},{16,24},{18,... | collective-permute-start | bytes 393224 | tf_op jit(solution)/shard_map/ppermute | solution.py:262
  10.6 5.8 %collective-permute-start.7 = (bf16[2,4,8,1024]{3,2,1,0:T(8,128)(2,1)S(1)}, bf16[2,4,8,1024]{3,2,1,0:T(8,128)(2,1)S(1)}, u32[]{:S(2)}, u32[]{:S(2)}) collective-permute-start(bf16[2,4,8,1024]{3,2,1,0:T(8,128)(2,1)S(1)} %shard_map.58), channel_id=1, source_target_pairs={{0,8},{2,6},{4,12},{6,2},{8,0},{10,14},{12,4},{14,10},{16,24},{18,... | collective-permute-start | bytes 393224 | tf_op jit(solution)/shard_map/ppermute | solution.py:262
  11.5 7.5 %collective-permute-start.3 = (bf16[4,8,1024]{2,1,0:T(8,128)(2,1)S(1)}, bf16[4,8,1024]{2,1,0:T(8,128)(2,1)S(1)}, u32[]{:S(2)}, u32[]{:S(2)}) collective-permute-start(bf16[4,8,1024]{2,1,0:T(8,128)(2,1)S(1)} %get-tuple-element.10.w_ref.a_ref.refs_1_), channel_id=1, source_target_pairs={{0,12},{2,14},{4,8},{6,10},{8,4},{10,6},{12,0},{14,2},{16,28},{18,... | collective-permute-start | bytes 196616 | tf_op jit(solution)/shard_map/ppermute | solution.py:262
  13.8 5.9 %collective-permute-start.9 = (bf16[4,8,1024]{2,1,0:T(8,128)(2,1)S(1)}, bf16[4,8,1024]{2,1,0:T(8,128)(2,1)S(1)}, u32[]{:S(2)}, u32[]{:S(2)}) collective-permute-start(bf16[4,8,1024]{2,1,0:T(8,128)(2,1)S(1)} %collective-permute-done.5.a_ref.refs_7_), channel_id=1, source_target_pairs={{0,12},{2,14},{4,8},{6,10},{8,4},{10,6},{12,0},{14,2},{16,28},{18,... | collective-permute-start | bytes 196616 | tf_op jit(solution)/shard_map/ppermute | solution.py:262
  14.4 6.6 %collective-permute-start.2 = (bf16[2,4,8,1024]{3,2,1,0:T(8,128)(2,1)S(1)}, bf16[2,4,8,1024]{3,2,1,0:T(8,128)(2,1)S(1)}, u32[]{:S(2)}, u32[]{:S(2)}) collective-permute-start(bf16[2,4,8,1024]{3,2,1,0:T(8,128)(2,1)S(1)} %collective-permute-done.1.refs_4_), channel_id=1, source_target_pairs={{0,2},{2,0},{4,6},{6,4},{8,10},{10,8},{12,14},{14,12},{16,18},{18,... | collective-permute-start | bytes 393224 | tf_op jit(solution)/shard_map/ppermute | solution.py:262
  16.3 4.7 %collective-permute-start.8 = (bf16[2,4,8,1024]{3,2,1,0:T(8,128)(2,1)S(1)}, bf16[2,4,8,1024]{3,2,1,0:T(8,128)(2,1)S(1)}, u32[]{:S(2)}, u32[]{:S(2)}) collective-permute-start(bf16[2,4,8,1024]{3,2,1,0:T(8,128)(2,1)S(1)} %collective-permute-done.7.refs_10_), channel_id=1, source_target_pairs={{0,2},{2,0},{4,6},{6,4},{8,10},{10,8},{12,14},{14,12},{16,18},{18,... | collective-permute-start | bytes 393224 | tf_op jit(solution)/shard_map/ppermute | solution.py:262
  19.0 1.3 %collective-permute-start.4 = (bf16[4,8,1024]{2,1,0:T(8,128)(2,1)S(1)}, bf16[4,8,1024]{2,1,0:T(8,128)(2,1)S(1)}, u32[]{:S(2)}, u32[]{:S(2)}) collective-permute-start(bf16[4,8,1024]{2,1,0:T(8,128)(2,1)S(1)} %collective-permute-done.3.refs_5_), channel_id=1, source_target_pairs={{0,2},{2,0},{4,6},{6,4},{8,10},{10,8},{12,14},{14,12},{16,18},{18,... | collective-permute-start | bytes 196616 | tf_op jit(solution)/shard_map/ppermute | solution.py:262
  19.7 1.3 %collective-permute-start.10 = (bf16[4,8,1024]{2,1,0:T(8,128)(2,1)S(1)}, bf16[4,8,1024]{2,1,0:T(8,128)(2,1)S(1)}, u32[]{:S(2)}, u32[]{:S(2)}) collective-permute-start(bf16[4,8,1024]{2,1,0:T(8,128)(2,1)S(1)} %collective-permute-done.9.refs_11_), channel_id=1, source_target_pairs={{0,2},{2,0},{4,6},{6,4},{8,10},{10,8},{12,14},{14,12},{16,18},{18,... | collective-permute-start | bytes 196616 | tf_op jit(solution)/shard_map/ppermute | solution.py:262
  21.7 4.4 %collective-permute-start.11 = (f32[136,128]{1,0:T(8,128)S(1)}, f32[136,128]{1,0:T(8,128)S(1)}, u32[]{:S(2)}, u32[]{:S(2)}) collective-permute-start(f32[136,128]{1,0:T(8,128)S(1)} %get-tuple-element.14), channel_id=1, source_target_pairs={{0,1},{1,0},{2,3},{3,2},{4,5},{5,4},{6,7},{7,6},{8,9},{9,8},{10,11... | collective-permute-start | bytes 208904 | tf_op jit(solution)/shard_map/ppermute | solution.py:351

commit v2 on v1

--- a/solution.py
+++ b/solution.py
@@ -107,16 +107,8 @@
     return out
 
 
-def whiten_kernel(
-    x_in, v_in, t_in, c_in, s_in, w_ref, c_out, s_out, x_ref, v_ref, t_ref, sems
-):
-    pairs = ((x_in, x_ref), (t_in, t_ref), (v_in, v_ref), (c_in, c_out), (s_in, s_out))
-    copies = [pltpu.make_async_copy(a, b, sems.at[i]) for i, (a, b) in enumerate(pairs)]
-    for copy in copies:
-        copy.start()
+def whiten_block(x_ref, v_ref, t_ref, w_ref):
     segs, own, length = x_ref.shape
-    for copy in copies[:3]:
-        copy.wait()
     quarter, half = length // 4, length // 2
     rows, group = segs * own, half // 4
     stacked = jnp.concatenate(
@@ -167,6 +159,18 @@
         for base, part in ((0, real[r]), (half, imag[r])):
             value = (part * factor).astype(jnp.bfloat16).reshape(segs, own, group)
             w_ref[:, :, base + r * group : base + (r + 1) * group] = value
+
+
+def whiten_own_kernel(
+    x_in, v_in, t_in, c_in, s_in, w_ref, t_ref, c_out, s_out, x_ref, v_ref, sems
+):
+    pairs = ((x_in, x_ref), (t_in, t_ref), (v_in, v_ref), (c_in, c_out), (s_in, s_out))
+    copies = [pltpu.make_async_copy(a, b, sems.at[i]) for i, (a, b) in enumerate(pairs)]
+    for copy in copies:
+        copy.start()
+    for copy in copies[:3]:
+        copy.wait()
+    whiten_block(x_ref, v_ref, t_ref, w_ref)
     for copy in copies[3:]:
         copy.wait()
 
@@ -262,29 +266,29 @@
     return lax.ppermute(array, "col", [(i, i ^ (other if i & 1 else distance)) for i in range(col)])
 
 
-def gather(own_block, col):
-    def swap(array):
-        return hop(array, col, CORE)
-
-    blocks = {0: own_block}
-    held, steps = far_blocks(col)
-    for block, source, distance in steps:
-        blocks[block] = hop(blocks[source], col, distance)
-    out = []
-    for m in held:
-        block = blocks[m]
-        mate = swap(block)
-        cross = hop(block, col, NEAR | SIDE)
-        pair = pl.pallas_call(
-            pair_kernel,
-            out_shape=jax.ShapeDtypeStruct((2, *block.shape), block.dtype),
-            in_specs=[VMEM] * 2,
-            out_specs=VMEM,
-            compiler_params=grant(2),
-        )(block, mate)
-        pair = hop(pair, col, NEAR, SIDE)
-        out += [block, mate, swap(pair), pair, cross, swap(cross)]
-    return out
+def far_copies(traces, valid, col):
+    raw = {0: (traces, valid)}
+    for block, source, distance in far_blocks(col)[1]:
+        far = hop(raw[source][0], col, distance)
+        flag = hop(raw[source][1], col, distance)
+        raw[block] = far, flag
+    return raw
+
+
+def spread(block, col):
+    mate = hop(block, col, CORE)
+    cross = hop(block, col, NEAR | SIDE)
+    pair = pl.pallas_call(
+        pair_kernel,
+        out_shape=jax.ShapeDtypeStruct((2, *block.shape), block.dtype),
+        in_specs=[VMEM] * 2,
+        out_specs=VMEM,
+        compiler_params=grant(2),
+    )(block, mate)
+    pair = hop(pair, col, NEAR, SIDE)
+    pair_mate = hop(pair, col, CORE)
+    cross_mate = hop(cross, col, CORE)
+    return [block, mate, pair_mate, pair, cross, cross_mate]
 
 
 def fast_device(traces, valid):
@@ -303,19 +307,20 @@
 
     table = quarter_table(length)
     lag_cos, lag_sin = lag_tables(length, MAXLAG, part, rows)
-    whitened, cosines, sines = pl.pallas_call(
-        whiten_kernel,
+    raw = far_copies(traces, valid, col)
+    whitened, table, cosines, sines = pl.pallas_call(
+        whiten_own_kernel,
         out_shape=[
             jax.ShapeDtypeStruct(traces.shape, jnp.bfloat16),
+            jax.ShapeDtypeStruct(table.shape, table.dtype),
             jax.ShapeDtypeStruct(lag_cos.shape, jnp.float32),
             jax.ShapeDtypeStruct(lag_sin.shape, jnp.float32),
         ],
         in_specs=[HBM] * 5,
-        out_specs=[VMEM] * 3,
+        out_specs=[VMEM] * 4,
         scratch_shapes=[
             pltpu.VMEM(traces.shape, traces.dtype),
             pltpu.VMEM(valid.shape, valid.dtype),
-            pltpu.VMEM(table.shape, table.dtype),
             pltpu.SemaphoreType.DMA((5,)),
         ],
         compiler_params=grant(4),
@@ -325,8 +330,19 @@
             for t in (traces, valid, table, lag_cos, lag_sin)
         ]
     )
-
-    blocks = gather(whitened, col)
+    blocks = []
+    for m, (far, flag) in raw.items():
+        if m == 0:
+            block = whitened
+        else:
+            block = pl.pallas_call(
+                whiten_block,
+                out_shape=jax.ShapeDtypeStruct(traces.shape, jnp.bfloat16),
+                in_specs=[VMEM] * 3,
+                out_specs=VMEM,
+                compiler_params=grant(4),
+            )(far, flag, table)
+        blocks += spread(block, col)
 
     rotated = pl.pallas_call(
         rotate_kernel,

time: 27.3 us -> 27.2 us (level)
  waiting for transfers between devices: 12.9 us -> 11.2 us
  starting transfers between devices: 10.4 us -> 11.6 us
  Pallas kernels: 3.86 us -> 4.24 us
    ppermute x11 -> x12, waiting for transfers between devices: 10.1 us -> 8.39 us  [hop(): lax.ppermute(array, 'col', [(i, i ^ (other if i & 1 else distance)) for i...]
    ppermute x11 -> x12, starting transfers between devices: 8.81 us -> 10 us  [hop(): lax.ppermute(array, 'col', [(i, i ^ (other if i & 1 else distance)) for i...]
    pallas_call x3 -> x4, Pallas kernels: 1.53 us -> 1.9 us  [the longest x1 1.51 us: fast_body(): pl.pallas_call(whiten_own_kernel, out_shape=[jax.ShapeDtypeStruct(traces....]
  transfers between devices with their start and end apart: 12 -> 13, of which waited for: 7 -> 6; matrix products, arithmetic and copies ran while one was open for 0% -> 0% of each run, Pallas kernels for 2% -> 9%
where the time goes in v2:
time: 27.2 us; the launch traced here: 27.1 us
  starting transfers between devices  11.6 us (43%)
  waiting for transfers between devices  11.2 us (41%)
  Pallas kernels  4.24 us (16%)
    ppermute x12, starting transfers between devices, hop(): lax.ppermute(array, 'col', [(i, i ^ (other if i & 1 else distance)) for i...  10 us
    ppermute x12, waiting for transfers between devices, hop(): lax.ppermute(array, 'col', [(i, i ^ (other if i & 1 else distance)) for i...  8.39 us
    ppermute x1, waiting for transfers between devices, fast_body(): got = lax.ppermute(send, 'seg', [(0, 1), (1, 0)])  2.82 us
    ppermute x1, starting transfers between devices, fast_body(): got = lax.ppermute(send, 'seg', [(0, 1), (1, 0)])  1.56 us
    pallas_call x1, Pallas kernels, fast_body(): pl.pallas_call(whiten_own_kernel, out_shape=[jax.ShapeDtypeStruct(traces....  1.51 us
    pallas_call x1, Pallas kernels, fast_body(): pl.pallas_call(functools.partial(finish_kernel, scale, own), out_shape=ja...  1.06 us
    pallas_call x1, Pallas kernels, fast_body(): pl.pallas_call(correlate_kernel, out_shape=[jax.ShapeDtypeStruct((rows, l...  0.74 us
  transfers between devices with their start and end apart: 13, of which 6 were waited for; matrix products, arithmetic and copies ran while one was open for 0% of the time, Pallas kernels for 9%

profile of v2, /device:TPU:0, one launch (start us, length us, event | category | flops | bytes accessed | tf_op | source)
XLA Modules:
  0.0 27.1 jit_solution(16429373350700611177)
XLA Ops:
  0.0 4.1 %collective-permute-start.5 = (bf16[4,8,1024]{2,1,0:T(8,128)(2,1)}, bf16[4,8,1024]{2,1,0:T(8,128)(2,1)S(1)}, u32[]{:S(2)}, u32[]{:S(2)}) collective-permute-start(bf16[4,8,1024]{2,1,0:T(8,128)(2,1)} %x_in.1), channel_id=1, source_target_pairs={{0,16},{2,18},{4,20},{6,22},{8,24},{10,26},{12,28},{14,30},{16,0},... | collective-permute-start | bytes 196616 | tf_op jit(solution)/shard_map/ppermute | solution.py:266
  4.1 0.0 collective-permute-start.6
  4.1 1.5 %shard_map.55 = (bf16[4,8,1024]{2,1,0:T(8,128)(2,1)S(1)}, bf16[256,1024]{1,0:T(8,128)(2,1)S(1)}, f32[136,512]{1,0:T(8,128)S(1)}, f32[136,512]{1,0:T(8,128)S(1)}) custom-call(bf16[4,8,1024]{2,1,0:T(8,128)(2,1)} %x_in.1, s32[4,8]{1,0:T(4,128)} %v_in.1, bf16[256,1024]{1,0:T(8,128)(2,1)} %constant.14.clone.t_in, f32[136,512]{1,0:T(8,128)} %constant.15.clone.c_in, ...), custom_call_target="tpu_custom_call" | custom-call | tf_op jit(solution)/shard_map/pallas_call | solution.py:311
  5.6 0.1 collective-permute-start
  5.7 3.1 %collective-permute-done.6.v_ref = s32[4,8]{1,0:T(4,128)S(1)} collective-permute-done((s32[4,8]{1,0:T(4,128)}, s32[4,8]{1,0:T(4,128)S(1)}, u32[]{:S(2)}, u32[]{:S(2)}) %collective-permute-start.6) | collective-permute-done | bytes 160 | tf_op jit(solution)/shard_map/ppermute | solution.py:266
  8.8 0.0 collective-permute-done.5.x_ref
  8.8 0.4 %shard_map.58.a_ref.refs_7_ = bf16[4,8,1024]{2,1,0:T(8,128)(2,1)S(1)} custom-call(bf16[4,8,1024]{2,1,0:T(8,128)(2,1)S(1)} %collective-permute-done.5.x_ref, s32[4,8]{1,0:T(4,128)S(1)} %collective-permute-done.6.v_ref, bf16[256,1024]{1,0:T(8,128)(2,1)S(1)} %get-tuple-element.14.t_ref), custom_call_target="tpu_custom_call" | custom-call | tf_op jit(solution)/shard_map/pallas_call | solution.py:338
  9.1 0.1 collective-permute-start.7
  9.2 0.0 collective-permute-done.b_ref.refs_2_
  9.3 1.6 %collective-permute-start.1 = (bf16[2,4,8,1024]{3,2,1,0:T(8,128)(2,1)S(1)}, bf16[2,4,8,1024]{3,2,1,0:T(8,128)(2,1)S(1)}, u32[]{:S(2)}, u32[]{:S(2)}) collective-permute-start(bf16[2,4,8,1024]{3,2,1,0:T(8,128)(2,1)S(1)} %shard_map.57), channel_id=1, source_target_pairs={{0,8},{2,6},{4,12},{6,2},{8,0},{10,14},{12,4},{14,10},{16,24},{18,... | collective-permute-start | bytes 393224 | tf_op jit(solution)/shard_map/ppermute | solution.py:266
  10.9 0.0 collective-permute-done.7.b_ref.refs_8_
  10.9 1.2 %collective-permute-start.8 = (bf16[2,4,8,1024]{3,2,1,0:T(8,128)(2,1)S(1)}, bf16[2,4,8,1024]{3,2,1,0:T(8,128)(2,1)S(1)}, u32[]{:S(2)}, u32[]{:S(2)}) collective-permute-start(bf16[2,4,8,1024]{3,2,1,0:T(8,128)(2,1)S(1)} %shard_map.59), channel_id=1, source_target_pairs={{0,8},{2,6},{4,12},{6,2},{8,0},{10,14},{12,4},{14,10},{16,24},{18,... | collective-permute-start | bytes 393224 | tf_op jit(solution)/shard_map/ppermute | solution.py:266
  12.1 1.8 %collective-permute-start.3 = (bf16[4,8,1024]{2,1,0:T(8,128)(2,1)S(1)}, bf16[4,8,1024]{2,1,0:T(8,128)(2,1)S(1)}, u32[]{:S(2)}, u32[]{:S(2)}) collective-permute-start(bf16[4,8,1024]{2,1,0:T(8,128)(2,1)S(1)} %get-tuple-element.11.w_ref.a_ref.refs_1_), channel_id=1, source_target_pairs={{0,12},{2,14},{4,8},{6,10},{8,4},{10,6},{12,0},{14,2},{16,28},{18,... | collective-permute-start | bytes 196616 | tf_op jit(solution)/shard_map/ppermute | solution.py:266
  14.0 1.1 %collective-permute-start.10 = (bf16[4,8,1024]{2,1,0:T(8,128)(2,1)S(1)}, bf16[4,8,1024]{2,1,0:T(8,128)(2,1)S(1)}, u32[]{:S(2)}, u32[]{:S(2)}) collective-permute-start(bf16[4,8,1024]{2,1,0:T(8,128)(2,1)S(1)} %shard_map.58.a_ref.refs_7_), channel_id=1, source_target_pairs={{0,12},{2,14},{4,8},{6,10},{8,4},{10,6},{12,0},{14,2},{16,28},{18,... | collective-permute-start | bytes 196616 | tf_op jit(solution)/shard_map/ppermute | solution.py:266
  15.1 0.0 collective-permute-done.1.refs_4_
  15.1 0.0 collective-permute-start.2
  15.1 1.6 %collective-permute-done.8.refs_10_ = bf16[2,4,8,1024]{3,2,1,0:T(8,128)(2,1)S(1)} collective-permute-done((bf16[2,4,8,1024]{3,2,1,0:T(8,128)(2,1)S(1)}, bf16[2,4,8,1024]{3,2,1,0:T(8,128)(2,1)S(1)}, u32[]{:S(2)}, u32[]{:S(2)}) %collective-permute-start.8) | collective-permute-done | bytes 131104 | tf_op jit(solution)/shard_map/ppermute | solution.py:266
  16.7 0.0 collective-permute-start.9
  16.7 2.3 %collective-permute-done.3.refs_5_ = bf16[4,8,1024]{2,1,0:T(8,128)(2,1)S(1)} collective-permute-done((bf16[4,8,1024]{2,1,0:T(8,128)(2,1)S(1)}, bf16[4,8,1024]{2,1,0:T(8,128)(2,1)S(1)}, u32[]{:S(2)}, u32[]{:S(2)}) %collective-permute-start.3) | collective-permute-done | bytes 65568 | tf_op jit(solution)/shard_map/ppermute | solution.py:266
  18.9 0.0 collective-permute-start.4
  19.0 0.7 %collective-permute-done.10.refs_11_ = bf16[4,8,1024]{2,1,0:T(8,128)(2,1)S(1)} collective-permute-done((bf16[4,8,1024]{2,1,0:T(8,128)(2,1)S(1)}, bf16[4,8,1024]{2,1,0:T(8,128)(2,1)S(1)}, u32[]{:S(2)}, u32[]{:S(2)}) %collective-permute-start.10) | collective-permute-done | bytes 65568 | tf_op jit(solution)/shard_map/ppermute | solution.py:266
  19.7 0.0 collective-permute-start.11
  19.7 0.5 %shard_map.56.refs_0_ = bf16[4,272,1024]{2,1,0:T(8,128)(2,1)S(1)} custom-call(s32[1]{0:T(128)} %bitcast.1.seg_ref, bf16[4,8,1024]{2,1,0:T(8,128)(2,1)S(1)} %get-tuple-element.11.w_ref.a_ref.refs_1_, f32[136,512]{1,0:T(8,128)S(1)} %get-tuple-element.12.c_ref, f32[136,512]{1,0:T(8,128)S(1)} %get-tuple-element.13.s_ref), custom_call_target="tpu_custom_call" | custom-call | flops 6684672 | bytes 2228224 | tf_op jit(solution)/shard_map/pallas_call | solution.py:347
  20.2 0.0 collective-permute-done.4.refs_6_
  20.2 0.7 %collective-permute-done.11.refs_12_ = bf16[4,8,1024]{2,1,0:T(8,128)(2,1)S(1)} collective-permute-done((bf16[4,8,1024]{2,1,0:T(8,128)(2,1)S(1)}, bf16[4,8,1024]{2,1,0:T(8,128)(2,1)S(1)}, u32[]{:S(2)}, u32[]{:S(2)}) %collective-permute-start.11) | collective-permute-done | bytes 65568 | tf_op jit(solution)/shard_map/ppermute | solution.py:266
  20.9 0.0 collective-permute-done.2.refs_3_
  20.9 0.0 collective-permute-done.9.refs_9_
  20.9 0.7 %shard_map.60 = (f32[136,128]{1,0:T(8,128)S(1)}, f32[136,128]{1,0:T(8,128)S(1)}) custom-call(bf16[4,272,1024]{2,1,0:T(8,128)(2,1)S(1)} %shard_map.56.refs_0_, bf16[4,8,1024]{2,1,0:T(8,128)(2,1)S(1)} %get-tuple-element.11.w_ref.a_ref.refs_1_, bf16[4,8,1024]{2,1,0:T(8,128)(2,1)S(1)} %collective-permute-done.b_ref.refs_2_, ...), custom_call_target="tpu_custom_call" | custom-call | tf_op jit(solution)/shard_map/pallas_call | solution.py:360
  21.7 1.6 %collective-permute-start.12 = (f32[136,128]{1,0:T(8,128)S(1)}, f32[136,128]{1,0:T(8,128)S(1)}, u32[]{:S(2)}, u32[]{:S(2)}) collective-permute-start(f32[136,128]{1,0:T(8,128)S(1)} %get-tuple-element.16), channel_id=1, source_target_pairs={{0,1},{1,0},{2,3},{3,2},{4,5},{5,4},{6,7},{7,6},{8,9},{9,8},{10,11... | collective-permute-start | bytes 208904 | tf_op jit(solution)/shard_map/ppermute | solution.py:367
  23.2 2.8 %collective-permute-done.12.got_ref = f32[136,128]{1,0:T(8,128)S(1)} collective-permute-done((f32[136,128]{1,0:T(8,128)S(1)}, f32[136,128]{1,0:T(8,128)S(1)}, u32[]{:S(2)}, u32[]{:S(2)}) %collective-permute-start.12) | collective-permute-done | bytes 69664 | tf_op jit(solution)/shard_map/ppermute | solution.py:367
  26.0 1.1 %shard_map.61 = f32[33,4,128]{2,1,0:T(4,128)} custom-call(s32[1]{0:T(128)} %bitcast.me_ref, f32[136,128]{1,0:T(8,128)S(1)} %get-tuple-element.15.keep_ref, f32[136,128]{1,0:T(8,128)S(1)} %collective-permute-done.12.got_ref), custom_call_target="tpu_custom_call" | custom-call | tf_op jit(solution)/shard_map/pallas_call | solution.py:368
  (2 shorter events, 0.0 us)
Async XLA Ops:
  0.0 8.8 %collective-permute-start.5 = (bf16[4,8,1024]{2,1,0:T(8,128)(2,1)}, bf16[4,8,1024]{2,1,0:T(8,128)(2,1)S(1)}, u32[]{:S(2)}, u32[]{:S(2)}) collective-permute-start(bf16[4,8,1024]{2,1,0:T(8,128)(2,1)} %x_in.1), channel_id=1, source_target_pairs={{0,16},{2,18},{4,20},{6,22},{8,24},{10,26},{12,28},{14,30},{16,0},... | collective-permute-start | bytes 196616 | tf_op jit(solution)/shard_map/ppermute | solution.py:266
  4.1 4.7 %collective-permute-start.6 = (s32[4,8]{1,0:T(4,128)}, s32[4,8]{1,0:T(4,128)S(1)}, u32[]{:S(2)}, u32[]{:S(2)}) collective-permute-start(s32[4,8]{1,0:T(4,128)} %v_in.1), channel_id=1, source_target_pairs={{0,16},{2,18},{4,20},{6,22},{8,24},{10,26},{12,28},{14,30},{16,0},... | collective-permute-start | bytes 392 | tf_op jit(solution)/shard_map/ppermute | solution.py:266
  5.6 3.6 %collective-permute-start = (bf16[4,8,1024]{2,1,0:T(8,128)(2,1)S(1)}, bf16[4,8,1024]{2,1,0:T(8,128)(2,1)S(1)}, u32[]{:S(2)}, u32[]{:S(2)}) collective-permute-start(bf16[4,8,1024]{2,1,0:T(8,128)(2,1)S(1)} %get-tuple-element.11.w_ref.a_ref.refs_1_), channel_id=1, source_target_pairs={{0,2},{2,0},{4,6},{6,4},{8,10},{10,8},{12,14},{14,12},{16,18},{18,... | collective-permute-start | bytes 196616 | tf_op jit(solution)/shard_map/ppermute | solution.py:266
  9.1 1.8 %collective-permute-start.7 = (bf16[4,8,1024]{2,1,0:T(8,128)(2,1)S(1)}, bf16[4,8,1024]{2,1,0:T(8,128)(2,1)S(1)}, u32[]{:S(2)}, u32[]{:S(2)}) collective-permute-start(bf16[4,8,1024]{2,1,0:T(8,128)(2,1)S(1)} %shard_map.58.a_ref.refs_7_), channel_id=1, source_target_pairs={{0,2},{2,0},{4,6},{6,4},{8,10},{10,8},{12,14},{14,12},{16,18},{18,... | collective-permute-start | bytes 196616 | tf_op jit(solution)/shard_map/ppermute | solution.py:266
  9.3 5.8 %collective-permute-start.1 = (bf16[2,4,8,1024]{3,2,1,0:T(8,128)(2,1)S(1)}, bf16[2,4,8,1024]{3,2,1,0:T(8,128)(2,1)S(1)}, u32[]{:S(2)}, u32[]{:S(2)}) collective-permute-start(bf16[2,4,8,1024]{3,2,1,0:T(8,128)(2,1)S(1)} %shard_map.57), channel_id=1, source_target_pairs={{0,8},{2,6},{4,12},{6,2},{8,0},{10,14},{12,4},{14,10},{16,24},{18,... | collective-permute-start | bytes 393224 | tf_op jit(solution)/shard_map/ppermute | solution.py:266
  10.9 5.7 %collective-permute-start.8 = (bf16[2,4,8,1024]{3,2,1,0:T(8,128)(2,1)S(1)}, bf16[2,4,8,1024]{3,2,1,0:T(8,128)(2,1)S(1)}, u32[]{:S(2)}, u32[]{:S(2)}) collective-permute-start(bf16[2,4,8,1024]{3,2,1,0:T(8,128)(2,1)S(1)} %shard_map.59), channel_id=1, source_target_pairs={{0,8},{2,6},{4,12},{6,2},{8,0},{10,14},{12,4},{14,10},{16,24},{18,... | collective-permute-start | bytes 393224 | tf_op jit(solution)/shard_map/ppermute | solution.py:266
  12.1 6.8 %collective-permute-start.3 = (bf16[4,8,1024]{2,1,0:T(8,128)(2,1)S(1)}, bf16[4,8,1024]{2,1,0:T(8,128)(2,1)S(1)}, u32[]{:S(2)}, u32[]{:S(2)}) collective-permute-start(bf16[4,8,1024]{2,1,0:T(8,128)(2,1)S(1)} %get-tuple-element.11.w_ref.a_ref.refs_1_), channel_id=1, source_target_pairs={{0,12},{2,14},{4,8},{6,10},{8,4},{10,6},{12,0},{14,2},{16,28},{18,... | collective-permute-start | bytes 196616 | tf_op jit(solution)/shard_map/ppermute | solution.py:266
  14.0 5.7 %collective-permute-start.10 = (bf16[4,8,1024]{2,1,0:T(8,128)(2,1)S(1)}, bf16[4,8,1024]{2,1,0:T(8,128)(2,1)S(1)}, u32[]{:S(2)}, u32[]{:S(2)}) collective-permute-start(bf16[4,8,1024]{2,1,0:T(8,128)(2,1)S(1)} %shard_map.58.a_ref.refs_7_), channel_id=1, source_target_pairs={{0,12},{2,14},{4,8},{6,10},{8,4},{10,6},{12,0},{14,2},{16,28},{18,... | collective-permute-start | bytes 196616 | tf_op jit(solution)/shard_map/ppermute | solution.py:266
  15.1 5.9 %collective-permute-start.2 = (bf16[2,4,8,1024]{3,2,1,0:T(8,128)(2,1)S(1)}, bf16[2,4,8,1024]{3,2,1,0:T(8,128)(2,1)S(1)}, u32[]{:S(2)}, u32[]{:S(2)}) collective-permute-start(bf16[2,4,8,1024]{3,2,1,0:T(8,128)(2,1)S(1)} %collective-permute-done.1.refs_4_), channel_id=1, source_target_pairs={{0,2},{2,0},{4,6},{6,4},{8,10},{10,8},{12,14},{14,12},{16,18},{18,... | collective-permute-start | bytes 393224 | tf_op jit(solution)/shard_map/ppermute | solution.py:266
  16.7 4.3 %collective-permute-start.9 = (bf16[2,4,8,1024]{3,2,1,0:T(8,128)(2,1)S(1)}, bf16[2,4,8,1024]{3,2,1,0:T(8,128)(2,1)S(1)}, u32[]{:S(2)}, u32[]{:S(2)}) collective-permute-start(bf16[2,4,8,1024]{3,2,1,0:T(8,128)(2,1)S(1)} %collective-permute-done.8.refs_10_), channel_id=1, source_target_pairs={{0,2},{2,0},{4,6},{6,4},{8,10},{10,8},{12,14},{14,12},{16,18},{18,... | collective-permute-start | bytes 393224 | tf_op jit(solution)/shard_map/ppermute | solution.py:266
  18.9 1.3 %collective-permute-start.4 = (bf16[4,8,1024]{2,1,0:T(8,128)(2,1)S(1)}, bf16[4,8,1024]{2,1,0:T(8,128)(2,1)S(1)}, u32[]{:S(2)}, u32[]{:S(2)}) collective-permute-start(bf16[4,8,1024]{2,1,0:T(8,128)(2,1)S(1)} %collective-permute-done.3.refs_5_), channel_id=1, source_target_pairs={{0,2},{2,0},{4,6},{6,4},{8,10},{10,8},{12,14},{14,12},{16,18},{18,... | collective-permute-start | bytes 196616 | tf_op jit(solution)/shard_map/ppermute | solution.py:266
  19.7 1.3 %collective-permute-start.11 = (bf16[4,8,1024]{2,1,0:T(8,128)(2,1)S(1)}, bf16[4,8,1024]{2,1,0:T(8,128)(2,1)S(1)}, u32[]{:S(2)}, u32[]{:S(2)}) collective-permute-start(bf16[4,8,1024]{2,1,0:T(8,128)(2,1)S(1)} %collective-permute-done.10.refs_11_), channel_id=1, source_target_pairs={{0,2},{2,0},{4,6},{6,4},{8,10},{10,8},{12,14},{14,12},{16,18},{18,... | collective-permute-start | bytes 196616 | tf_op jit(solution)/shard_map/ppermute | solution.py:266
  21.7 4.4 %collective-permute-start.12 = (f32[136,128]{1,0:T(8,128)S(1)}, f32[136,128]{1,0:T(8,128)S(1)}, u32[]{:S(2)}, u32[]{:S(2)}) collective-permute-start(f32[136,128]{1,0:T(8,128)S(1)} %get-tuple-element.16), channel_id=1, source_target_pairs={{0,1},{1,0},{2,3},{3,2},{4,5},{5,4},{6,7},{7,6},{8,9},{9,8},{10,11... | collective-permute-start | bytes 208904 | tf_op jit(solution)/shard_map/ppermute | solution.py:367

commit v3 on v1

--- a/solution.py
+++ b/solution.py
@@ -199,24 +199,32 @@
             r_ref[seg, start:stop, half:] = jnp.concatenate(bottom, axis=0).astype(jnp.bfloat16)
 
 
-def correlate_kernel(*refs):
-    r_ref, keep_ref, send_ref = refs[0], refs[-2], refs[-1]
-    blocks = refs[1:-2]
-    rows = keep_ref.shape[0]
+def products(r_ref, blocks, start, rows):
     total = None
     for seg in range(r_ref.shape[0]):
-        first = []
-        for at in range(0, len(blocks), 6):
-            block, mate, pair_mate, pair, cross, cross_mate = blocks[at : at + 6]
-            first += [block[seg], mate[seg], pair_mate[1, seg], pair_mate[0, seg]]
-            first += [pair[0, seg], pair[1, seg], cross[seg], cross_mate[seg]]
-        first = jnp.concatenate(first, axis=0)
+        block, mate, pair_mate, pair, cross, cross_mate = blocks[:6]
+        first = [block[seg], mate[seg], pair_mate[1, seg], pair_mate[0, seg]]
+        first += [pair[0, seg], pair[1, seg], cross[seg], cross_mate[seg]]
+        first += [b[seg] for b in blocks[6:]]
         term = lax.dot_general(
-            r_ref[seg], first, (((1,), (1,)), ((), ())), preferred_element_type=jnp.float32
+            r_ref[seg, start : start + rows],
+            jnp.concatenate(first, axis=0),
+            (((1,), (1,)), ((), ())),
+            preferred_element_type=jnp.float32,
         )
         total = term if total is None else total + term
-    keep_ref[...] = total[:rows]
-    send_ref[...] = total[rows:]
+    return total
+
+
+def send_kernel(*refs):
+    r_ref, blocks, send_ref = refs[0], refs[1:-1], refs[-1]
+    rows = send_ref.shape[0]
+    send_ref[...] = products(r_ref, blocks, rows, rows).astype(send_ref.dtype)
+
+
+def keep_kernel(*refs):
+    r_ref, blocks, keep_ref = refs[0], refs[1:-1], refs[-1]
+    keep_ref[...] = products(r_ref, blocks, 0, keep_ref.shape[0])
 
 
 def pair_kernel(a_ref, b_ref, out_ref):
@@ -225,21 +233,14 @@
 
 
 def finish_kernel(scale, own, me_ref, keep_ref, got_ref, out_ref):
-    lags, part, lanes = out_ref.shape
-    value = (keep_ref[: lags * part] + got_ref[: lags * part]) * scale
+    lags, part, _ = out_ref.shape
+    value = (keep_ref[...] + got_ref[...].astype(jnp.float32)) * scale
     lane = lax.broadcasted_iota(jnp.int32, value.shape, 1)
-    low, high = (lane & (2 * own)) != 0, (lane & (4 * own)) != 0
-    after, before = pltpu.roll(value, lanes - 2 * own, 1), pltpu.roll(value, 2 * own, 1)
-    crossed = jnp.where(low & ~high, after, jnp.where(high & ~low, before, value))
-    value = jnp.where((me_ref[0] & 1) != 0, crossed, value)
-    width = own
-    bit = 1
-    while width < lanes:
-        up = pltpu.roll(value, width, 1)
-        down = pltpu.roll(value, lanes - width, 1)
-        swapped = jnp.where((lane & width) != 0, up, down)
-        value = jnp.where((me_ref[0] & bit) != 0, swapped, value)
-        width, bit = 2 * width, 2 * bit
+    me = me_ref[0]
+    block = (lane // own) ^ me
+    crossed = (block & ~6) | ((block & 2) << 1) | ((block & 4) >> 1)
+    block = jnp.where(((me & 1) != 0) & (block < 8), crossed, block)
+    value = jnp.take_along_axis(value, block * own + lane % own, axis=1)
     for lag in range(lags):
         out_ref[lag] = value[lag * part : (lag + 1) * part]
 
@@ -273,6 +274,14 @@
     out = []
     for m in held:
         block = blocks[m]
+        if m:
+            parts = []
+            for distance in (NEAR | SIDE, NEAR, SIDE):
+                parts.append(hop(block, col, distance))
+            cross, near, side = parts
+            out += [block, swap(block), side, swap(side)]
+            out += [near, swap(near), cross, swap(cross)]
+            continue
         mate = swap(block)
         cross = hop(block, col, NEAR | SIDE)
         pair = pl.pallas_call(
@@ -341,14 +350,23 @@
         ),
     )(seg_index, whitened, cosines, sines)
 
-    keep, send = pl.pallas_call(
-        correlate_kernel,
-        out_shape=[jax.ShapeDtypeStruct((rows, lanes), jnp.float32)] * 2,
-        in_specs=[VMEM] * (1 + len(blocks)),
-        out_specs=[VMEM] * 2,
-        compiler_params=grant(12),
-    )(rotated, *blocks)
+    def multiply(kernel, dtype):
+        return pl.pallas_call(
+            kernel,
+            out_shape=jax.ShapeDtypeStruct((rows, lanes), dtype),
+            in_specs=[VMEM] * (1 + len(blocks)),
+            out_specs=VMEM,
+            compiler_params=grant(8),
+            cost_estimate=pl.CostEstimate(
+                flops=2 * rows * segs * length * lanes,
+                bytes_accessed=2 * (rows + lanes) * segs * length,
+                transcendentals=0,
+            ),
+        )(rotated, *blocks)
+
+    send = multiply(send_kernel, jnp.bfloat16)
     got = lax.ppermute(send, "seg", [(0, 1), (1, 0)])
+    keep = multiply(keep_kernel, jnp.float32)
     out = pl.pallas_call(
         functools.partial(finish_kernel, scale, own),
         out_shape=jax.ShapeDtypeStruct((lags, part, lanes), jnp.float32),

time: 27.3 us -> 29.6 us (1.084)
  starting transfers between devices: 10.4 us -> 13.1 us
  waiting for transfers between devices: 12.9 us -> 10.5 us
  Pallas kernels: 3.86 us -> 5.66 us
    ppermute x11 -> x13, starting transfers between devices: 8.81 us -> 11.5 us  [hop(): lax.ppermute(array, 'col', [(i, i ^ (other if i & 1 else distance)) for i...]
    pallas_call x1 -> x2, Pallas kernels: 0.74 us -> 2.87 us  [multiply(): pl.pallas_call(kernel, out_shape=jax.ShapeDtypeStruct((rows, lanes), dtyp...]
    ppermute x1, waiting for transfers between devices: 2.82 us -> 1.01 us  [fast_body(): got = lax.ppermute(send, 'seg', [(0, 1), (1, 0)])]
    ppermute x11 -> x13, waiting for transfers between devices: 10.1 us -> 9.51 us  [hop(): lax.ppermute(array, 'col', [(i, i ^ (other if i & 1 else distance)) for i...]
    pallas_call x1, Pallas kernels: 1.06 us -> 0.73 us  [fast_body(): pl.pallas_call(functools.partial(finish_kernel, scale, own), out_shape=ja...]
  transfers between devices with their start and end apart: 12 -> 14, of which waited for: 7 -> 8; matrix products, arithmetic and copies ran while one was open for 0% -> 0% of each run, Pallas kernels for 2% -> 7%
where the time goes in v3:
time: 29.6 us; the launch traced here: 29.3 us
  starting transfers between devices  13.1 us (44%)
  waiting for transfers between devices  10.5 us (35%)
  Pallas kernels  5.66 us (19%)
    ppermute x13, starting transfers between devices, hop(): lax.ppermute(array, 'col', [(i, i ^ (other if i & 1 else distance)) for i...  11.5 us
    ppermute x13, waiting for transfers between devices, hop(): lax.ppermute(array, 'col', [(i, i ^ (other if i & 1 else distance)) for i...  9.51 us
    pallas_call x2, Pallas kernels, multiply(): pl.pallas_call(kernel, out_shape=jax.ShapeDtypeStruct((rows, lanes), dtyp...  2.87 us
    ppermute x1, starting transfers between devices, fast_body(): got = lax.ppermute(send, 'seg', [(0, 1), (1, 0)])  1.55 us
    pallas_call x1, Pallas kernels, fast_body(): pl.pallas_call(whiten_kernel, out_shape=[jax.ShapeDtypeStruct(traces.shap...  1.51 us
    ppermute x1, waiting for transfers between devices, fast_body(): got = lax.ppermute(send, 'seg', [(0, 1), (1, 0)])  1.01 us
    pallas_call x1, Pallas kernels, fast_body(): pl.pallas_call(functools.partial(finish_kernel, scale, own), out_shape=ja...  0.73 us
  transfers between devices with their start and end apart: 14, of which 8 were waited for; matrix products, arithmetic and copies ran while one was open for 0% of the time, Pallas kernels for 7%

profile of v3, /device:TPU:0, one launch (start us, length us, event | category | flops | bytes accessed | tf_op | source)
XLA Modules:
  0.0 29.3 jit_solution(8821901466322009343)
XLA Ops:
  0.0 1.5 %shard_map.55 = (bf16[4,8,1024]{2,1,0:T(8,128)(2,1)S(1)}, f32[136,512]{1,0:T(8,128)S(1)}, f32[136,512]{1,0:T(8,128)S(1)}) custom-call(bf16[4,8,1024]{2,1,0:T(8,128)(2,1)} %x_in.1, s32[4,8]{1,0:T(4,128)} %v_in.1, bf16[256,1024]{1,0:T(8,128)(2,1)} %constant.14.clone.t_in, f32[136,512]{1,0:T(8,128)} %constant.15.clone.c_in, f32[136,512]{1,0:T(8,128)} %constant.16.clone.s_in), custom_call_target="tpu_custom_call" | custom-call | tf_op jit(solution)/shard_map/pallas_call | solution.py:315
  1.5 0.6 %collective-permute-start = (bf16[4,8,1024]{2,1,0:T(8,128)(2,1)S(1)}, bf16[4,8,1024]{2,1,0:T(8,128)(2,1)S(1)}, u32[]{:S(2)}, u32[]{:S(2)}) collective-permute-start(bf16[4,8,1024]{2,1,0:T(8,128)(2,1)S(1)} %get-tuple-element.8.w_ref.a_ref.refs_1_), channel_id=1, source_target_pairs={{0,2},{2,0},{4,6},{6,4},{8,10},{10,8},{12,14},{14,12},{16,18},{18,... | collective-permute-start | bytes 196616 | tf_op jit(solution)/shard_map/ppermute | solution.py:263
  2.1 0.9 %collective-permute-done.b_ref.refs_2_ = bf16[4,8,1024]{2,1,0:T(8,128)(2,1)S(1)} collective-permute-done((bf16[4,8,1024]{2,1,0:T(8,128)(2,1)S(1)}, bf16[4,8,1024]{2,1,0:T(8,128)(2,1)S(1)}, u32[]{:S(2)}, u32[]{:S(2)}) %collective-permute-start) | collective-permute-done | bytes 65568 | tf_op jit(solution)/shard_map/ppermute | solution.py:263
  3.0 3.0 %collective-permute-start.1 = (bf16[2,4,8,1024]{3,2,1,0:T(8,128)(2,1)S(1)}, bf16[2,4,8,1024]{3,2,1,0:T(8,128)(2,1)S(1)}, u32[]{:S(2)}, u32[]{:S(2)}) collective-permute-start(bf16[2,4,8,1024]{3,2,1,0:T(8,128)(2,1)S(1)} %shard_map.57), channel_id=1, source_target_pairs={{0,8},{2,6},{4,12},{6,2},{8,0},{10,14},{12,4},{14,10},{16,24},{18,... | collective-permute-start | bytes 393224 | tf_op jit(solution)/shard_map/ppermute | solution.py:263
  6.0 1.4 %collective-permute-start.3 = (bf16[4,8,1024]{2,1,0:T(8,128)(2,1)S(1)}, bf16[4,8,1024]{2,1,0:T(8,128)(2,1)S(1)}, u32[]{:S(2)}, u32[]{:S(2)}) collective-permute-start(bf16[4,8,1024]{2,1,0:T(8,128)(2,1)S(1)} %get-tuple-element.8.w_ref.a_ref.refs_1_), channel_id=1, source_target_pairs={{0,12},{2,14},{4,8},{6,10},{8,4},{10,6},{12,0},{14,2},{16,28},{18,... | collective-permute-start | bytes 196616 | tf_op jit(solution)/shard_map/ppermute | solution.py:263
  7.4 2.6 %collective-permute-start.5 = (bf16[4,8,1024]{2,1,0:T(8,128)(2,1)S(1)}, bf16[4,8,1024]{2,1,0:T(8,128)(2,1)S(1)}, u32[]{:S(2)}, u32[]{:S(2)}) collective-permute-start(bf16[4,8,1024]{2,1,0:T(8,128)(2,1)S(1)} %get-tuple-element.8.w_ref.a_ref.refs_1_), channel_id=1, source_target_pairs={{0,16},{2,18},{4,20},{6,22},{8,24},{10,26},{12,28},{14,30},{16,0},... | collective-permute-start | bytes 196616 | tf_op jit(solution)/shard_map/ppermute | solution.py:263
  10.0 3.2 %collective-permute-done.3.refs_5_ = bf16[4,8,1024]{2,1,0:T(8,128)(2,1)S(1)} collective-permute-done((bf16[4,8,1024]{2,1,0:T(8,128)(2,1)S(1)}, bf16[4,8,1024]{2,1,0:T(8,128)(2,1)S(1)}, u32[]{:S(2)}, u32[]{:S(2)}) %collective-permute-start.3) | collective-permute-done | bytes 65568 | tf_op jit(solution)/shard_map/ppermute | solution.py:263
  13.1 0.0 collective-permute-start.4
  13.1 0.1 collective-permute-done.5.refs_7_
  13.2 0.4 %collective-permute-start.7 = (bf16[4,8,1024]{2,1,0:T(8,128)(2,1)S(1)}, bf16[4,8,1024]{2,1,0:T(8,128)(2,1)S(1)}, u32[]{:S(2)}, u32[]{:S(2)}) collective-permute-start(bf16[4,8,1024]{2,1,0:T(8,128)(2,1)S(1)} %collective-permute-done.5.refs_7_), channel_id=1, source_target_pairs={{0,4},{2,6},{4,0},{6,2},{8,12},{10,14},{12,8},{14,10},{16,20},{18,... | collective-permute-start | bytes 196616 | tf_op jit(solution)/shard_map/ppermute | solution.py:263
  13.6 2.7 %collective-permute-start.9 = (bf16[4,8,1024]{2,1,0:T(8,128)(2,1)S(1)}, bf16[4,8,1024]{2,1,0:T(8,128)(2,1)S(1)}, u32[]{:S(2)}, u32[]{:S(2)}) collective-permute-start(bf16[4,8,1024]{2,1,0:T(8,128)(2,1)S(1)} %collective-permute-done.5.refs_7_), channel_id=1, source_target_pairs={{0,8},{2,10},{4,12},{6,14},{8,0},{10,2},{12,4},{14,6},{16,24},{18,... | collective-permute-start | bytes 196616 | tf_op jit(solution)/shard_map/ppermute | solution.py:263
  16.3 0.4 %collective-permute-start.11 = (bf16[4,8,1024]{2,1,0:T(8,128)(2,1)S(1)}, bf16[4,8,1024]{2,1,0:T(8,128)(2,1)}, u32[]{:S(2)}, u32[]{:S(2)}) collective-permute-start(bf16[4,8,1024]{2,1,0:T(8,128)(2,1)S(1)} %collective-permute-done.5.refs_7_), channel_id=1, source_target_pairs={{0,12},{2,14},{4,8},{6,10},{8,4},{10,6},{12,0},{14,2},{16,28},{18,... | collective-permute-start | bytes 196616 | tf_op jit(solution)/shard_map/ppermute | solution.py:263
  16.7 0.0 collective-permute-done.1.refs_4_
  16.7 0.0 collective-permute-start.2
  16.7 0.0 collective-permute-done.4.refs_6_
  16.7 0.5 %collective-permute-start.6 = (bf16[4,8,1024]{2,1,0:T(8,128)(2,1)S(1)}, bf16[4,8,1024]{2,1,0:T(8,128)(2,1)}, u32[]{:S(2)}, u32[]{:S(2)}) collective-permute-start(bf16[4,8,1024]{2,1,0:T(8,128)(2,1)S(1)} %collective-permute-done.5.refs_7_), channel_id=1, source_target_pairs={{0,2},{2,0},{4,6},{6,4},{8,10},{10,8},{12,14},{14,12},{16,18},{18,... | collective-permute-start | bytes 196616 | tf_op jit(solution)/shard_map/ppermute | solution.py:263
  17.2 0.4 %collective-permute-done.7.refs_9_ = bf16[4,8,1024]{2,1,0:T(8,128)(2,1)S(1)} collective-permute-done((bf16[4,8,1024]{2,1,0:T(8,128)(2,1)S(1)}, bf16[4,8,1024]{2,1,0:T(8,128)(2,1)S(1)}, u32[]{:S(2)}, u32[]{:S(2)}) %collective-permute-start.7) | collective-permute-done | bytes 65568 | tf_op jit(solution)/shard_map/ppermute | solution.py:263
  17.6 0.0 collective-permute-start.8
  17.6 1.2 %collective-permute-done.9.refs_11_ = bf16[4,8,1024]{2,1,0:T(8,128)(2,1)S(1)} collective-permute-done((bf16[4,8,1024]{2,1,0:T(8,128)(2,1)S(1)}, bf16[4,8,1024]{2,1,0:T(8,128)(2,1)S(1)}, u32[]{:S(2)}, u32[]{:S(2)}) %collective-permute-start.9) | collective-permute-done | bytes 65568 | tf_op jit(solution)/shard_map/ppermute | solution.py:263
  18.8 0.0 collective-permute-start.10
  18.8 2.7 %collective-permute-done.11.refs_13_ = bf16[4,8,1024]{2,1,0:T(8,128)(2,1)} collective-permute-done((bf16[4,8,1024]{2,1,0:T(8,128)(2,1)S(1)}, bf16[4,8,1024]{2,1,0:T(8,128)(2,1)}, u32[]{:S(2)}, u32[]{:S(2)}) %collective-permute-start.11) | collective-permute-done | bytes 65568 | tf_op jit(solution)/shard_map/ppermute | solution.py:263
  21.5 0.0 collective-permute-start.12
  21.6 0.5 %shard_map.56.refs_0_ = bf16[4,272,1024]{2,1,0:T(8,128)(2,1)S(1)} custom-call(s32[1]{0:T(128)} %bitcast.1.seg_ref, bf16[4,8,1024]{2,1,0:T(8,128)(2,1)S(1)} %get-tuple-element.8.w_ref.a_ref.refs_1_, f32[136,512]{1,0:T(8,128)S(1)} %get-tuple-element.9.c_ref, f32[136,512]{1,0:T(8,128)S(1)} %get-tuple-element.10.s_ref), custom_call_target="tpu_custom_call" | custom-call | flops 6684672 | bytes 2228224 | tf_op jit(solution)/shard_map/pallas_call | solution.py:340
  22.1 0.0 collective-permute-done.6.refs_8_
  22.1 0.0 collective-permute-done.8.refs_10_
  22.1 0.0 collective-permute-done.10.refs_12_
  22.1 1.0 %collective-permute-done.12.refs_14_ = bf16[4,8,1024]{2,1,0:T(8,128)(2,1)} collective-permute-done((bf16[4,8,1024]{2,1,0:T(8,128)(2,1)}, bf16[4,8,1024]{2,1,0:T(8,128)(2,1)}, u32[]{:S(2)}, u32[]{:S(2)}) %collective-permute-start.12) | collective-permute-done | bytes 65568 | tf_op jit(solution)/shard_map/ppermute | solution.py:263
  23.1 0.0 collective-permute-done.2.refs_3_
  23.1 1.4 %shard_map.59 = bf16[136,128]{1,0:T(8,128)(2,1)S(1)} custom-call(bf16[4,272,1024]{2,1,0:T(8,128)(2,1)S(1)} %shard_map.56.refs_0_, bf16[4,8,1024]{2,1,0:T(8,128)(2,1)S(1)} %get-tuple-element.8.w_ref.a_ref.refs_1_, bf16[4,8,1024]{2,1,0:T(8,128)(2,1)S(1)} %collective-permute-done.b_ref.refs_2_, bf16[2,4,8,1024]{3,2,1,0:T(8,128)(2,1)S(1)} %collective-permute-done.2.refs_3_, ...), custom_call_target="tpu_custom_call" | custom-call | flops 142606336 | bytes 2162688 | tf_op jit(solution)/shard_map/pallas_call | solution.py:354
  24.6 1.6 %collective-permute-start.13 = (bf16[136,128]{1,0:T(8,128)(2,1)S(1)}, bf16[136,128]{1,0:T(8,128)(2,1)S(1)}, u32[]{:S(2)}, u32[]{:S(2)}) collective-permute-start(bf16[136,128]{1,0:T(8,128)(2,1)S(1)} %shard_map.59), channel_id=1, source_target_pairs={{0,1},{1,0},{2,3},{3,2},{4,5},{5,4},{6,7},{7,6},{8,9},{9,8},{10,11... | collective-permute-start | bytes 104456 | tf_op jit(solution)/shard_map/ppermute | solution.py:368
  26.2 1.4 %shard_map.58.keep_ref = f32[136,128]{1,0:T(8,128)S(1)} custom-call(bf16[4,272,1024]{2,1,0:T(8,128)(2,1)S(1)} %shard_map.56.refs_0_, bf16[4,8,1024]{2,1,0:T(8,128)(2,1)S(1)} %get-tuple-element.8.w_ref.a_ref.refs_1_, bf16[4,8,1024]{2,1,0:T(8,128)(2,1)S(1)} %collective-permute-done.b_ref.refs_2_, bf16[2,4,8,1024]{3,2,1,0:T(8,128)(2,1)S(1)} %collective-permute-done.2.refs_3_, ...), custom_call_target="tpu_custom_call" | custom-call | flops 142606336 | bytes 2162688 | tf_op jit(solution)/shard_map/pallas_call | solution.py:354
  27.6 1.0 %collective-permute-done.13.got_ref = bf16[136,128]{1,0:T(8,128)(2,1)S(1)} collective-permute-done((bf16[136,128]{1,0:T(8,128)(2,1)S(1)}, bf16[136,128]{1,0:T(8,128)(2,1)S(1)}, u32[]{:S(2)}, u32[]{:S(2)}) %collective-permute-start.13) | collective-permute-done | bytes 34848 | tf_op jit(solution)/shard_map/ppermute | solution.py:368
  28.6 0.7 %shard_map.60 = f32[33,4,128]{2,1,0:T(4,128)} custom-call(s32[1]{0:T(128)} %bitcast.me_ref, f32[136,128]{1,0:T(8,128)S(1)} %shard_map.58.keep_ref, bf16[136,128]{1,0:T(8,128)(2,1)S(1)} %collective-permute-done.13.got_ref), custom_call_target="tpu_custom_call" | custom-call | tf_op jit(solution)/shard_map/pallas_call | solution.py:370
  (1 shorter events, 0.0 us)
Async XLA Ops:
  1.5 1.5 %collective-permute-start = (bf16[4,8,1024]{2,1,0:T(8,128)(2,1)S(1)}, bf16[4,8,1024]{2,1,0:T(8,128)(2,1)S(1)}, u32[]{:S(2)}, u32[]{:S(2)}) collective-permute-start(bf16[4,8,1024]{2,1,0:T(8,128)(2,1)S(1)} %get-tuple-element.8.w_ref.a_ref.refs_1_), channel_id=1, source_target_pairs={{0,2},{2,0},{4,6},{6,4},{8,10},{10,8},{12,14},{14,12},{16,18},{18,... | collective-permute-start | bytes 196616 | tf_op jit(solution)/shard_map/ppermute | solution.py:263
  3.0 13.7 %collective-permute-start.1 = (bf16[2,4,8,1024]{3,2,1,0:T(8,128)(2,1)S(1)}, bf16[2,4,8,1024]{3,2,1,0:T(8,128)(2,1)S(1)}, u32[]{:S(2)}, u32[]{:S(2)}) collective-permute-start(bf16[2,4,8,1024]{3,2,1,0:T(8,128)(2,1)S(1)} %shard_map.57), channel_id=1, source_target_pairs={{0,8},{2,6},{4,12},{6,2},{8,0},{10,14},{12,4},{14,10},{16,24},{18,... | collective-permute-start | bytes 393224 | tf_op jit(solution)/shard_map/ppermute | solution.py:263
  6.0 7.2 %collective-permute-start.3 = (bf16[4,8,1024]{2,1,0:T(8,128)(2,1)S(1)}, bf16[4,8,1024]{2,1,0:T(8,128)(2,1)S(1)}, u32[]{:S(2)}, u32[]{:S(2)}) collective-permute-start(bf16[4,8,1024]{2,1,0:T(8,128)(2,1)S(1)} %get-tuple-element.8.w_ref.a_ref.refs_1_), channel_id=1, source_target_pairs={{0,12},{2,14},{4,8},{6,10},{8,4},{10,6},{12,0},{14,2},{16,28},{18,... | collective-permute-start | bytes 196616 | tf_op jit(solution)/shard_map/ppermute | solution.py:263
  7.4 5.8 %collective-permute-start.5 = (bf16[4,8,1024]{2,1,0:T(8,128)(2,1)S(1)}, bf16[4,8,1024]{2,1,0:T(8,128)(2,1)S(1)}, u32[]{:S(2)}, u32[]{:S(2)}) collective-permute-start(bf16[4,8,1024]{2,1,0:T(8,128)(2,1)S(1)} %get-tuple-element.8.w_ref.a_ref.refs_1_), channel_id=1, source_target_pairs={{0,16},{2,18},{4,20},{6,22},{8,24},{10,26},{12,28},{14,30},{16,0},... | collective-permute-start | bytes 196616 | tf_op jit(solution)/shard_map/ppermute | solution.py:263
  13.1 3.6 %collective-permute-start.4 = (bf16[4,8,1024]{2,1,0:T(8,128)(2,1)S(1)}, bf16[4,8,1024]{2,1,0:T(8,128)(2,1)S(1)}, u32[]{:S(2)}, u32[]{:S(2)}) collective-permute-start(bf16[4,8,1024]{2,1,0:T(8,128)(2,1)S(1)} %collective-permute-done.3.refs_5_), channel_id=1, source_target_pairs={{0,2},{2,0},{4,6},{6,4},{8,10},{10,8},{12,14},{14,12},{16,18},{18,... | collective-permute-start | bytes 196616 | tf_op jit(solution)/shard_map/ppermute | solution.py:263
  13.2 4.4 %collective-permute-start.7 = (bf16[4,8,1024]{2,1,0:T(8,128)(2,1)S(1)}, bf16[4,8,1024]{2,1,0:T(8,128)(2,1)S(1)}, u32[]{:S(2)}, u32[]{:S(2)}) collective-permute-start(bf16[4,8,1024]{2,1,0:T(8,128)(2,1)S(1)} %collective-permute-done.5.refs_7_), channel_id=1, source_target_pairs={{0,4},{2,6},{4,0},{6,2},{8,12},{10,14},{12,8},{14,10},{16,20},{18,... | collective-permute-start | bytes 196616 | tf_op jit(solution)/shard_map/ppermute | solution.py:263
  13.6 5.3 %collective-permute-start.9 = (bf16[4,8,1024]{2,1,0:T(8,128)(2,1)S(1)}, bf16[4,8,1024]{2,1,0:T(8,128)(2,1)S(1)}, u32[]{:S(2)}, u32[]{:S(2)}) collective-permute-start(bf16[4,8,1024]{2,1,0:T(8,128)(2,1)S(1)} %collective-permute-done.5.refs_7_), channel_id=1, source_target_pairs={{0,8},{2,10},{4,12},{6,14},{8,0},{10,2},{12,4},{14,6},{16,24},{18,... | collective-permute-start | bytes 196616 | tf_op jit(solution)/shard_map/ppermute | solution.py:263
  16.3 5.3 %collective-permute-start.11 = (bf16[4,8,1024]{2,1,0:T(8,128)(2,1)S(1)}, bf16[4,8,1024]{2,1,0:T(8,128)(2,1)}, u32[]{:S(2)}, u32[]{:S(2)}) collective-permute-start(bf16[4,8,1024]{2,1,0:T(8,128)(2,1)S(1)} %collective-permute-done.5.refs_7_), channel_id=1, source_target_pairs={{0,12},{2,14},{4,8},{6,10},{8,4},{10,6},{12,0},{14,2},{16,28},{18,... | collective-permute-start | bytes 196616 | tf_op jit(solution)/shard_map/ppermute | solution.py:263
  16.7 6.5 %collective-permute-start.2 = (bf16[2,4,8,1024]{3,2,1,0:T(8,128)(2,1)S(1)}, bf16[2,4,8,1024]{3,2,1,0:T(8,128)(2,1)S(1)}, u32[]{:S(2)}, u32[]{:S(2)}) collective-permute-start(bf16[2,4,8,1024]{3,2,1,0:T(8,128)(2,1)S(1)} %collective-permute-done.1.refs_4_), channel_id=1, source_target_pairs={{0,2},{2,0},{4,6},{6,4},{8,10},{10,8},{12,14},{14,12},{16,18},{18,... | collective-permute-start | bytes 393224 | tf_op jit(solution)/shard_map/ppermute | solution.py:263
  16.7 5.4 %collective-permute-start.6 = (bf16[4,8,1024]{2,1,0:T(8,128)(2,1)S(1)}, bf16[4,8,1024]{2,1,0:T(8,128)(2,1)}, u32[]{:S(2)}, u32[]{:S(2)}) collective-permute-start(bf16[4,8,1024]{2,1,0:T(8,128)(2,1)S(1)} %collective-permute-done.5.refs_7_), channel_id=1, source_target_pairs={{0,2},{2,0},{4,6},{6,4},{8,10},{10,8},{12,14},{14,12},{16,18},{18,... | collective-permute-start | bytes 196616 | tf_op jit(solution)/shard_map/ppermute | solution.py:263
  17.6 4.5 %collective-permute-start.8 = (bf16[4,8,1024]{2,1,0:T(8,128)(2,1)S(1)}, bf16[4,8,1024]{2,1,0:T(8,128)(2,1)}, u32[]{:S(2)}, u32[]{:S(2)}) collective-permute-start(bf16[4,8,1024]{2,1,0:T(8,128)(2,1)S(1)} %collective-permute-done.7.refs_9_), channel_id=1, source_target_pairs={{0,2},{2,0},{4,6},{6,4},{8,10},{10,8},{12,14},{14,12},{16,18},{18,... | collective-permute-start | bytes 196616 | tf_op jit(solution)/shard_map/ppermute | solution.py:263
  18.8 3.3 %collective-permute-start.10 = (bf16[4,8,1024]{2,1,0:T(8,128)(2,1)S(1)}, bf16[4,8,1024]{2,1,0:T(8,128)(2,1)}, u32[]{:S(2)}, u32[]{:S(2)}) collective-permute-start(bf16[4,8,1024]{2,1,0:T(8,128)(2,1)S(1)} %collective-permute-done.9.refs_11_), channel_id=1, source_target_pairs={{0,2},{2,0},{4,6},{6,4},{8,10},{10,8},{12,14},{14,12},{16,18},{18,... | collective-permute-start | bytes 196616 | tf_op jit(solution)/shard_map/ppermute | solution.py:263
  21.5 1.6 %collective-permute-start.12 = (bf16[4,8,1024]{2,1,0:T(8,128)(2,1)}, bf16[4,8,1024]{2,1,0:T(8,128)(2,1)}, u32[]{:S(2)}, u32[]{:S(2)}) collective-permute-start(bf16[4,8,1024]{2,1,0:T(8,128)(2,1)} %collective-permute-done.11.refs_13_), channel_id=1, source_target_pairs={{0,2},{2,0},{4,6},{6,4},{8,10},{10,8},{12,14},{14,12},{16,18},{18,... | collective-permute-start | bytes 196616 | tf_op jit(solution)/shard_map/ppermute | solution.py:263
  24.6 4.0 %collective-permute-start.13 = (bf16[136,128]{1,0:T(8,128)(2,1)S(1)}, bf16[136,128]{1,0:T(8,128)(2,1)S(1)}, u32[]{:S(2)}, u32[]{:S(2)}) collective-permute-start(bf16[136,128]{1,0:T(8,128)(2,1)S(1)} %shard_map.59), channel_id=1, source_target_pairs={{0,1},{1,0},{2,3},{3,2},{4,5},{5,4},{6,7},{7,6},{8,9},{9,8},{10,11... | collective-permute-start | bytes 104456 | tf_op jit(solution)/shard_map/ppermute | solution.py:368

commit v4 on v3

--- a/solution.py
+++ b/solution.py
@@ -89,12 +89,6 @@
     return np.concatenate([np.arange(r, length // 2, 4) for r in range(4)])
 
 
-def quarter_table(length):
-    product = np.arange(length // 4)[:, None] * bin_order(length)[None, :] % length
-    angle = 2.0 * np.pi / length * product
-    return np.concatenate([np.cos(angle), -np.sin(angle)], axis=1).astype(jnp.bfloat16)
-
-
 def lag_tables(length, max_shift, copies, rows):
     shifts = np.arange(2 * max_shift + 1) - max_shift
     product = shifts[:, None] * bin_order(length)[None, :] % length
@@ -107,15 +101,47 @@
     return out
 
 
-def whiten_kernel(
-    x_in, v_in, t_in, c_in, s_in, w_ref, c_out, s_out, x_ref, v_ref, t_ref, sems
-):
-    pairs = ((x_in, x_ref), (t_in, t_ref), (v_in, v_ref), (c_in, c_out), (s_in, s_out))
+def turn(index, length):
+    quadrant = (index + length // 8) // (length // 4)
+    angle = (index - quadrant * (length // 4)).astype(jnp.float32) * (2.0 * math.pi / length)
+    square = angle * angle
+    sine, cosine = 1.0 / 362880, 1.0 / 40320
+    for top, bottom in ((-1.0 / 5040, -1.0 / 720), (1.0 / 120, 1.0 / 24), (-1.0 / 6, -0.5), (1.0, 1.0)):
+        sine, cosine = sine * square + top, cosine * square + bottom
+    sine = sine * angle
+    odd = (quadrant & 1) != 0
+    flip_sine = (quadrant & 2) != 0
+    flip_cosine = ((quadrant + 1) & 2) != 0
+    first, second = jnp.where(odd, sine, cosine), jnp.where(odd, cosine, sine)
+    return jnp.where(flip_cosine, -first, first), jnp.where(flip_sine, -second, second)
+
+
+def make_quarter_table(t_ref, e_ref):
+    _, length = t_ref.shape
+    half, coarse = length // 2, t_ref.shape[0] // 16
+    column = lax.broadcasted_iota(jnp.int32, (16, half), 1)
+    group = half // 4
+    bins = 4 * (column % group) + column // group
+    row = lax.broadcasted_iota(jnp.int32, (16, half), 0)
+    fine_cos, fine_sin = turn(row * bins % length, length)
+    for start in range(0, coarse, 16):
+        cosine, sine = turn((row + start) * 16 * bins % length, length)
+        e_ref[0, start : start + 16], e_ref[1, start : start + 16] = cosine, sine
+    for i in range(coarse):
+        cosine, sine = e_ref[0, i : i + 1], e_ref[1, i : i + 1]
+        at = slice(16 * i, 16 * i + 16)
+        t_ref[at, :half] = (cosine * fine_cos - sine * fine_sin).astype(t_ref.dtype)
+        t_ref[at, half:] = (-(sine * fine_cos + cosine * fine_sin)).astype(t_ref.dtype)
+
+
+def whiten_kernel(x_in, v_in, c_in, s_in, w_ref, c_out, s_out, x_ref, v_ref, t_ref, e_ref, sems):
+    pairs = ((x_in, x_ref), (v_in, v_ref), (c_in, c_out), (s_in, s_out))
     copies = [pltpu.make_async_copy(a, b, sems.at[i]) for i, (a, b) in enumerate(pairs)]
     for copy in copies:
         copy.start()
     segs, own, length = x_ref.shape
-    for copy in copies[:3]:
+    make_quarter_table(t_ref, e_ref)
+    for copy in copies[:2]:
         copy.wait()
     quarter, half = length // 4, length // 2
     rows, group = segs * own, half // 4
@@ -167,7 +193,7 @@
         for base, part in ((0, real[r]), (half, imag[r])):
             value = (part * factor).astype(jnp.bfloat16).reshape(segs, own, group)
             w_ref[:, :, base + r * group : base + (r + 1) * group] = value
-    for copy in copies[3:]:
+    for copy in copies[2:]:
         copy.wait()
 
 
@@ -310,7 +336,6 @@
     seg_index = lax.axis_index("seg").astype(jnp.int32).reshape(1)
     scale = 1.0 / math.sqrt(segs * lax.axis_size("seg") * half)
 
-    table = quarter_table(length)
     lag_cos, lag_sin = lag_tables(length, MAXLAG, part, rows)
     whitened, cosines, sines = pl.pallas_call(
         whiten_kernel,
@@ -319,19 +344,20 @@
             jax.ShapeDtypeStruct(lag_cos.shape, jnp.float32),
             jax.ShapeDtypeStruct(lag_sin.shape, jnp.float32),
         ],
-        in_specs=[HBM] * 5,
+        in_specs=[HBM] * 4,
         out_specs=[VMEM] * 3,
         scratch_shapes=[
             pltpu.VMEM(traces.shape, traces.dtype),
             pltpu.VMEM(valid.shape, valid.dtype),
-            pltpu.VMEM(table.shape, table.dtype),
-            pltpu.SemaphoreType.DMA((5,)),
+            pltpu.VMEM((length // 4, length), jnp.bfloat16),
+            pltpu.VMEM((2, length // 64, half), jnp.float32),
+            pltpu.SemaphoreType.DMA((4,)),
         ],
         compiler_params=grant(4),
     )(
         *[
             pltpu.with_memory_space_constraint(jnp.asarray(t), pltpu.HBM)
-            for t in (traces, valid, table, lag_cos, lag_sin)
+            for t in (traces, valid, lag_cos, lag_sin)
         ]
     )
 

time: 29.6 us -> 29.3 us (0.990)
  no operation moved by 1% of the time
where the time goes in v4:
time: 29.3 us; the launch traced here: 29.1 us
  starting transfers between devices  13.1 us (45%)
  waiting for transfers between devices  10.5 us (36%)
  Pallas kernels  5.39 us (18%)
    ppermute x13, starting transfers between devices, hop(): lax.ppermute(array, 'col', [(i, i ^ (other if i & 1 else distance)) for i...  11.5 us
    ppermute x13, waiting for transfers between devices, hop(): lax.ppermute(array, 'col', [(i, i ^ (other if i & 1 else distance)) for i...  9.51 us
    pallas_call x2, Pallas kernels, multiply(): pl.pallas_call(kernel, out_shape=jax.ShapeDtypeStruct((rows, lanes), dtyp...  2.87 us
    ppermute x1, starting transfers between devices, fast_body(): got = lax.ppermute(send, 'seg', [(0, 1), (1, 0)])  1.56 us
    pallas_call x1, Pallas kernels, fast_body(): pl.pallas_call(whiten_kernel, out_shape=[jax.ShapeDtypeStruct(traces.shap...  1.25 us
    ppermute x1, waiting for transfers between devices, fast_body(): got = lax.ppermute(send, 'seg', [(0, 1), (1, 0)])  0.99 us
    pallas_call x1, Pallas kernels, fast_body(): pl.pallas_call(functools.partial(finish_kernel, scale, own), out_shape=ja...  0.73 us
  transfers between devices with their start and end apart: 14, of which 8 were waited for; matrix products, arithmetic and copies ran while one was open for 0% of the time, Pallas kernels for 7%

profile of v4, /device:TPU:0, one launch (start us, length us, event | category | flops | bytes accessed | tf_op | source)
XLA Modules:
  0.0 29.1 jit_solution(11757720999865756512)
XLA Ops:
  0.0 1.2 %shard_map.46 = (bf16[4,8,1024]{2,1,0:T(8,128)(2,1)S(1)}, f32[136,512]{1,0:T(8,128)S(1)}, f32[136,512]{1,0:T(8,128)S(1)}) custom-call(bf16[4,8,1024]{2,1,0:T(8,128)(2,1)} %x_in.1, s32[4,8]{1,0:T(4,128)} %v_in.1, f32[136,512]{1,0:T(8,128)} %constant.12.clone.c_in, f32[136,512]{1,0:T(8,128)} %constant.13.clone.s_in), custom_call_target="tpu_custom_call" | custom-call | tf_op jit(solution)/shard_map/pallas_call | solution.py:340
  1.3 0.6 %collective-permute-start = (bf16[4,8,1024]{2,1,0:T(8,128)(2,1)S(1)}, bf16[4,8,1024]{2,1,0:T(8,128)(2,1)S(1)}, u32[]{:S(2)}, u32[]{:S(2)}) collective-permute-start(bf16[4,8,1024]{2,1,0:T(8,128)(2,1)S(1)} %get-tuple-element.8.w_ref.a_ref.refs_1_), channel_id=1, source_target_pairs={{0,2},{2,0},{4,6},{6,4},{8,10},{10,8},{12,14},{14,12},{16,18},{18,... | collective-permute-start | bytes 196616 | tf_op jit(solution)/shard_map/ppermute | solution.py:289
  1.8 0.9 %collective-permute-done.b_ref.refs_2_ = bf16[4,8,1024]{2,1,0:T(8,128)(2,1)S(1)} collective-permute-done((bf16[4,8,1024]{2,1,0:T(8,128)(2,1)S(1)}, bf16[4,8,1024]{2,1,0:T(8,128)(2,1)S(1)}, u32[]{:S(2)}, u32[]{:S(2)}) %collective-permute-start) | collective-permute-done | bytes 65568 | tf_op jit(solution)/shard_map/ppermute | solution.py:289
  2.7 3.0 %collective-permute-start.1 = (bf16[2,4,8,1024]{3,2,1,0:T(8,128)(2,1)S(1)}, bf16[2,4,8,1024]{3,2,1,0:T(8,128)(2,1)S(1)}, u32[]{:S(2)}, u32[]{:S(2)}) collective-permute-start(bf16[2,4,8,1024]{3,2,1,0:T(8,128)(2,1)S(1)} %shard_map.48), channel_id=1, source_target_pairs={{0,8},{2,6},{4,12},{6,2},{8,0},{10,14},{12,4},{14,10},{16,24},{18,... | collective-permute-start | bytes 393224 | tf_op jit(solution)/shard_map/ppermute | solution.py:289
  5.7 1.4 %collective-permute-start.3 = (bf16[4,8,1024]{2,1,0:T(8,128)(2,1)S(1)}, bf16[4,8,1024]{2,1,0:T(8,128)(2,1)S(1)}, u32[]{:S(2)}, u32[]{:S(2)}) collective-permute-start(bf16[4,8,1024]{2,1,0:T(8,128)(2,1)S(1)} %get-tuple-element.8.w_ref.a_ref.refs_1_), channel_id=1, source_target_pairs={{0,12},{2,14},{4,8},{6,10},{8,4},{10,6},{12,0},{14,2},{16,28},{18,... | collective-permute-start | bytes 196616 | tf_op jit(solution)/shard_map/ppermute | solution.py:289
  7.1 2.6 %collective-permute-start.5 = (bf16[4,8,1024]{2,1,0:T(8,128)(2,1)S(1)}, bf16[4,8,1024]{2,1,0:T(8,128)(2,1)S(1)}, u32[]{:S(2)}, u32[]{:S(2)}) collective-permute-start(bf16[4,8,1024]{2,1,0:T(8,128)(2,1)S(1)} %get-tuple-element.8.w_ref.a_ref.refs_1_), channel_id=1, source_target_pairs={{0,16},{2,18},{4,20},{6,22},{8,24},{10,26},{12,28},{14,30},{16,0},... | collective-permute-start | bytes 196616 | tf_op jit(solution)/shard_map/ppermute | solution.py:289
  9.7 3.2 %collective-permute-done.3.refs_5_ = bf16[4,8,1024]{2,1,0:T(8,128)(2,1)S(1)} collective-permute-done((bf16[4,8,1024]{2,1,0:T(8,128)(2,1)S(1)}, bf16[4,8,1024]{2,1,0:T(8,128)(2,1)S(1)}, u32[]{:S(2)}, u32[]{:S(2)}) %collective-permute-start.3) | collective-permute-done | bytes 65568 | tf_op jit(solution)/shard_map/ppermute | solution.py:289
  12.9 0.0 collective-permute-start.4
  12.9 0.1 collective-permute-done.5.refs_7_
  12.9 0.4 %collective-permute-start.7 = (bf16[4,8,1024]{2,1,0:T(8,128)(2,1)S(1)}, bf16[4,8,1024]{2,1,0:T(8,128)(2,1)S(1)}, u32[]{:S(2)}, u32[]{:S(2)}) collective-permute-start(bf16[4,8,1024]{2,1,0:T(8,128)(2,1)S(1)} %collective-permute-done.5.refs_7_), channel_id=1, source_target_pairs={{0,4},{2,6},{4,0},{6,2},{8,12},{10,14},{12,8},{14,10},{16,20},{18,... | collective-permute-start | bytes 196616 | tf_op jit(solution)/shard_map/ppermute | solution.py:289
  13.3 2.7 %collective-permute-start.9 = (bf16[4,8,1024]{2,1,0:T(8,128)(2,1)S(1)}, bf16[4,8,1024]{2,1,0:T(8,128)(2,1)S(1)}, u32[]{:S(2)}, u32[]{:S(2)}) collective-permute-start(bf16[4,8,1024]{2,1,0:T(8,128)(2,1)S(1)} %collective-permute-done.5.refs_7_), channel_id=1, source_target_pairs={{0,8},{2,10},{4,12},{6,14},{8,0},{10,2},{12,4},{14,6},{16,24},{18,... | collective-permute-start | bytes 196616 | tf_op jit(solution)/shard_map/ppermute | solution.py:289
  16.0 0.4 %collective-permute-start.11 = (bf16[4,8,1024]{2,1,0:T(8,128)(2,1)S(1)}, bf16[4,8,1024]{2,1,0:T(8,128)(2,1)}, u32[]{:S(2)}, u32[]{:S(2)}) collective-permute-start(bf16[4,8,1024]{2,1,0:T(8,128)(2,1)S(1)} %collective-permute-done.5.refs_7_), channel_id=1, source_target_pairs={{0,12},{2,14},{4,8},{6,10},{8,4},{10,6},{12,0},{14,2},{16,28},{18,... | collective-permute-start | bytes 196616 | tf_op jit(solution)/shard_map/ppermute | solution.py:289
  16.4 0.0 collective-permute-done.1.refs_4_
  16.4 0.0 collective-permute-start.2
  16.4 0.0 collective-permute-done.4.refs_6_
  16.4 0.5 %collective-permute-start.6 = (bf16[4,8,1024]{2,1,0:T(8,128)(2,1)S(1)}, bf16[4,8,1024]{2,1,0:T(8,128)(2,1)}, u32[]{:S(2)}, u32[]{:S(2)}) collective-permute-start(bf16[4,8,1024]{2,1,0:T(8,128)(2,1)S(1)} %collective-permute-done.5.refs_7_), channel_id=1, source_target_pairs={{0,2},{2,0},{4,6},{6,4},{8,10},{10,8},{12,14},{14,12},{16,18},{18,... | collective-permute-start | bytes 196616 | tf_op jit(solution)/shard_map/ppermute | solution.py:289
  16.9 0.4 %collective-permute-done.7.refs_9_ = bf16[4,8,1024]{2,1,0:T(8,128)(2,1)S(1)} collective-permute-done((bf16[4,8,1024]{2,1,0:T(8,128)(2,1)S(1)}, bf16[4,8,1024]{2,1,0:T(8,128)(2,1)S(1)}, u32[]{:S(2)}, u32[]{:S(2)}) %collective-permute-start.7) | collective-permute-done | bytes 65568 | tf_op jit(solution)/shard_map/ppermute | solution.py:289
  17.4 0.0 collective-permute-start.8
  17.4 1.2 %collective-permute-done.9.refs_11_ = bf16[4,8,1024]{2,1,0:T(8,128)(2,1)S(1)} collective-permute-done((bf16[4,8,1024]{2,1,0:T(8,128)(2,1)S(1)}, bf16[4,8,1024]{2,1,0:T(8,128)(2,1)S(1)}, u32[]{:S(2)}, u32[]{:S(2)}) %collective-permute-start.9) | collective-permute-done | bytes 65568 | tf_op jit(solution)/shard_map/ppermute | solution.py:289
  18.6 0.0 collective-permute-start.10
  18.6 2.7 %collective-permute-done.11.refs_13_ = bf16[4,8,1024]{2,1,0:T(8,128)(2,1)} collective-permute-done((bf16[4,8,1024]{2,1,0:T(8,128)(2,1)S(1)}, bf16[4,8,1024]{2,1,0:T(8,128)(2,1)}, u32[]{:S(2)}, u32[]{:S(2)}) %collective-permute-start.11) | collective-permute-done | bytes 65568 | tf_op jit(solution)/shard_map/ppermute | solution.py:289
  21.3 0.0 collective-permute-start.12
  21.3 0.5 %shard_map.47.refs_0_ = bf16[4,272,1024]{2,1,0:T(8,128)(2,1)S(1)} custom-call(s32[1]{0:T(128)} %bitcast.1.seg_ref, bf16[4,8,1024]{2,1,0:T(8,128)(2,1)S(1)} %get-tuple-element.8.w_ref.a_ref.refs_1_, f32[136,512]{1,0:T(8,128)S(1)} %get-tuple-element.9.c_ref, f32[136,512]{1,0:T(8,128)S(1)} %get-tuple-element.10.s_ref), custom_call_target="tpu_custom_call" | custom-call | flops 6684672 | bytes 2228224 | tf_op jit(solution)/shard_map/pallas_call | solution.py:366
  21.8 0.0 collective-permute-done.6.refs_8_
  21.8 0.0 collective-permute-done.8.refs_10_
  21.9 0.0 collective-permute-done.10.refs_12_
  21.9 1.0 %collective-permute-done.12.refs_14_ = bf16[4,8,1024]{2,1,0:T(8,128)(2,1)} collective-permute-done((bf16[4,8,1024]{2,1,0:T(8,128)(2,1)}, bf16[4,8,1024]{2,1,0:T(8,128)(2,1)}, u32[]{:S(2)}, u32[]{:S(2)}) %collective-permute-start.12) | collective-permute-done | bytes 65568 | tf_op jit(solution)/shard_map/ppermute | solution.py:289
  22.9 0.0 collective-permute-done.2.refs_3_
  22.9 1.4 %shard_map.50 = bf16[136,128]{1,0:T(8,128)(2,1)S(1)} custom-call(bf16[4,272,1024]{2,1,0:T(8,128)(2,1)S(1)} %shard_map.47.refs_0_, bf16[4,8,1024]{2,1,0:T(8,128)(2,1)S(1)} %get-tuple-element.8.w_ref.a_ref.refs_1_, bf16[4,8,1024]{2,1,0:T(8,128)(2,1)S(1)} %collective-permute-done.b_ref.refs_2_, bf16[2,4,8,1024]{3,2,1,0:T(8,128)(2,1)S(1)} %collective-permute-done.2.refs_3_, ...), custom_call_target="tpu_custom_call" | custom-call | flops 142606336 | bytes 2162688 | tf_op jit(solution)/shard_map/pallas_call | solution.py:380
  24.3 1.6 %collective-permute-start.13 = (bf16[136,128]{1,0:T(8,128)(2,1)S(1)}, bf16[136,128]{1,0:T(8,128)(2,1)S(1)}, u32[]{:S(2)}, u32[]{:S(2)}) collective-permute-start(bf16[136,128]{1,0:T(8,128)(2,1)S(1)} %shard_map.50), channel_id=1, source_target_pairs={{0,1},{1,0},{2,3},{3,2},{4,5},{5,4},{6,7},{7,6},{8,9},{9,8},{10,11... | collective-permute-start | bytes 104456 | tf_op jit(solution)/shard_map/ppermute | solution.py:394
  25.9 1.4 %shard_map.49.keep_ref = f32[136,128]{1,0:T(8,128)S(1)} custom-call(bf16[4,272,1024]{2,1,0:T(8,128)(2,1)S(1)} %shard_map.47.refs_0_, bf16[4,8,1024]{2,1,0:T(8,128)(2,1)S(1)} %get-tuple-element.8.w_ref.a_ref.refs_1_, bf16[4,8,1024]{2,1,0:T(8,128)(2,1)S(1)} %collective-permute-done.b_ref.refs_2_, bf16[2,4,8,1024]{3,2,1,0:T(8,128)(2,1)S(1)} %collective-permute-done.2.refs_3_, ...), custom_call_target="tpu_custom_call" | custom-call | flops 142606336 | bytes 2162688 | tf_op jit(solution)/shard_map/pallas_call | solution.py:380
  27.3 1.0 %collective-permute-done.13.got_ref = bf16[136,128]{1,0:T(8,128)(2,1)S(1)} collective-permute-done((bf16[136,128]{1,0:T(8,128)(2,1)S(1)}, bf16[136,128]{1,0:T(8,128)(2,1)S(1)}, u32[]{:S(2)}, u32[]{:S(2)}) %collective-permute-start.13) | collective-permute-done | bytes 34848 | tf_op jit(solution)/shard_map/ppermute | solution.py:394
  28.3 0.7 %shard_map.51 = f32[33,4,128]{2,1,0:T(4,128)} custom-call(s32[1]{0:T(128)} %bitcast.me_ref, f32[136,128]{1,0:T(8,128)S(1)} %shard_map.49.keep_ref, bf16[136,128]{1,0:T(8,128)(2,1)S(1)} %collective-permute-done.13.got_ref), custom_call_target="tpu_custom_call" | custom-call | tf_op jit(solution)/shard_map/pallas_call | solution.py:396
  (1 shorter events, 0.0 us)
Async XLA Ops:
  1.3 1.5 %collective-permute-start = (bf16[4,8,1024]{2,1,0:T(8,128)(2,1)S(1)}, bf16[4,8,1024]{2,1,0:T(8,128)(2,1)S(1)}, u32[]{:S(2)}, u32[]{:S(2)}) collective-permute-start(bf16[4,8,1024]{2,1,0:T(8,128)(2,1)S(1)} %get-tuple-element.8.w_ref.a_ref.refs_1_), channel_id=1, source_target_pairs={{0,2},{2,0},{4,6},{6,4},{8,10},{10,8},{12,14},{14,12},{16,18},{18,... | collective-permute-start | bytes 196616 | tf_op jit(solution)/shard_map/ppermute | solution.py:289
  2.7 13.7 %collective-permute-start.1 = (bf16[2,4,8,1024]{3,2,1,0:T(8,128)(2,1)S(1)}, bf16[2,4,8,1024]{3,2,1,0:T(8,128)(2,1)S(1)}, u32[]{:S(2)}, u32[]{:S(2)}) collective-permute-start(bf16[2,4,8,1024]{3,2,1,0:T(8,128)(2,1)S(1)} %shard_map.48), channel_id=1, source_target_pairs={{0,8},{2,6},{4,12},{6,2},{8,0},{10,14},{12,4},{14,10},{16,24},{18,... | collective-permute-start | bytes 393224 | tf_op jit(solution)/shard_map/ppermute | solution.py:289
  5.7 7.2 %collective-permute-start.3 = (bf16[4,8,1024]{2,1,0:T(8,128)(2,1)S(1)}, bf16[4,8,1024]{2,1,0:T(8,128)(2,1)S(1)}, u32[]{:S(2)}, u32[]{:S(2)}) collective-permute-start(bf16[4,8,1024]{2,1,0:T(8,128)(2,1)S(1)} %get-tuple-element.8.w_ref.a_ref.refs_1_), channel_id=1, source_target_pairs={{0,12},{2,14},{4,8},{6,10},{8,4},{10,6},{12,0},{14,2},{16,28},{18,... | collective-permute-start | bytes 196616 | tf_op jit(solution)/shard_map/ppermute | solution.py:289
  7.1 5.8 %collective-permute-start.5 = (bf16[4,8,1024]{2,1,0:T(8,128)(2,1)S(1)}, bf16[4,8,1024]{2,1,0:T(8,128)(2,1)S(1)}, u32[]{:S(2)}, u32[]{:S(2)}) collective-permute-start(bf16[4,8,1024]{2,1,0:T(8,128)(2,1)S(1)} %get-tuple-element.8.w_ref.a_ref.refs_1_), channel_id=1, source_target_pairs={{0,16},{2,18},{4,20},{6,22},{8,24},{10,26},{12,28},{14,30},{16,0},... | collective-permute-start | bytes 196616 | tf_op jit(solution)/shard_map/ppermute | solution.py:289
  12.9 3.6 %collective-permute-start.4 = (bf16[4,8,1024]{2,1,0:T(8,128)(2,1)S(1)}, bf16[4,8,1024]{2,1,0:T(8,128)(2,1)S(1)}, u32[]{:S(2)}, u32[]{:S(2)}) collective-permute-start(bf16[4,8,1024]{2,1,0:T(8,128)(2,1)S(1)} %collective-permute-done.3.refs_5_), channel_id=1, source_target_pairs={{0,2},{2,0},{4,6},{6,4},{8,10},{10,8},{12,14},{14,12},{16,18},{18,... | collective-permute-start | bytes 196616 | tf_op jit(solution)/shard_map/ppermute | solution.py:289
  12.9 4.4 %collective-permute-start.7 = (bf16[4,8,1024]{2,1,0:T(8,128)(2,1)S(1)}, bf16[4,8,1024]{2,1,0:T(8,128)(2,1)S(1)}, u32[]{:S(2)}, u32[]{:S(2)}) collective-permute-start(bf16[4,8,1024]{2,1,0:T(8,128)(2,1)S(1)} %collective-permute-done.5.refs_7_), channel_id=1, source_target_pairs={{0,4},{2,6},{4,0},{6,2},{8,12},{10,14},{12,8},{14,10},{16,20},{18,... | collective-permute-start | bytes 196616 | tf_op jit(solution)/shard_map/ppermute | solution.py:289
  13.3 5.3 %collective-permute-start.9 = (bf16[4,8,1024]{2,1,0:T(8,128)(2,1)S(1)}, bf16[4,8,1024]{2,1,0:T(8,128)(2,1)S(1)}, u32[]{:S(2)}, u32[]{:S(2)}) collective-permute-start(bf16[4,8,1024]{2,1,0:T(8,128)(2,1)S(1)} %collective-permute-done.5.refs_7_), channel_id=1, source_target_pairs={{0,8},{2,10},{4,12},{6,14},{8,0},{10,2},{12,4},{14,6},{16,24},{18,... | collective-permute-start | bytes 196616 | tf_op jit(solution)/shard_map/ppermute | solution.py:289
  16.0 5.3 %collective-permute-start.11 = (bf16[4,8,1024]{2,1,0:T(8,128)(2,1)S(1)}, bf16[4,8,1024]{2,1,0:T(8,128)(2,1)}, u32[]{:S(2)}, u32[]{:S(2)}) collective-permute-start(bf16[4,8,1024]{2,1,0:T(8,128)(2,1)S(1)} %collective-permute-done.5.refs_7_), channel_id=1, source_target_pairs={{0,12},{2,14},{4,8},{6,10},{8,4},{10,6},{12,0},{14,2},{16,28},{18,... | collective-permute-start | bytes 196616 | tf_op jit(solution)/shard_map/ppermute | solution.py:289
  16.4 6.5 %collective-permute-start.2 = (bf16[2,4,8,1024]{3,2,1,0:T(8,128)(2,1)S(1)}, bf16[2,4,8,1024]{3,2,1,0:T(8,128)(2,1)S(1)}, u32[]{:S(2)}, u32[]{:S(2)}) collective-permute-start(bf16[2,4,8,1024]{3,2,1,0:T(8,128)(2,1)S(1)} %collective-permute-done.1.refs_4_), channel_id=1, source_target_pairs={{0,2},{2,0},{4,6},{6,4},{8,10},{10,8},{12,14},{14,12},{16,18},{18,... | collective-permute-start | bytes 393224 | tf_op jit(solution)/shard_map/ppermute | solution.py:289
  16.4 5.4 %collective-permute-start.6 = (bf16[4,8,1024]{2,1,0:T(8,128)(2,1)S(1)}, bf16[4,8,1024]{2,1,0:T(8,128)(2,1)}, u32[]{:S(2)}, u32[]{:S(2)}) collective-permute-start(bf16[4,8,1024]{2,1,0:T(8,128)(2,1)S(1)} %collective-permute-done.5.refs_7_), channel_id=1, source_target_pairs={{0,2},{2,0},{4,6},{6,4},{8,10},{10,8},{12,14},{14,12},{16,18},{18,... | collective-permute-start | bytes 196616 | tf_op jit(solution)/shard_map/ppermute | solution.py:289
  17.4 4.5 %collective-permute-start.8 = (bf16[4,8,1024]{2,1,0:T(8,128)(2,1)S(1)}, bf16[4,8,1024]{2,1,0:T(8,128)(2,1)}, u32[]{:S(2)}, u32[]{:S(2)}) collective-permute-start(bf16[4,8,1024]{2,1,0:T(8,128)(2,1)S(1)} %collective-permute-done.7.refs_9_), channel_id=1, source_target_pairs={{0,2},{2,0},{4,6},{6,4},{8,10},{10,8},{12,14},{14,12},{16,18},{18,... | collective-permute-start | bytes 196616 | tf_op jit(solution)/shard_map/ppermute | solution.py:289
  18.6 3.3 %collective-permute-start.10 = (bf16[4,8,1024]{2,1,0:T(8,128)(2,1)S(1)}, bf16[4,8,1024]{2,1,0:T(8,128)(2,1)}, u32[]{:S(2)}, u32[]{:S(2)}) collective-permute-start(bf16[4,8,1024]{2,1,0:T(8,128)(2,1)S(1)} %collective-permute-done.9.refs_11_), channel_id=1, source_target_pairs={{0,2},{2,0},{4,6},{6,4},{8,10},{10,8},{12,14},{14,12},{16,18},{18,... | collective-permute-start | bytes 196616 | tf_op jit(solution)/shard_map/ppermute | solution.py:289
  21.3 1.6 %collective-permute-start.12 = (bf16[4,8,1024]{2,1,0:T(8,128)(2,1)}, bf16[4,8,1024]{2,1,0:T(8,128)(2,1)}, u32[]{:S(2)}, u32[]{:S(2)}) collective-permute-start(bf16[4,8,1024]{2,1,0:T(8,128)(2,1)} %collective-permute-done.11.refs_13_), channel_id=1, source_target_pairs={{0,2},{2,0},{4,6},{6,4},{8,10},{10,8},{12,14},{14,12},{16,18},{18,... | collective-permute-start | bytes 196616 | tf_op jit(solution)/shard_map/ppermute | solution.py:289
  24.3 4.0 %collective-permute-start.13 = (bf16[136,128]{1,0:T(8,128)(2,1)S(1)}, bf16[136,128]{1,0:T(8,128)(2,1)S(1)}, u32[]{:S(2)}, u32[]{:S(2)}) collective-permute-start(bf16[136,128]{1,0:T(8,128)(2,1)S(1)} %shard_map.50), channel_id=1, source_target_pairs={{0,1},{1,0},{2,3},{3,2},{4,5},{5,4},{6,7},{7,6},{8,9},{9,8},{10,11... | collective-permute-start | bytes 104456 | tf_op jit(solution)/shard_map/ppermute | solution.py:394

commit v5 on v4

--- a/solution.py
+++ b/solution.py
@@ -137,11 +137,14 @@
 def whiten_kernel(x_in, v_in, c_in, s_in, w_ref, c_out, s_out, x_ref, v_ref, t_ref, e_ref, sems):
     pairs = ((x_in, x_ref), (v_in, v_ref), (c_in, c_out), (s_in, s_out))
     copies = [pltpu.make_async_copy(a, b, sems.at[i]) for i, (a, b) in enumerate(pairs)]
-    for copy in copies:
+    segs, own, length = x_ref.shape
+    parts = [
+        pltpu.make_async_copy(x_in.at[i], x_ref.at[i], sems.at[len(pairs) + i]) for i in range(segs)
+    ]
+    for copy in parts + copies[1:]:
         copy.start()
-    segs, own, length = x_ref.shape
     make_quarter_table(t_ref, e_ref)
-    for copy in copies[:2]:
+    for copy in parts + copies[1:2]:
         copy.wait()
     quarter, half = length // 4, length // 2
     rows, group = segs * own, half // 4
@@ -229,8 +232,8 @@
     total = None
     for seg in range(r_ref.shape[0]):
         block, mate, pair_mate, pair, cross, cross_mate = blocks[:6]
-        first = [block[seg], mate[seg], pair_mate[1, seg], pair_mate[0, seg]]
-        first += [pair[0, seg], pair[1, seg], cross[seg], cross_mate[seg]]
+        first = [block[seg], mate[seg], pair[0, seg], pair[1, seg]]
+        first += [pair_mate[1, seg], pair_mate[0, seg], cross[seg], cross_mate[seg]]
         first += [b[seg] for b in blocks[6:]]
         term = lax.dot_general(
             r_ref[seg, start : start + rows],
@@ -302,8 +305,8 @@
         block = blocks[m]
         if m:
             parts = []
-            for distance in (NEAR | SIDE, NEAR, SIDE):
-                parts.append(hop(block, col, distance))
+            for name, distance in (("cross", m | NEAR | SIDE), ("near", NEAR), ("side", SIDE)):
+                parts.append(hop(own_block if name == "cross" else block, col, distance))
             cross, near, side = parts
             out += [block, swap(block), side, swap(side)]
             out += [near, swap(near), cross, swap(cross)]
@@ -317,7 +320,7 @@
             out_specs=VMEM,
             compiler_params=grant(2),
         )(block, mate)
-        pair = hop(pair, col, NEAR, SIDE)
+        pair = hop(pair, col, SIDE, NEAR)
         out += [block, mate, swap(pair), pair, cross, swap(cross)]
     return out
 
@@ -351,7 +354,7 @@
             pltpu.VMEM(valid.shape, valid.dtype),
             pltpu.VMEM((length // 4, length), jnp.bfloat16),
             pltpu.VMEM((2, length // 64, half), jnp.float32),
-            pltpu.SemaphoreType.DMA((4,)),
+            pltpu.SemaphoreType.DMA((4 + segs,)),
         ],
         compiler_params=grant(4),
     )(

time: 29.3 us -> 28.1 us (0.959)
  waiting for transfers between devices: 10.5 us -> 7.71 us
  starting transfers between devices: 13.1 us -> 14.7 us
    ppermute x13, waiting for transfers between devices: 9.51 us -> 6.7 us  [hop(): lax.ppermute(array, 'col', [(i, i ^ (other if i & 1 else distance)) for i...]
    ppermute x13, starting transfers between devices: 11.5 us -> 13.1 us  [hop(): lax.ppermute(array, 'col', [(i, i ^ (other if i & 1 else distance)) for i...]
where the time goes in v5:
time: 28.1 us; the launch traced here: 27.8 us
  starting transfers between devices  14.7 us (52%)
  waiting for transfers between devices  7.71 us (27%)
  Pallas kernels  5.37 us (19%)
    ppermute x13, starting transfers between devices, hop(): lax.ppermute(array, 'col', [(i, i ^ (other if i & 1 else distance)) for i...  13.1 us
    ppermute x13, waiting for transfers between devices, hop(): lax.ppermute(array, 'col', [(i, i ^ (other if i & 1 else distance)) for i...  6.7 us
    pallas_call x2, Pallas kernels, multiply(): pl.pallas_call(kernel, out_shape=jax.ShapeDtypeStruct((rows, lanes), dtyp...  2.88 us
    ppermute x1, starting transfers between devices, fast_body(): got = lax.ppermute(send, 'seg', [(0, 1), (1, 0)])  1.55 us
    pallas_call x1, Pallas kernels, fast_body(): pl.pallas_call(whiten_kernel, out_shape=[jax.ShapeDtypeStruct(traces.shap...  1.21 us
    ppermute x1, waiting for transfers between devices, fast_body(): got = lax.ppermute(send, 'seg', [(0, 1), (1, 0)])  1 us
    pallas_call x1, Pallas kernels, fast_body(): pl.pallas_call(functools.partial(finish_kernel, scale, own), out_shape=ja...  0.73 us
  transfers between devices with their start and end apart: 14, of which 8 were waited for; matrix products, arithmetic and copies ran while one was open for 0% of the time, Pallas kernels for 7%

profile of v5, /device:TPU:0, one launch (start us, length us, event | category | flops | bytes accessed | tf_op | source)
XLA Modules:
  0.0 27.8 jit_solution(16896972393328590418)
XLA Ops:
  0.0 1.2 %shard_map.46 = (bf16[4,8,1024]{2,1,0:T(8,128)(2,1)S(1)}, f32[136,512]{1,0:T(8,128)S(1)}, f32[136,512]{1,0:T(8,128)S(1)}) custom-call(bf16[4,8,1024]{2,1,0:T(8,128)(2,1)} %x_in.1, s32[4,8]{1,0:T(4,128)} %v_in.1, f32[136,512]{1,0:T(8,128)} %constant.12.clone.c_in, f32[136,512]{1,0:T(8,128)} %constant.13.clone.s_in), custom_call_target="tpu_custom_call" | custom-call | tf_op jit(solution)/shard_map/pallas_call | solution.py:343
  1.2 0.6 %collective-permute-start = (bf16[4,8,1024]{2,1,0:T(8,128)(2,1)S(1)}, bf16[4,8,1024]{2,1,0:T(8,128)(2,1)S(1)}, u32[]{:S(2)}, u32[]{:S(2)}) collective-permute-start(bf16[4,8,1024]{2,1,0:T(8,128)(2,1)S(1)} %get-tuple-element.8.w_ref.a_ref.refs_1_), channel_id=1, source_target_pairs={{0,2},{2,0},{4,6},{6,4},{8,10},{10,8},{12,14},{14,12},{16,18},{18,... | collective-permute-start | bytes 196616 | tf_op jit(solution)/shard_map/ppermute | solution.py:292
  1.8 0.9 %collective-permute-done.b_ref.refs_2_ = bf16[4,8,1024]{2,1,0:T(8,128)(2,1)S(1)} collective-permute-done((bf16[4,8,1024]{2,1,0:T(8,128)(2,1)S(1)}, bf16[4,8,1024]{2,1,0:T(8,128)(2,1)S(1)}, u32[]{:S(2)}, u32[]{:S(2)}) %collective-permute-start) | collective-permute-done | bytes 65568 | tf_op jit(solution)/shard_map/ppermute | solution.py:292
  2.7 2.9 %collective-permute-start.1 = (bf16[2,4,8,1024]{3,2,1,0:T(8,128)(2,1)S(1)}, bf16[2,4,8,1024]{3,2,1,0:T(8,128)(2,1)S(1)}, u32[]{:S(2)}, u32[]{:S(2)}) collective-permute-start(bf16[2,4,8,1024]{3,2,1,0:T(8,128)(2,1)S(1)} %shard_map.48), channel_id=1, source_target_pairs={{0,4},{2,10},{4,0},{6,14},{8,12},{10,2},{12,8},{14,6},{16,20},{18,... | collective-permute-start | bytes 393224 | tf_op jit(solution)/shard_map/ppermute | solution.py:292
  5.6 1.5 %collective-permute-start.3 = (bf16[4,8,1024]{2,1,0:T(8,128)(2,1)S(1)}, bf16[4,8,1024]{2,1,0:T(8,128)(2,1)S(1)}, u32[]{:S(2)}, u32[]{:S(2)}) collective-permute-start(bf16[4,8,1024]{2,1,0:T(8,128)(2,1)S(1)} %get-tuple-element.8.w_ref.a_ref.refs_1_), channel_id=1, source_target_pairs={{0,12},{2,14},{4,8},{6,10},{8,4},{10,6},{12,0},{14,2},{16,28},{18,... | collective-permute-start | bytes 196616 | tf_op jit(solution)/shard_map/ppermute | solution.py:292
  7.1 2.6 %collective-permute-start.5 = (bf16[4,8,1024]{2,1,0:T(8,128)(2,1)S(1)}, bf16[4,8,1024]{2,1,0:T(8,128)(2,1)S(1)}, u32[]{:S(2)}, u32[]{:S(2)}) collective-permute-start(bf16[4,8,1024]{2,1,0:T(8,128)(2,1)S(1)} %get-tuple-element.8.w_ref.a_ref.refs_1_), channel_id=1, source_target_pairs={{0,16},{2,18},{4,20},{6,22},{8,24},{10,26},{12,28},{14,30},{16,0},... | collective-permute-start | bytes 196616 | tf_op jit(solution)/shard_map/ppermute | solution.py:292
  9.7 1.2 %collective-permute-start.11 = (bf16[4,8,1024]{2,1,0:T(8,128)(2,1)S(1)}, bf16[4,8,1024]{2,1,0:T(8,128)(2,1)S(1)}, u32[]{:S(2)}, u32[]{:S(2)}) collective-permute-start(bf16[4,8,1024]{2,1,0:T(8,128)(2,1)S(1)} %get-tuple-element.8.w_ref.a_ref.refs_1_), channel_id=1, source_target_pairs={{0,28},{2,30},{4,24},{6,26},{8,20},{10,22},{12,16},{14,18},{16,12}... | collective-permute-start | bytes 196616 | tf_op jit(solution)/shard_map/ppermute | solution.py:292
  10.9 0.6 %collective-permute-done.3.refs_5_ = bf16[4,8,1024]{2,1,0:T(8,128)(2,1)S(1)} collective-permute-done((bf16[4,8,1024]{2,1,0:T(8,128)(2,1)S(1)}, bf16[4,8,1024]{2,1,0:T(8,128)(2,1)S(1)}, u32[]{:S(2)}, u32[]{:S(2)}) %collective-permute-start.3) | collective-permute-done | bytes 65568 | tf_op jit(solution)/shard_map/ppermute | solution.py:292
  11.5 0.0 collective-permute-start.4
  11.5 0.8 %collective-permute-done.5.refs_7_ = bf16[4,8,1024]{2,1,0:T(8,128)(2,1)S(1)} collective-permute-done((bf16[4,8,1024]{2,1,0:T(8,128)(2,1)S(1)}, bf16[4,8,1024]{2,1,0:T(8,128)(2,1)S(1)}, u32[]{:S(2)}, u32[]{:S(2)}) %collective-permute-start.5) | collective-permute-done | bytes 65568 | tf_op jit(solution)/shard_map/ppermute | solution.py:292
  12.3 3.4 %collective-permute-start.7 = (bf16[4,8,1024]{2,1,0:T(8,128)(2,1)S(1)}, bf16[4,8,1024]{2,1,0:T(8,128)(2,1)S(1)}, u32[]{:S(2)}, u32[]{:S(2)}) collective-permute-start(bf16[4,8,1024]{2,1,0:T(8,128)(2,1)S(1)} %collective-permute-done.5.refs_7_), channel_id=1, source_target_pairs={{0,4},{2,6},{4,0},{6,2},{8,12},{10,14},{12,8},{14,10},{16,20},{18,... | collective-permute-start | bytes 196616 | tf_op jit(solution)/shard_map/ppermute | solution.py:292
  15.7 0.5 %collective-permute-start.9 = (bf16[4,8,1024]{2,1,0:T(8,128)(2,1)S(1)}, bf16[4,8,1024]{2,1,0:T(8,128)(2,1)}, u32[]{:S(2)}, u32[]{:S(2)}) collective-permute-start(bf16[4,8,1024]{2,1,0:T(8,128)(2,1)S(1)} %collective-permute-done.5.refs_7_), channel_id=1, source_target_pairs={{0,8},{2,10},{4,12},{6,14},{8,0},{10,2},{12,4},{14,6},{16,24},{18,... | collective-permute-start | bytes 196616 | tf_op jit(solution)/shard_map/ppermute | solution.py:292
  16.1 0.0 collective-permute-done.1.refs_4_
  16.1 0.0 collective-permute-start.2
  16.1 0.6 %collective-permute-done.11.refs_13_ = bf16[4,8,1024]{2,1,0:T(8,128)(2,1)S(1)} collective-permute-done((bf16[4,8,1024]{2,1,0:T(8,128)(2,1)S(1)}, bf16[4,8,1024]{2,1,0:T(8,128)(2,1)S(1)}, u32[]{:S(2)}, u32[]{:S(2)}) %collective-permute-start.11) | collective-permute-done | bytes 65568 | tf_op jit(solution)/shard_map/ppermute | solution.py:292
  16.8 0.0 collective-permute-start.6
  16.8 0.0 collective-permute-done.4.refs_6_
  16.8 0.5 %collective-permute-start.12 = (bf16[4,8,1024]{2,1,0:T(8,128)(2,1)S(1)}, bf16[4,8,1024]{2,1,0:T(8,128)(2,1)}, u32[]{:S(2)}, u32[]{:S(2)}) collective-permute-start(bf16[4,8,1024]{2,1,0:T(8,128)(2,1)S(1)} %collective-permute-done.11.refs_13_), channel_id=1, source_target_pairs={{0,2},{2,0},{4,6},{6,4},{8,10},{10,8},{12,14},{14,12},{16,18},{18,... | collective-permute-start | bytes 196616 | tf_op jit(solution)/shard_map/ppermute | solution.py:292
  17.3 0.6 %collective-permute-done.7.refs_9_ = bf16[4,8,1024]{2,1,0:T(8,128)(2,1)S(1)} collective-permute-done((bf16[4,8,1024]{2,1,0:T(8,128)(2,1)S(1)}, bf16[4,8,1024]{2,1,0:T(8,128)(2,1)S(1)}, u32[]{:S(2)}, u32[]{:S(2)}) %collective-permute-start.7) | collective-permute-done | bytes 65568 | tf_op jit(solution)/shard_map/ppermute | solution.py:292
  17.9 0.0 collective-permute-start.8
  17.9 2.1 %collective-permute-done.9.refs_11_ = bf16[4,8,1024]{2,1,0:T(8,128)(2,1)} collective-permute-done((bf16[4,8,1024]{2,1,0:T(8,128)(2,1)S(1)}, bf16[4,8,1024]{2,1,0:T(8,128)(2,1)}, u32[]{:S(2)}, u32[]{:S(2)}) %collective-permute-start.9) | collective-permute-done | bytes 65568 | tf_op jit(solution)/shard_map/ppermute | solution.py:292
  20.0 0.0 collective-permute-start.10
  20.0 0.5 %shard_map.47.refs_0_ = bf16[4,272,1024]{2,1,0:T(8,128)(2,1)S(1)} custom-call(s32[1]{0:T(128)} %bitcast.1.seg_ref, bf16[4,8,1024]{2,1,0:T(8,128)(2,1)S(1)} %get-tuple-element.8.w_ref.a_ref.refs_1_, f32[136,512]{1,0:T(8,128)S(1)} %get-tuple-element.9.c_ref, f32[136,512]{1,0:T(8,128)S(1)} %get-tuple-element.10.s_ref), custom_call_target="tpu_custom_call" | custom-call | flops 6684672 | bytes 2228224 | tf_op jit(solution)/shard_map/pallas_call | solution.py:369
  20.6 0.0 collective-permute-done.6.refs_8_
  20.6 0.0 collective-permute-done.12.refs_14_
  20.6 0.0 collective-permute-done.8.refs_10_
  20.6 1.0 %collective-permute-done.10.refs_12_ = bf16[4,8,1024]{2,1,0:T(8,128)(2,1)} collective-permute-done((bf16[4,8,1024]{2,1,0:T(8,128)(2,1)}, bf16[4,8,1024]{2,1,0:T(8,128)(2,1)}, u32[]{:S(2)}, u32[]{:S(2)}) %collective-permute-start.10) | collective-permute-done | bytes 65568 | tf_op jit(solution)/shard_map/ppermute | solution.py:292
  21.6 0.0 collective-permute-done.2.refs_3_
  21.6 1.4 %shard_map.50 = bf16[136,128]{1,0:T(8,128)(2,1)S(1)} custom-call(bf16[4,272,1024]{2,1,0:T(8,128)(2,1)S(1)} %shard_map.47.refs_0_, bf16[4,8,1024]{2,1,0:T(8,128)(2,1)S(1)} %get-tuple-element.8.w_ref.a_ref.refs_1_, bf16[4,8,1024]{2,1,0:T(8,128)(2,1)S(1)} %collective-permute-done.b_ref.refs_2_, bf16[2,4,8,1024]{3,2,1,0:T(8,128)(2,1)S(1)} %collective-permute-done.2.refs_3_, ...), custom_call_target="tpu_custom_call" | custom-call | flops 142606336 | bytes 2162688 | tf_op jit(solution)/shard_map/pallas_call | solution.py:383
  23.1 1.5 %collective-permute-start.13 = (bf16[136,128]{1,0:T(8,128)(2,1)S(1)}, bf16[136,128]{1,0:T(8,128)(2,1)S(1)}, u32[]{:S(2)}, u32[]{:S(2)}) collective-permute-start(bf16[136,128]{1,0:T(8,128)(2,1)S(1)} %shard_map.50), channel_id=1, source_target_pairs={{0,1},{1,0},{2,3},{3,2},{4,5},{5,4},{6,7},{7,6},{8,9},{9,8},{10,11... | collective-permute-start | bytes 104456 | tf_op jit(solution)/shard_map/ppermute | solution.py:397
  24.6 1.4 %shard_map.49.keep_ref = f32[136,128]{1,0:T(8,128)S(1)} custom-call(bf16[4,272,1024]{2,1,0:T(8,128)(2,1)S(1)} %shard_map.47.refs_0_, bf16[4,8,1024]{2,1,0:T(8,128)(2,1)S(1)} %get-tuple-element.8.w_ref.a_ref.refs_1_, bf16[4,8,1024]{2,1,0:T(8,128)(2,1)S(1)} %collective-permute-done.b_ref.refs_2_, bf16[2,4,8,1024]{3,2,1,0:T(8,128)(2,1)S(1)} %collective-permute-done.2.refs_3_, ...), custom_call_target="tpu_custom_call" | custom-call | flops 142606336 | bytes 2162688 | tf_op jit(solution)/shard_map/pallas_call | solution.py:383
  26.1 1.0 %collective-permute-done.13.got_ref = bf16[136,128]{1,0:T(8,128)(2,1)S(1)} collective-permute-done((bf16[136,128]{1,0:T(8,128)(2,1)S(1)}, bf16[136,128]{1,0:T(8,128)(2,1)S(1)}, u32[]{:S(2)}, u32[]{:S(2)}) %collective-permute-start.13) | collective-permute-done | bytes 34848 | tf_op jit(solution)/shard_map/ppermute | solution.py:397
  27.1 0.7 %shard_map.51 = f32[33,4,128]{2,1,0:T(4,128)} custom-call(s32[1]{0:T(128)} %bitcast.me_ref, f32[136,128]{1,0:T(8,128)S(1)} %shard_map.49.keep_ref, bf16[136,128]{1,0:T(8,128)(2,1)S(1)} %collective-permute-done.13.got_ref), custom_call_target="tpu_custom_call" | custom-call | tf_op jit(solution)/shard_map/pallas_call | solution.py:399
  (1 shorter events, 0.0 us)
Async XLA Ops:
  1.2 1.5 %collective-permute-start = (bf16[4,8,1024]{2,1,0:T(8,128)(2,1)S(1)}, bf16[4,8,1024]{2,1,0:T(8,128)(2,1)S(1)}, u32[]{:S(2)}, u32[]{:S(2)}) collective-permute-start(bf16[4,8,1024]{2,1,0:T(8,128)(2,1)S(1)} %get-tuple-element.8.w_ref.a_ref.refs_1_), channel_id=1, source_target_pairs={{0,2},{2,0},{4,6},{6,4},{8,10},{10,8},{12,14},{14,12},{16,18},{18,... | collective-permute-start | bytes 196616 | tf_op jit(solution)/shard_map/ppermute | solution.py:292
  2.7 13.4 %collective-permute-start.1 = (bf16[2,4,8,1024]{3,2,1,0:T(8,128)(2,1)S(1)}, bf16[2,4,8,1024]{3,2,1,0:T(8,128)(2,1)S(1)}, u32[]{:S(2)}, u32[]{:S(2)}) collective-permute-start(bf16[2,4,8,1024]{3,2,1,0:T(8,128)(2,1)S(1)} %shard_map.48), channel_id=1, source_target_pairs={{0,4},{2,10},{4,0},{6,14},{8,12},{10,2},{12,8},{14,6},{16,20},{18,... | collective-permute-start | bytes 393224 | tf_op jit(solution)/shard_map/ppermute | solution.py:292
  5.6 5.8 %collective-permute-start.3 = (bf16[4,8,1024]{2,1,0:T(8,128)(2,1)S(1)}, bf16[4,8,1024]{2,1,0:T(8,128)(2,1)S(1)}, u32[]{:S(2)}, u32[]{:S(2)}) collective-permute-start(bf16[4,8,1024]{2,1,0:T(8,128)(2,1)S(1)} %get-tuple-element.8.w_ref.a_ref.refs_1_), channel_id=1, source_target_pairs={{0,12},{2,14},{4,8},{6,10},{8,4},{10,6},{12,0},{14,2},{16,28},{18,... | collective-permute-start | bytes 196616 | tf_op jit(solution)/shard_map/ppermute | solution.py:292
  7.1 5.2 %collective-permute-start.5 = (bf16[4,8,1024]{2,1,0:T(8,128)(2,1)S(1)}, bf16[4,8,1024]{2,1,0:T(8,128)(2,1)S(1)}, u32[]{:S(2)}, u32[]{:S(2)}) collective-permute-start(bf16[4,8,1024]{2,1,0:T(8,128)(2,1)S(1)} %get-tuple-element.8.w_ref.a_ref.refs_1_), channel_id=1, source_target_pairs={{0,16},{2,18},{4,20},{6,22},{8,24},{10,26},{12,28},{14,30},{16,0},... | collective-permute-start | bytes 196616 | tf_op jit(solution)/shard_map/ppermute | solution.py:292
  9.7 7.1 %collective-permute-start.11 = (bf16[4,8,1024]{2,1,0:T(8,128)(2,1)S(1)}, bf16[4,8,1024]{2,1,0:T(8,128)(2,1)S(1)}, u32[]{:S(2)}, u32[]{:S(2)}) collective-permute-start(bf16[4,8,1024]{2,1,0:T(8,128)(2,1)S(1)} %get-tuple-element.8.w_ref.a_ref.refs_1_), channel_id=1, source_target_pairs={{0,28},{2,30},{4,24},{6,26},{8,20},{10,22},{12,16},{14,18},{16,12}... | collective-permute-start | bytes 196616 | tf_op jit(solution)/shard_map/ppermute | solution.py:292
  11.5 5.3 %collective-permute-start.4 = (bf16[4,8,1024]{2,1,0:T(8,128)(2,1)S(1)}, bf16[4,8,1024]{2,1,0:T(8,128)(2,1)S(1)}, u32[]{:S(2)}, u32[]{:S(2)}) collective-permute-start(bf16[4,8,1024]{2,1,0:T(8,128)(2,1)S(1)} %collective-permute-done.3.refs_5_), channel_id=1, source_target_pairs={{0,2},{2,0},{4,6},{6,4},{8,10},{10,8},{12,14},{14,12},{16,18},{18,... | collective-permute-start | bytes 196616 | tf_op jit(solution)/shard_map/ppermute | solution.py:292
  12.3 5.6 %collective-permute-start.7 = (bf16[4,8,1024]{2,1,0:T(8,128)(2,1)S(1)}, bf16[4,8,1024]{2,1,0:T(8,128)(2,1)S(1)}, u32[]{:S(2)}, u32[]{:S(2)}) collective-permute-start(bf16[4,8,1024]{2,1,0:T(8,128)(2,1)S(1)} %collective-permute-done.5.refs_7_), channel_id=1, source_target_pairs={{0,4},{2,6},{4,0},{6,2},{8,12},{10,14},{12,8},{14,10},{16,20},{18,... | collective-permute-start | bytes 196616 | tf_op jit(solution)/shard_map/ppermute | solution.py:292
  15.7 4.4 %collective-permute-start.9 = (bf16[4,8,1024]{2,1,0:T(8,128)(2,1)S(1)}, bf16[4,8,1024]{2,1,0:T(8,128)(2,1)}, u32[]{:S(2)}, u32[]{:S(2)}) collective-permute-start(bf16[4,8,1024]{2,1,0:T(8,128)(2,1)S(1)} %collective-permute-done.5.refs_7_), channel_id=1, source_target_pairs={{0,8},{2,10},{4,12},{6,14},{8,0},{10,2},{12,4},{14,6},{16,24},{18,... | collective-permute-start | bytes 196616 | tf_op jit(solution)/shard_map/ppermute | solution.py:292
  16.1 5.5 %collective-permute-start.2 = (bf16[2,4,8,1024]{3,2,1,0:T(8,128)(2,1)S(1)}, bf16[2,4,8,1024]{3,2,1,0:T(8,128)(2,1)S(1)}, u32[]{:S(2)}, u32[]{:S(2)}) collective-permute-start(bf16[2,4,8,1024]{3,2,1,0:T(8,128)(2,1)S(1)} %collective-permute-done.1.refs_4_), channel_id=1, source_target_pairs={{0,2},{2,0},{4,6},{6,4},{8,10},{10,8},{12,14},{14,12},{16,18},{18,... | collective-permute-start | bytes 393224 | tf_op jit(solution)/shard_map/ppermute | solution.py:292
  16.8 3.8 %collective-permute-start.6 = (bf16[4,8,1024]{2,1,0:T(8,128)(2,1)S(1)}, bf16[4,8,1024]{2,1,0:T(8,128)(2,1)}, u32[]{:S(2)}, u32[]{:S(2)}) collective-permute-start(bf16[4,8,1024]{2,1,0:T(8,128)(2,1)S(1)} %collective-permute-done.5.refs_7_), channel_id=1, source_target_pairs={{0,2},{2,0},{4,6},{6,4},{8,10},{10,8},{12,14},{14,12},{16,18},{18,... | collective-permute-start | bytes 196616 | tf_op jit(solution)/shard_map/ppermute | solution.py:292
  16.8 3.8 %collective-permute-start.12 = (bf16[4,8,1024]{2,1,0:T(8,128)(2,1)S(1)}, bf16[4,8,1024]{2,1,0:T(8,128)(2,1)}, u32[]{:S(2)}, u32[]{:S(2)}) collective-permute-start(bf16[4,8,1024]{2,1,0:T(8,128)(2,1)S(1)} %collective-permute-done.11.refs_13_), channel_id=1, source_target_pairs={{0,2},{2,0},{4,6},{6,4},{8,10},{10,8},{12,14},{14,12},{16,18},{18,... | collective-permute-start | bytes 196616 | tf_op jit(solution)/shard_map/ppermute | solution.py:292
  17.9 2.7 %collective-permute-start.8 = (bf16[4,8,1024]{2,1,0:T(8,128)(2,1)S(1)}, bf16[4,8,1024]{2,1,0:T(8,128)(2,1)}, u32[]{:S(2)}, u32[]{:S(2)}) collective-permute-start(bf16[4,8,1024]{2,1,0:T(8,128)(2,1)S(1)} %collective-permute-done.7.refs_9_), channel_id=1, source_target_pairs={{0,2},{2,0},{4,6},{6,4},{8,10},{10,8},{12,14},{14,12},{16,18},{18,... | collective-permute-start | bytes 196616 | tf_op jit(solution)/shard_map/ppermute | solution.py:292
  20.0 1.6 %collective-permute-start.10 = (bf16[4,8,1024]{2,1,0:T(8,128)(2,1)}, bf16[4,8,1024]{2,1,0:T(8,128)(2,1)}, u32[]{:S(2)}, u32[]{:S(2)}) collective-permute-start(bf16[4,8,1024]{2,1,0:T(8,128)(2,1)} %collective-permute-done.9.refs_11_), channel_id=1, source_target_pairs={{0,2},{2,0},{4,6},{6,4},{8,10},{10,8},{12,14},{14,12},{16,18},{18,... | collective-permute-start | bytes 196616 | tf_op jit(solution)/shard_map/ppermute | solution.py:292
  23.1 4.0 %collective-permute-start.13 = (bf16[136,128]{1,0:T(8,128)(2,1)S(1)}, bf16[136,128]{1,0:T(8,128)(2,1)S(1)}, u32[]{:S(2)}, u32[]{:S(2)}) collective-permute-start(bf16[136,128]{1,0:T(8,128)(2,1)S(1)} %shard_map.50), channel_id=1, source_target_pairs={{0,1},{1,0},{2,3},{3,2},{4,5},{5,4},{6,7},{7,6},{8,9},{9,8},{10,11... | collective-permute-start | bytes 104456 | tf_op jit(solution)/shard_map/ppermute | solution.py:397

commit v6 on v4

--- a/solution.py
+++ b/solution.py
@@ -228,13 +228,9 @@
 def products(r_ref, blocks, start, rows):
     total = None
     for seg in range(r_ref.shape[0]):
-        block, mate, pair_mate, pair, cross, cross_mate = blocks[:6]
-        first = [block[seg], mate[seg], pair_mate[1, seg], pair_mate[0, seg]]
-        first += [pair[0, seg], pair[1, seg], cross[seg], cross_mate[seg]]
-        first += [b[seg] for b in blocks[6:]]
         term = lax.dot_general(
             r_ref[seg, start : start + rows],
-            jnp.concatenate(first, axis=0),
+            jnp.concatenate([block[seg] for block in blocks], axis=0),
             (((1,), (1,)), ((), ())),
             preferred_element_type=jnp.float32,
         )
@@ -253,20 +249,12 @@
     keep_ref[...] = products(r_ref, blocks, 0, keep_ref.shape[0])
 
 
-def pair_kernel(a_ref, b_ref, out_ref):
-    out_ref[0] = a_ref[...]
-    out_ref[1] = b_ref[...]
-
-
 def finish_kernel(scale, own, me_ref, keep_ref, got_ref, out_ref):
     lags, part, _ = out_ref.shape
     value = (keep_ref[...] + got_ref[...].astype(jnp.float32)) * scale
     lane = lax.broadcasted_iota(jnp.int32, value.shape, 1)
-    me = me_ref[0]
-    block = (lane // own) ^ me
-    crossed = (block & ~6) | ((block & 2) << 1) | ((block & 4) >> 1)
-    block = jnp.where(((me & 1) != 0) & (block < 8), crossed, block)
-    value = jnp.take_along_axis(value, block * own + lane % own, axis=1)
+    index = ((lane // own) ^ me_ref[0]) * own + lane % own
+    value = jnp.take_along_axis(value, index, axis=1)
     for lag in range(lags):
         out_ref[lag] = value[lag * part : (lag + 1) * part]
 
@@ -274,52 +262,29 @@
 CORE, SIDE, NEAR = 1, 2, 4
 
 
-def far_blocks(col):
-    held, steps = [0], []
+def gather_plan(col):
+    cross = NEAR | SIDE
+    held, plan = [0], []
     bit = col // 2
     while bit > NEAR:
-        steps += [(m | bit, m, bit) for m in held]
+        plan += [(m | bit, m, bit) for m in held]
         held += [m | bit for m in held]
         bit //= 2
-    return held, steps
-
-
-def hop(array, col, distance, other=None):
-    other = distance if other is None else other
-    return lax.ppermute(array, "col", [(i, i ^ (other if i & 1 else distance)) for i in range(col)])
+    far = held[1:]
+    plan += [(m | cross, 0, m | cross) for m in held]
+    for m in held:
+        plan += [(m | SIDE, m, SIDE), (m | NEAR, m, NEAR)]
+    mates = [cross, 0, SIDE] + far + [NEAR]
+    for m in far:
+        mates += [m | cross, m | SIDE, m | NEAR]
+    return plan + [(m | CORE, m, CORE) for m in mates]
 
 
 def gather(own_block, col):
-    def swap(array):
-        return hop(array, col, CORE)
-
     blocks = {0: own_block}
-    held, steps = far_blocks(col)
-    for block, source, distance in steps:
-        blocks[block] = hop(blocks[source], col, distance)
-    out = []
-    for m in held:
-        block = blocks[m]
-        if m:
-            parts = []
-            for distance in (NEAR | SIDE, NEAR, SIDE):
-                parts.append(hop(block, col, distance))
-            cross, near, side = parts
-            out += [block, swap(block), side, swap(side)]
-            out += [near, swap(near), cross, swap(cross)]
-            continue
-        mate = swap(block)
-        cross = hop(block, col, NEAR | SIDE)
-        pair = pl.pallas_call(
-            pair_kernel,
-            out_shape=jax.ShapeDtypeStruct((2, *block.shape), block.dtype),
-            in_specs=[VMEM] * 2,
-            out_specs=VMEM,
-            compiler_params=grant(2),
-        )(block, mate)
-        pair = hop(pair, col, NEAR, SIDE)
-        out += [block, mate, swap(pair), pair, cross, swap(cross)]
-    return out
+    for block, source, distance in gather_plan(col):
+        blocks[block] = lax.ppermute(blocks[source], "col", [(i, i ^ distance) for i in range(col)])
+    return [blocks[m] for m in range(col)]
 
 
 def fast_device(traces, valid):
@@ -388,7 +353,7 @@
                 bytes_accessed=2 * (rows + lanes) * segs * length,
                 transcendentals=0,
             ),
-        )(rotated, *blocks)
+        )(pltpu.with_memory_space_constraint(rotated, pltpu.VMEM), *blocks)
 
     send = multiply(send_kernel, jnp.bfloat16)
     got = lax.ppermute(send, "seg", [(0, 1), (1, 0)])

time: 29.3 us -> 26.6 us (0.908)
  waiting for transfers between devices: 10.5 us -> 6.78 us
  starting transfers between devices: 13.1 us -> 14.1 us
    ppermute x13 -> x15, waiting for transfers between devices: 9.51 us -> 5.77 us  [gather(): lax.ppermute(blocks[source], 'col', [(i, i ^ distance) for i in range(col)])]
    ppermute x13 -> x15, starting transfers between devices: 11.5 us -> 12.6 us  [gather(): lax.ppermute(blocks[source], 'col', [(i, i ^ distance) for i in range(col)])]
  transfers between devices with their start and end apart: 14 -> 16, of which waited for: 8 -> 8; matrix products, arithmetic and copies ran while one was open for 0% -> 0% of each run, Pallas kernels for 7% -> 7%
where the time goes in v6:
time: 26.6 us; the launch traced here: 26.3 us
  starting transfers between devices  14.1 us (53%)
  waiting for transfers between devices  6.78 us (25%)
  Pallas kernels  5.38 us (20%)
    ppermute x15, starting transfers between devices, gather(): lax.ppermute(blocks[source], 'col', [(i, i ^ distance) for i in range(col)])  12.6 us
    ppermute x15, waiting for transfers between devices, gather(): lax.ppermute(blocks[source], 'col', [(i, i ^ distance) for i in range(col)])  5.77 us
    pallas_call x2, Pallas kernels, multiply(): pl.pallas_call(kernel, out_shape=jax.ShapeDtypeStruct((rows, lanes), dtyp...  2.88 us
    ppermute x1, starting transfers between devices, fast_body(): got = lax.ppermute(send, 'seg', [(0, 1), (1, 0)])  1.55 us
    pallas_call x1, Pallas kernels, fast_body(): pl.pallas_call(whiten_kernel, out_shape=[jax.ShapeDtypeStruct(traces.shap...  1.25 us
    ppermute x1, waiting for transfers between devices, fast_body(): got = lax.ppermute(send, 'seg', [(0, 1), (1, 0)])  1 us
    pallas_call x1, Pallas kernels, fast_body(): pl.pallas_call(functools.partial(finish_kernel, scale, own), out_shape=ja...  0.73 us
    pallas_call x1, Pallas kernels, fast_body(): pl.pallas_call(rotate_kernel, out_shape=jax.ShapeDtypeStruct((segs, 2 * r...  0.53 us
  transfers between devices with their start and end apart: 16, of which 8 were waited for; matrix products, arithmetic and copies ran while one was open for 0% of the time, Pallas kernels for 7%

profile of v6, /device:TPU:0, one launch (start us, length us, event | category | flops | bytes accessed | tf_op | source)
XLA Modules:
  0.0 26.3 jit_solution(12083674707177485362)
XLA Ops:
  0.0 1.2 %shard_map.46 = (bf16[4,8,1024]{2,1,0:T(8,128)(2,1)S(1)}, f32[136,512]{1,0:T(8,128)S(1)}, f32[136,512]{1,0:T(8,128)S(1)}) custom-call(bf16[4,8,1024]{2,1,0:T(8,128)(2,1)} %x_in.1, s32[4,8]{1,0:T(4,128)} %v_in.1, f32[136,512]{1,0:T(8,128)} %constant.12.clone.c_in, f32[136,512]{1,0:T(8,128)} %constant.13.clone.s_in), custom_call_target="tpu_custom_call" | custom-call | tf_op jit(solution)/shard_map/pallas_call | solution.py:305
  1.3 4.1 %collective-permute-start.7 = (bf16[4,8,1024]{2,1,0:T(8,128)(2,1)S(1)}, bf16[4,8,1024]{2,1,0:T(8,128)(2,1)S(1)}, u32[]{:S(2)}, u32[]{:S(2)}) collective-permute-start(bf16[4,8,1024]{2,1,0:T(8,128)(2,1)S(1)} %get-tuple-element.8.w_ref.refs_1_), channel_id=1, source_target_pairs={{0,16},{2,18},{4,20},{6,22},{8,24},{10,26},{12,28},{14,30},{16,0},... | collective-permute-start | bytes 196616 | tf_op jit(solution)/shard_map/ppermute | solution.py:286
  5.4 2.3 %collective-permute-start.13 = (bf16[4,8,1024]{2,1,0:T(8,128)(2,1)S(1)}, bf16[4,8,1024]{2,1,0:T(8,128)(2,1)S(1)}, u32[]{:S(2)}, u32[]{:S(2)}) collective-permute-start(bf16[4,8,1024]{2,1,0:T(8,128)(2,1)S(1)} %get-tuple-element.8.w_ref.refs_1_), channel_id=1, source_target_pairs={{0,28},{2,30},{4,24},{6,26},{8,20},{10,22},{12,16},{14,18},{16,12}... | collective-permute-start | bytes 196616 | tf_op jit(solution)/shard_map/ppermute | solution.py:286
  7.7 0.5 %collective-permute-start.1 = (bf16[4,8,1024]{2,1,0:T(8,128)(2,1)S(1)}, bf16[4,8,1024]{2,1,0:T(8,128)(2,1)S(1)}, u32[]{:S(2)}, u32[]{:S(2)}) collective-permute-start(bf16[4,8,1024]{2,1,0:T(8,128)(2,1)S(1)} %get-tuple-element.8.w_ref.refs_1_), channel_id=1, source_target_pairs={{0,4},{2,6},{4,0},{6,2},{8,12},{10,14},{12,8},{14,10},{16,20},{18,... | collective-permute-start | bytes 196616 | tf_op jit(solution)/shard_map/ppermute | solution.py:286
  8.2 0.3 %collective-permute-start.3 = (bf16[4,8,1024]{2,1,0:T(8,128)(2,1)S(1)}, bf16[4,8,1024]{2,1,0:T(8,128)(2,1)S(1)}, u32[]{:S(2)}, u32[]{:S(2)}) collective-permute-start(bf16[4,8,1024]{2,1,0:T(8,128)(2,1)S(1)} %get-tuple-element.8.w_ref.refs_1_), channel_id=1, source_target_pairs={{0,8},{2,10},{4,12},{6,14},{8,0},{10,2},{12,4},{14,6},{16,24},{18,... | collective-permute-start | bytes 196616 | tf_op jit(solution)/shard_map/ppermute | solution.py:286
  8.5 2.7 %collective-permute-start.5 = (bf16[4,8,1024]{2,1,0:T(8,128)(2,1)S(1)}, bf16[4,8,1024]{2,1,0:T(8,128)(2,1)S(1)}, u32[]{:S(2)}, u32[]{:S(2)}) collective-permute-start(bf16[4,8,1024]{2,1,0:T(8,128)(2,1)S(1)} %get-tuple-element.8.w_ref.refs_1_), channel_id=1, source_target_pairs={{0,12},{2,14},{4,8},{6,10},{8,4},{10,6},{12,0},{14,2},{16,28},{18,... | collective-permute-start | bytes 196616 | tf_op jit(solution)/shard_map/ppermute | solution.py:286
  11.2 0.0 collective-permute-done.7.refs_9_
  11.2 0.0 collective-permute-start
  11.2 1.6 %collective-permute-done.13.refs_15_ = bf16[4,8,1024]{2,1,0:T(8,128)(2,1)S(1)} collective-permute-done((bf16[4,8,1024]{2,1,0:T(8,128)(2,1)S(1)}, bf16[4,8,1024]{2,1,0:T(8,128)(2,1)S(1)}, u32[]{:S(2)}, u32[]{:S(2)}) %collective-permute-start.13) | collective-permute-done | bytes 65568 | tf_op jit(solution)/shard_map/ppermute | solution.py:286
  12.8 1.2 %collective-permute-start.9 = (bf16[4,8,1024]{2,1,0:T(8,128)(2,1)S(1)}, bf16[4,8,1024]{2,1,0:T(8,128)(2,1)S(1)}, u32[]{:S(2)}, u32[]{:S(2)}) collective-permute-start(bf16[4,8,1024]{2,1,0:T(8,128)(2,1)S(1)} %collective-permute-done.7.refs_9_), channel_id=1, source_target_pairs={{0,4},{2,6},{4,0},{6,2},{8,12},{10,14},{12,8},{14,10},{16,20},{18,... | collective-permute-start | bytes 196616 | tf_op jit(solution)/shard_map/ppermute | solution.py:286
  14.0 0.0 collective-permute-done.1.refs_3_
  14.0 0.4 %collective-permute-start.11 = (bf16[4,8,1024]{2,1,0:T(8,128)(2,1)S(1)}, bf16[4,8,1024]{2,1,0:T(8,128)(2,1)S(1)}, u32[]{:S(2)}, u32[]{:S(2)}) collective-permute-start(bf16[4,8,1024]{2,1,0:T(8,128)(2,1)S(1)} %collective-permute-done.7.refs_9_), channel_id=1, source_target_pairs={{0,8},{2,10},{4,12},{6,14},{8,0},{10,2},{12,4},{14,6},{16,24},{18,... | collective-permute-start | bytes 196616 | tf_op jit(solution)/shard_map/ppermute | solution.py:286
  14.4 0.0 collective-permute-done.3.refs_5_
  14.4 0.0 collective-permute-start.8
  14.4 0.2 collective-permute-done.5.refs_7_
  14.6 0.3 %collective-permute-start.14 = (bf16[4,8,1024]{2,1,0:T(8,128)(2,1)S(1)}, bf16[4,8,1024]{2,1,0:T(8,128)(2,1)S(1)}, u32[]{:S(2)}, u32[]{:S(2)}) collective-permute-start(bf16[4,8,1024]{2,1,0:T(8,128)(2,1)S(1)} %collective-permute-done.13.refs_15_), channel_id=1, source_target_pairs={{0,2},{2,0},{4,6},{6,4},{8,10},{10,8},{12,14},{14,12},{16,18},{18,... | collective-permute-start | bytes 196616 | tf_op jit(solution)/shard_map/ppermute | solution.py:286
  14.9 0.0 collective-permute-done.refs_2_
  14.9 0.2 collective-permute-start.2
  15.1 2.0 %collective-permute-done.9.refs_11_ = bf16[4,8,1024]{2,1,0:T(8,128)(2,1)S(1)} collective-permute-done((bf16[4,8,1024]{2,1,0:T(8,128)(2,1)S(1)}, bf16[4,8,1024]{2,1,0:T(8,128)(2,1)S(1)}, u32[]{:S(2)}, u32[]{:S(2)}) %collective-permute-start.9) | collective-permute-done | bytes 65568 | tf_op jit(solution)/shard_map/ppermute | solution.py:286
  17.1 0.0 collective-permute-start.4
  17.1 1.2 %collective-permute-done.11.refs_13_ = bf16[4,8,1024]{2,1,0:T(8,128)(2,1)S(1)} collective-permute-done((bf16[4,8,1024]{2,1,0:T(8,128)(2,1)S(1)}, bf16[4,8,1024]{2,1,0:T(8,128)(2,1)S(1)}, u32[]{:S(2)}, u32[]{:S(2)}) %collective-permute-start.11) | collective-permute-done | bytes 65568 | tf_op jit(solution)/shard_map/ppermute | solution.py:286
  18.2 0.0 collective-permute-start.6
  18.2 0.0 collective-permute-done.8.refs_10_
  18.3 0.5 %collective-permute-start.10 = (bf16[4,8,1024]{2,1,0:T(8,128)(2,1)S(1)}, bf16[4,8,1024]{2,1,0:T(8,128)(2,1)}, u32[]{:S(2)}, u32[]{:S(2)}) collective-permute-start(bf16[4,8,1024]{2,1,0:T(8,128)(2,1)S(1)} %collective-permute-done.9.refs_11_), channel_id=1, source_target_pairs={{0,2},{2,0},{4,6},{6,4},{8,10},{10,8},{12,14},{14,12},{16,18},{18,... | collective-permute-start | bytes 196616 | tf_op jit(solution)/shard_map/ppermute | solution.py:286
  18.8 0.0 collective-permute-done.14.refs_16_
  18.8 0.1 collective-permute-start.12
  18.8 0.5 %shard_map.47.refs_0_ = bf16[4,272,1024]{2,1,0:T(8,128)(2,1)S(1)} custom-call(s32[1]{0:T(128)} %bitcast.1.seg_ref, bf16[4,8,1024]{2,1,0:T(8,128)(2,1)S(1)} %get-tuple-element.8.w_ref.refs_1_, f32[136,512]{1,0:T(8,128)S(1)} %get-tuple-element.9.c_ref, f32[136,512]{1,0:T(8,128)S(1)} %get-tuple-element.10.s_ref), custom_call_target="tpu_custom_call" | custom-call | flops 6684672 | bytes 2228224 | tf_op jit(solution)/shard_map/pallas_call | solution.py:331
  19.4 0.0 collective-permute-done.2.refs_4_
  19.4 0.0 collective-permute-done.4.refs_6_
  19.4 0.2 collective-permute-done.6.refs_8_
  19.6 0.2 collective-permute-done.10.refs_12_
  19.8 0.4 %collective-permute-done.12.refs_14_ = bf16[4,8,1024]{2,1,0:T(8,128)(2,1)} collective-permute-done((bf16[4,8,1024]{2,1,0:T(8,128)(2,1)S(1)}, bf16[4,8,1024]{2,1,0:T(8,128)(2,1)}, u32[]{:S(2)}, u32[]{:S(2)}) %collective-permute-start.12) | collective-permute-done | bytes 65568 | tf_op jit(solution)/shard_map/ppermute | solution.py:286
  20.2 1.4 %shard_map.49 = bf16[136,128]{1,0:T(8,128)(2,1)S(1)} custom-call(bf16[4,272,1024]{2,1,0:T(8,128)(2,1)S(1)} %shard_map.47.refs_0_, bf16[4,8,1024]{2,1,0:T(8,128)(2,1)S(1)} %get-tuple-element.8.w_ref.refs_1_, bf16[4,8,1024]{2,1,0:T(8,128)(2,1)S(1)} %collective-permute-done.refs_2_, bf16[4,8,1024]{2,1,0:T(8,128)(2,1)S(1)} %collective-permute-done.1.refs_3_, ...), custom_call_target="tpu_custom_call" | custom-call | flops 142606336 | bytes 2162688 | tf_op jit(solution)/shard_map/pallas_call | solution.py:345
  21.6 1.6 %collective-permute-start.15 = (bf16[136,128]{1,0:T(8,128)(2,1)S(1)}, bf16[136,128]{1,0:T(8,128)(2,1)S(1)}, u32[]{:S(2)}, u32[]{:S(2)}) collective-permute-start(bf16[136,128]{1,0:T(8,128)(2,1)S(1)} %shard_map.49), channel_id=1, source_target_pairs={{0,1},{1,0},{2,3},{3,2},{4,5},{5,4},{6,7},{7,6},{8,9},{9,8},{10,11... | collective-permute-start | bytes 104456 | tf_op jit(solution)/shard_map/ppermute | solution.py:359
  23.2 1.4 %shard_map.48.keep_ref = f32[136,128]{1,0:T(8,128)S(1)} custom-call(bf16[4,272,1024]{2,1,0:T(8,128)(2,1)S(1)} %shard_map.47.refs_0_, bf16[4,8,1024]{2,1,0:T(8,128)(2,1)S(1)} %get-tuple-element.8.w_ref.refs_1_, bf16[4,8,1024]{2,1,0:T(8,128)(2,1)S(1)} %collective-permute-done.refs_2_, bf16[4,8,1024]{2,1,0:T(8,128)(2,1)S(1)} %collective-permute-done.1.refs_3_, ...), custom_call_target="tpu_custom_call" | custom-call | flops 142606336 | bytes 2162688 | tf_op jit(solution)/shard_map/pallas_call | solution.py:345
  24.6 1.0 %collective-permute-done.15.got_ref = bf16[136,128]{1,0:T(8,128)(2,1)S(1)} collective-permute-done((bf16[136,128]{1,0:T(8,128)(2,1)S(1)}, bf16[136,128]{1,0:T(8,128)(2,1)S(1)}, u32[]{:S(2)}, u32[]{:S(2)}) %collective-permute-start.15) | collective-permute-done | bytes 34848 | tf_op jit(solution)/shard_map/ppermute | solution.py:359
  25.6 0.7 %shard_map.50 = f32[33,4,128]{2,1,0:T(4,128)} custom-call(s32[1]{0:T(128)} %bitcast.me_ref, f32[136,128]{1,0:T(8,128)S(1)} %shard_map.48.keep_ref, bf16[136,128]{1,0:T(8,128)(2,1)S(1)} %collective-permute-done.15.got_ref), custom_call_target="tpu_custom_call" | custom-call | tf_op jit(solution)/shard_map/pallas_call | solution.py:361
Async XLA Ops:
  1.3 9.9 %collective-permute-start.7 = (bf16[4,8,1024]{2,1,0:T(8,128)(2,1)S(1)}, bf16[4,8,1024]{2,1,0:T(8,128)(2,1)S(1)}, u32[]{:S(2)}, u32[]{:S(2)}) collective-permute-start(bf16[4,8,1024]{2,1,0:T(8,128)(2,1)S(1)} %get-tuple-element.8.w_ref.refs_1_), channel_id=1, source_target_pairs={{0,16},{2,18},{4,20},{6,22},{8,24},{10,26},{12,28},{14,30},{16,0},... | collective-permute-start | bytes 196616 | tf_op jit(solution)/shard_map/ppermute | solution.py:286
  5.4 7.4 %collective-permute-start.13 = (bf16[4,8,1024]{2,1,0:T(8,128)(2,1)S(1)}, bf16[4,8,1024]{2,1,0:T(8,128)(2,1)S(1)}, u32[]{:S(2)}, u32[]{:S(2)}) collective-permute-start(bf16[4,8,1024]{2,1,0:T(8,128)(2,1)S(1)} %get-tuple-element.8.w_ref.refs_1_), channel_id=1, source_target_pairs={{0,28},{2,30},{4,24},{6,26},{8,20},{10,22},{12,16},{14,18},{16,12}... | collective-permute-start | bytes 196616 | tf_op jit(solution)/shard_map/ppermute | solution.py:286
  7.7 6.3 %collective-permute-start.1 = (bf16[4,8,1024]{2,1,0:T(8,128)(2,1)S(1)}, bf16[4,8,1024]{2,1,0:T(8,128)(2,1)S(1)}, u32[]{:S(2)}, u32[]{:S(2)}) collective-permute-start(bf16[4,8,1024]{2,1,0:T(8,128)(2,1)S(1)} %get-tuple-element.8.w_ref.refs_1_), channel_id=1, source_target_pairs={{0,4},{2,6},{4,0},{6,2},{8,12},{10,14},{12,8},{14,10},{16,20},{18,... | collective-permute-start | bytes 196616 | tf_op jit(solution)/shard_map/ppermute | solution.py:286
  8.2 6.2 %collective-permute-start.3 = (bf16[4,8,1024]{2,1,0:T(8,128)(2,1)S(1)}, bf16[4,8,1024]{2,1,0:T(8,128)(2,1)S(1)}, u32[]{:S(2)}, u32[]{:S(2)}) collective-permute-start(bf16[4,8,1024]{2,1,0:T(8,128)(2,1)S(1)} %get-tuple-element.8.w_ref.refs_1_), channel_id=1, source_target_pairs={{0,8},{2,10},{4,12},{6,14},{8,0},{10,2},{12,4},{14,6},{16,24},{18,... | collective-permute-start | bytes 196616 | tf_op jit(solution)/shard_map/ppermute | solution.py:286
  8.5 6.1 %collective-permute-start.5 = (bf16[4,8,1024]{2,1,0:T(8,128)(2,1)S(1)}, bf16[4,8,1024]{2,1,0:T(8,128)(2,1)S(1)}, u32[]{:S(2)}, u32[]{:S(2)}) collective-permute-start(bf16[4,8,1024]{2,1,0:T(8,128)(2,1)S(1)} %get-tuple-element.8.w_ref.refs_1_), channel_id=1, source_target_pairs={{0,12},{2,14},{4,8},{6,10},{8,4},{10,6},{12,0},{14,2},{16,28},{18,... | collective-permute-start | bytes 196616 | tf_op jit(solution)/shard_map/ppermute | solution.py:286
  11.2 3.7 %collective-permute-start = (bf16[4,8,1024]{2,1,0:T(8,128)(2,1)S(1)}, bf16[4,8,1024]{2,1,0:T(8,128)(2,1)S(1)}, u32[]{:S(2)}, u32[]{:S(2)}) collective-permute-start(bf16[4,8,1024]{2,1,0:T(8,128)(2,1)S(1)} %get-tuple-element.8.w_ref.refs_1_), channel_id=1, source_target_pairs={{0,2},{2,0},{4,6},{6,4},{8,10},{10,8},{12,14},{14,12},{16,18},{18,... | collective-permute-start | bytes 196616 | tf_op jit(solution)/shard_map/ppermute | solution.py:286
  12.8 4.3 %collective-permute-start.9 = (bf16[4,8,1024]{2,1,0:T(8,128)(2,1)S(1)}, bf16[4,8,1024]{2,1,0:T(8,128)(2,1)S(1)}, u32[]{:S(2)}, u32[]{:S(2)}) collective-permute-start(bf16[4,8,1024]{2,1,0:T(8,128)(2,1)S(1)} %collective-permute-done.7.refs_9_), channel_id=1, source_target_pairs={{0,4},{2,6},{4,0},{6,2},{8,12},{10,14},{12,8},{14,10},{16,20},{18,... | collective-permute-start | bytes 196616 | tf_op jit(solution)/shard_map/ppermute | solution.py:286
  14.0 4.3 %collective-permute-start.11 = (bf16[4,8,1024]{2,1,0:T(8,128)(2,1)S(1)}, bf16[4,8,1024]{2,1,0:T(8,128)(2,1)S(1)}, u32[]{:S(2)}, u32[]{:S(2)}) collective-permute-start(bf16[4,8,1024]{2,1,0:T(8,128)(2,1)S(1)} %collective-permute-done.7.refs_9_), channel_id=1, source_target_pairs={{0,8},{2,10},{4,12},{6,14},{8,0},{10,2},{12,4},{14,6},{16,24},{18,... | collective-permute-start | bytes 196616 | tf_op jit(solution)/shard_map/ppermute | solution.py:286
  14.4 3.9 %collective-permute-start.8 = (bf16[4,8,1024]{2,1,0:T(8,128)(2,1)S(1)}, bf16[4,8,1024]{2,1,0:T(8,128)(2,1)S(1)}, u32[]{:S(2)}, u32[]{:S(2)}) collective-permute-start(bf16[4,8,1024]{2,1,0:T(8,128)(2,1)S(1)} %collective-permute-done.7.refs_9_), channel_id=1, source_target_pairs={{0,2},{2,0},{4,6},{6,4},{8,10},{10,8},{12,14},{14,12},{16,18},{18,... | collective-permute-start | bytes 196616 | tf_op jit(solution)/shard_map/ppermute | solution.py:286
  14.6 4.2 %collective-permute-start.14 = (bf16[4,8,1024]{2,1,0:T(8,128)(2,1)S(1)}, bf16[4,8,1024]{2,1,0:T(8,128)(2,1)S(1)}, u32[]{:S(2)}, u32[]{:S(2)}) collective-permute-start(bf16[4,8,1024]{2,1,0:T(8,128)(2,1)S(1)} %collective-permute-done.13.refs_15_), channel_id=1, source_target_pairs={{0,2},{2,0},{4,6},{6,4},{8,10},{10,8},{12,14},{14,12},{16,18},{18,... | collective-permute-start | bytes 196616 | tf_op jit(solution)/shard_map/ppermute | solution.py:286
  14.9 4.5 %collective-permute-start.2 = (bf16[4,8,1024]{2,1,0:T(8,128)(2,1)S(1)}, bf16[4,8,1024]{2,1,0:T(8,128)(2,1)}, u32[]{:S(2)}, u32[]{:S(2)}) collective-permute-start(bf16[4,8,1024]{2,1,0:T(8,128)(2,1)S(1)} %collective-permute-done.1.refs_3_), channel_id=1, source_target_pairs={{0,2},{2,0},{4,6},{6,4},{8,10},{10,8},{12,14},{14,12},{16,18},{18,... | collective-permute-start | bytes 196616 | tf_op jit(solution)/shard_map/ppermute | solution.py:286
  17.1 2.3 %collective-permute-start.4 = (bf16[4,8,1024]{2,1,0:T(8,128)(2,1)S(1)}, bf16[4,8,1024]{2,1,0:T(8,128)(2,1)}, u32[]{:S(2)}, u32[]{:S(2)}) collective-permute-start(bf16[4,8,1024]{2,1,0:T(8,128)(2,1)S(1)} %collective-permute-done.3.refs_5_), channel_id=1, source_target_pairs={{0,2},{2,0},{4,6},{6,4},{8,10},{10,8},{12,14},{14,12},{16,18},{18,... | collective-permute-start | bytes 196616 | tf_op jit(solution)/shard_map/ppermute | solution.py:286
  18.2 1.4 %collective-permute-start.6 = (bf16[4,8,1024]{2,1,0:T(8,128)(2,1)S(1)}, bf16[4,8,1024]{2,1,0:T(8,128)(2,1)}, u32[]{:S(2)}, u32[]{:S(2)}) collective-permute-start(bf16[4,8,1024]{2,1,0:T(8,128)(2,1)S(1)} %collective-permute-done.5.refs_7_), channel_id=1, source_target_pairs={{0,2},{2,0},{4,6},{6,4},{8,10},{10,8},{12,14},{14,12},{16,18},{18,... | collective-permute-start | bytes 196616 | tf_op jit(solution)/shard_map/ppermute | solution.py:286
  18.3 1.5 %collective-permute-start.10 = (bf16[4,8,1024]{2,1,0:T(8,128)(2,1)S(1)}, bf16[4,8,1024]{2,1,0:T(8,128)(2,1)}, u32[]{:S(2)}, u32[]{:S(2)}) collective-permute-start(bf16[4,8,1024]{2,1,0:T(8,128)(2,1)S(1)} %collective-permute-done.9.refs_11_), channel_id=1, source_target_pairs={{0,2},{2,0},{4,6},{6,4},{8,10},{10,8},{12,14},{14,12},{16,18},{18,... | collective-permute-start | bytes 196616 | tf_op jit(solution)/shard_map/ppermute | solution.py:286
  18.8 1.4 %collective-permute-start.12 = (bf16[4,8,1024]{2,1,0:T(8,128)(2,1)S(1)}, bf16[4,8,1024]{2,1,0:T(8,128)(2,1)}, u32[]{:S(2)}, u32[]{:S(2)}) collective-permute-start(bf16[4,8,1024]{2,1,0:T(8,128)(2,1)S(1)} %collective-permute-done.11.refs_13_), channel_id=1, source_target_pairs={{0,2},{2,0},{4,6},{6,4},{8,10},{10,8},{12,14},{14,12},{16,18},{18,... | collective-permute-start | bytes 196616 | tf_op jit(solution)/shard_map/ppermute | solution.py:286
  21.6 4.0 %collective-permute-start.15 = (bf16[136,128]{1,0:T(8,128)(2,1)S(1)}, bf16[136,128]{1,0:T(8,128)(2,1)S(1)}, u32[]{:S(2)}, u32[]{:S(2)}) collective-permute-start(bf16[136,128]{1,0:T(8,128)(2,1)S(1)} %shard_map.49), channel_id=1, source_target_pairs={{0,1},{1,0},{2,3},{3,2},{4,5},{5,4},{6,7},{7,6},{8,9},{9,8},{10,11... | collective-permute-start | bytes 104456 | tf_op jit(solution)/shard_map/ppermute | solution.py:359

commit v7 on v6

--- a/solution.py
+++ b/solution.py
@@ -253,7 +253,11 @@
     lags, part, _ = out_ref.shape
     value = (keep_ref[...] + got_ref[...].astype(jnp.float32)) * scale
     lane = lax.broadcasted_iota(jnp.int32, value.shape, 1)
-    index = ((lane // own) ^ me_ref[0]) * own + lane % own
+    me = me_ref[0]
+    block = (lane // own) ^ me
+    crossed = (block & ~6) | ((block & 2) << 1) | ((block & 4) >> 1)
+    block = jnp.where((me & 1) != 0, crossed, block)
+    index = block * own + lane % own
     value = jnp.take_along_axis(value, index, axis=1)
     for lag in range(lags):
         out_ref[lag] = value[lag * part : (lag + 1) * part]
@@ -267,24 +271,26 @@
     held, plan = [0], []
     bit = col // 2
     while bit > NEAR:
-        plan += [(m | bit, m, bit) for m in held]
+        plan += [(m | bit, m, bit, bit) for m in held]
         held += [m | bit for m in held]
         bit //= 2
     far = held[1:]
-    plan += [(m | cross, 0, m | cross) for m in held]
+    plan += [(m | cross, 0, m | cross, m | cross) for m in held]
     for m in held:
-        plan += [(m | SIDE, m, SIDE), (m | NEAR, m, NEAR)]
-    mates = [cross, 0, SIDE] + far + [NEAR]
+        plan += [(m | SIDE, m, SIDE, NEAR), (m | NEAR, m, NEAR, SIDE)]
+    mates = [0, cross] + far + [SIDE, NEAR]
     for m in far:
-        mates += [m | cross, m | SIDE, m | NEAR]
-    return plan + [(m | CORE, m, CORE) for m in mates]
+        mates += [m | SIDE, m | cross, m | NEAR]
+    return plan + [(m | CORE, m, CORE, CORE) for m in mates]
 
 
 def gather(own_block, col):
     blocks = {0: own_block}
-    for block, source, distance in gather_plan(col):
-        blocks[block] = lax.ppermute(blocks[source], "col", [(i, i ^ distance) for i in range(col)])
-    return [blocks[m] for m in range(col)]
+    for block, source, even, odd in gather_plan(col):
+        pairs = [(i, i ^ (odd if i & 1 else even)) for i in range(col)]
+        blocks[block] = lax.ppermute(blocks[source], "col", pairs)
+    order = [m ^ (6 if m & 1 and (m & 6) in (SIDE, NEAR) else 0) for m in range(col)]
+    return [blocks[m] for m in order]
 
 
 def fast_device(traces, valid):
@@ -353,7 +359,7 @@
                 bytes_accessed=2 * (rows + lanes) * segs * length,
                 transcendentals=0,
             ),
-        )(pltpu.with_memory_space_constraint(rotated, pltpu.VMEM), *blocks)
+        )(*[pltpu.with_memory_space_constraint(x, pltpu.VMEM) for x in (rotated, *blocks)])
 
     send = multiply(send_kernel, jnp.bfloat16)
     got = lax.ppermute(send, "seg", [(0, 1), (1, 0)])

time: 26.6 us -> 26.3 us (0.989)
  starting transfers between devices: 14.1 us -> 13.7 us
    ppermute x15, starting transfers between devices: 12.6 us -> 12.2 us  [gather(): blocks[block] = lax.ppermute(blocks[source], 'col', pairs)]
  transfers between devices with their start and end apart: 16 -> 16, of which waited for: 8 -> 8; matrix products, arithmetic and copies ran while one was open for 0% -> 0% of each run, Pallas kernels for 7% -> 8%
where the time goes in v7:
time: 26.3 us; the launch traced here: 26.1 us
  starting transfers between devices  13.7 us (52%)
  waiting for transfers between devices  6.88 us (26%)
  Pallas kernels  5.39 us (20%)
    ppermute x15, starting transfers between devices, gather(): blocks[block] = lax.ppermute(blocks[source], 'col', pairs)  12.2 us
    ppermute x15, waiting for transfers between devices, gather(): blocks[block] = lax.ppermute(blocks[source], 'col', pairs)  5.87 us
    pallas_call x2, Pallas kernels, multiply(): pl.pallas_call(kernel, out_shape=jax.ShapeDtypeStruct((rows, lanes), dtyp...  2.88 us
    ppermute x1, starting transfers between devices, fast_body(): got = lax.ppermute(send, 'seg', [(0, 1), (1, 0)])  1.55 us
    pallas_call x1, Pallas kernels, fast_body(): pl.pallas_call(whiten_kernel, out_shape=[jax.ShapeDtypeStruct(traces.shap...  1.25 us
    ppermute x1, waiting for transfers between devices, fast_body(): got = lax.ppermute(send, 'seg', [(0, 1), (1, 0)])  1 us
    pallas_call x1, Pallas kernels, fast_body(): pl.pallas_call(functools.partial(finish_kernel, scale, own), out_shape=ja...  0.73 us
    pallas_call x1, Pallas kernels, fast_body(): pl.pallas_call(rotate_kernel, out_shape=jax.ShapeDtypeStruct((segs, 2 * r...  0.53 us
  transfers between devices with their start and end apart: 16, of which 8 were waited for; matrix products, arithmetic and copies ran while one was open for 0% of the time, Pallas kernels for 8%

profile of v7, /device:TPU:0, one launch (start us, length us, event | category | flops | bytes accessed | tf_op | source)
XLA Modules:
  0.0 26.1 jit_solution(6768673936137523633)
XLA Ops:
  0.0 1.2 %shard_map.46 = (bf16[4,8,1024]{2,1,0:T(8,128)(2,1)S(1)}, f32[136,512]{1,0:T(8,128)S(1)}, f32[136,512]{1,0:T(8,128)S(1)}) custom-call(bf16[4,8,1024]{2,1,0:T(8,128)(2,1)} %x_in.1, s32[4,8]{1,0:T(4,128)} %v_in.1, f32[136,512]{1,0:T(8,128)} %constant.12.clone.c_in, f32[136,512]{1,0:T(8,128)} %constant.13.clone.s_in), custom_call_target="tpu_custom_call" | custom-call | tf_op jit(solution)/shard_map/pallas_call | solution.py:311
  1.3 4.1 %collective-permute-start.7 = (bf16[4,8,1024]{2,1,0:T(8,128)(2,1)S(1)}, bf16[4,8,1024]{2,1,0:T(8,128)(2,1)S(1)}, u32[]{:S(2)}, u32[]{:S(2)}) collective-permute-start(bf16[4,8,1024]{2,1,0:T(8,128)(2,1)S(1)} %get-tuple-element.8.w_ref.refs_1_), channel_id=1, source_target_pairs={{0,16},{2,18},{4,20},{6,22},{8,24},{10,26},{12,28},{14,30},{16,0},... | collective-permute-start | bytes 196616 | tf_op jit(solution)/shard_map/ppermute | solution.py:291
  5.4 2.3 %collective-permute-start.13 = (bf16[4,8,1024]{2,1,0:T(8,128)(2,1)S(1)}, bf16[4,8,1024]{2,1,0:T(8,128)(2,1)S(1)}, u32[]{:S(2)}, u32[]{:S(2)}) collective-permute-start(bf16[4,8,1024]{2,1,0:T(8,128)(2,1)S(1)} %get-tuple-element.8.w_ref.refs_1_), channel_id=1, source_target_pairs={{0,28},{2,30},{4,24},{6,26},{8,20},{10,22},{12,16},{14,18},{16,12}... | collective-permute-start | bytes 196616 | tf_op jit(solution)/shard_map/ppermute | solution.py:291
  7.7 0.0 collective-permute-start.2
  7.7 0.8 %collective-permute-start.1 = (bf16[4,8,1024]{2,1,0:T(8,128)(2,1)S(1)}, bf16[4,8,1024]{2,1,0:T(8,128)(2,1)S(1)}, u32[]{:S(2)}, u32[]{:S(2)}) collective-permute-start(bf16[4,8,1024]{2,1,0:T(8,128)(2,1)S(1)} %get-tuple-element.8.w_ref.refs_1_), channel_id=1, source_target_pairs={{0,4},{2,10},{4,0},{6,14},{8,12},{10,2},{12,8},{14,6},{16,20},{18,... | collective-permute-start | bytes 196616 | tf_op jit(solution)/shard_map/ppermute | solution.py:291
  8.5 2.7 %collective-permute-start.5 = (bf16[4,8,1024]{2,1,0:T(8,128)(2,1)S(1)}, bf16[4,8,1024]{2,1,0:T(8,128)(2,1)S(1)}, u32[]{:S(2)}, u32[]{:S(2)}) collective-permute-start(bf16[4,8,1024]{2,1,0:T(8,128)(2,1)S(1)} %get-tuple-element.8.w_ref.refs_1_), channel_id=1, source_target_pairs={{0,12},{2,14},{4,8},{6,10},{8,4},{10,6},{12,0},{14,2},{16,28},{18,... | collective-permute-start | bytes 196616 | tf_op jit(solution)/shard_map/ppermute | solution.py:291
  11.2 0.0 collective-permute-done.7.refs_9_
  11.2 0.0 collective-permute-start
  11.2 1.6 %collective-permute-done.13.refs_15_ = bf16[4,8,1024]{2,1,0:T(8,128)(2,1)S(1)} collective-permute-done((bf16[4,8,1024]{2,1,0:T(8,128)(2,1)S(1)}, bf16[4,8,1024]{2,1,0:T(8,128)(2,1)S(1)}, u32[]{:S(2)}, u32[]{:S(2)}) %collective-permute-start.13) | collective-permute-done | bytes 65568 | tf_op jit(solution)/shard_map/ppermute | solution.py:291
  12.8 0.9 %collective-permute-start.10 = (bf16[4,8,1024]{2,1,0:T(8,128)(2,1)S(1)}, bf16[4,8,1024]{2,1,0:T(8,128)(2,1)S(1)}, u32[]{:S(2)}, u32[]{:S(2)}) collective-permute-start(bf16[4,8,1024]{2,1,0:T(8,128)(2,1)S(1)} %collective-permute-done.7.refs_9_), channel_id=1, source_target_pairs={{0,8},{2,6},{4,12},{6,2},{8,0},{10,14},{12,4},{14,10},{16,24},{18,... | collective-permute-start | bytes 196616 | tf_op jit(solution)/shard_map/ppermute | solution.py:291
  13.7 0.0 collective-permute-done.2.refs_5_
  13.7 0.3 %collective-permute-start.9 = (bf16[4,8,1024]{2,1,0:T(8,128)(2,1)S(1)}, bf16[4,8,1024]{2,1,0:T(8,128)(2,1)S(1)}, u32[]{:S(2)}, u32[]{:S(2)}) collective-permute-start(bf16[4,8,1024]{2,1,0:T(8,128)(2,1)S(1)} %collective-permute-done.7.refs_9_), channel_id=1, source_target_pairs={{0,4},{2,10},{4,0},{6,14},{8,12},{10,2},{12,8},{14,6},{16,20},{18,... | collective-permute-start | bytes 196616 | tf_op jit(solution)/shard_map/ppermute | solution.py:291
  14.0 0.0 collective-permute-done.1.refs_3_
  14.0 0.0 collective-permute-start.8
  14.0 0.6 %collective-permute-done.5.refs_7_ = bf16[4,8,1024]{2,1,0:T(8,128)(2,1)S(1)} collective-permute-done((bf16[4,8,1024]{2,1,0:T(8,128)(2,1)S(1)}, bf16[4,8,1024]{2,1,0:T(8,128)(2,1)S(1)}, u32[]{:S(2)}, u32[]{:S(2)}) %collective-permute-start.5) | collective-permute-done | bytes 65568 | tf_op jit(solution)/shard_map/ppermute | solution.py:291
  14.6 0.0 collective-permute-start.14
  14.6 0.0 collective-permute-done.refs_2_
  14.6 0.5 %collective-permute-start.3 = (bf16[4,8,1024]{2,1,0:T(8,128)(2,1)S(1)}, bf16[4,8,1024]{2,1,0:T(8,128)(2,1)}, u32[]{:S(2)}, u32[]{:S(2)}) collective-permute-start(bf16[4,8,1024]{2,1,0:T(8,128)(2,1)S(1)} %collective-permute-done.2.refs_5_), channel_id=1, source_target_pairs={{0,2},{2,0},{4,6},{6,4},{8,10},{10,8},{12,14},{14,12},{16,18},{18,... | collective-permute-start | bytes 196616 | tf_op jit(solution)/shard_map/ppermute | solution.py:291
  15.1 2.0 %collective-permute-done.10.refs_13_ = bf16[4,8,1024]{2,1,0:T(8,128)(2,1)S(1)} collective-permute-done((bf16[4,8,1024]{2,1,0:T(8,128)(2,1)S(1)}, bf16[4,8,1024]{2,1,0:T(8,128)(2,1)S(1)}, u32[]{:S(2)}, u32[]{:S(2)}) %collective-permute-start.10) | collective-permute-done | bytes 65568 | tf_op jit(solution)/shard_map/ppermute | solution.py:291
  17.1 0.0 collective-permute-start.4
  17.1 0.9 %collective-permute-done.9.refs_11_ = bf16[4,8,1024]{2,1,0:T(8,128)(2,1)S(1)} collective-permute-done((bf16[4,8,1024]{2,1,0:T(8,128)(2,1)S(1)}, bf16[4,8,1024]{2,1,0:T(8,128)(2,1)S(1)}, u32[]{:S(2)}, u32[]{:S(2)}) %collective-permute-start.9) | collective-permute-done | bytes 65568 | tf_op jit(solution)/shard_map/ppermute | solution.py:291
  18.0 0.0 collective-permute-start.6
  18.0 0.0 collective-permute-done.8.refs_10_
  18.0 0.5 %collective-permute-start.11 = (bf16[4,8,1024]{2,1,0:T(8,128)(2,1)S(1)}, bf16[4,8,1024]{2,1,0:T(8,128)(2,1)}, u32[]{:S(2)}, u32[]{:S(2)}) collective-permute-start(bf16[4,8,1024]{2,1,0:T(8,128)(2,1)S(1)} %collective-permute-done.10.refs_13_), channel_id=1, source_target_pairs={{0,2},{2,0},{4,6},{6,4},{8,10},{10,8},{12,14},{14,12},{16,18},{18,... | collective-permute-start | bytes 196616 | tf_op jit(solution)/shard_map/ppermute | solution.py:291
  18.5 0.0 collective-permute-done.14.refs_16_
  18.5 0.1 collective-permute-start.12
  18.6 0.5 %shard_map.47.refs_0_ = bf16[4,272,1024]{2,1,0:T(8,128)(2,1)S(1)} custom-call(s32[1]{0:T(128)} %bitcast.1.seg_ref, bf16[4,8,1024]{2,1,0:T(8,128)(2,1)S(1)} %get-tuple-element.8.w_ref.refs_1_, f32[136,512]{1,0:T(8,128)S(1)} %get-tuple-element.9.c_ref, f32[136,512]{1,0:T(8,128)S(1)} %get-tuple-element.10.s_ref), custom_call_target="tpu_custom_call" | custom-call | flops 6684672 | bytes 2228224 | tf_op jit(solution)/shard_map/pallas_call | solution.py:337
  19.1 0.0 collective-permute-done.3.refs_4_
  19.1 0.0 collective-permute-done.4.refs_6_
  19.1 0.2 collective-permute-done.6.refs_8_
  19.4 0.2 collective-permute-done.11.refs_12_
  19.5 0.4 %collective-permute-done.12.refs_14_ = bf16[4,8,1024]{2,1,0:T(8,128)(2,1)} collective-permute-done((bf16[4,8,1024]{2,1,0:T(8,128)(2,1)S(1)}, bf16[4,8,1024]{2,1,0:T(8,128)(2,1)}, u32[]{:S(2)}, u32[]{:S(2)}) %collective-permute-start.12) | collective-permute-done | bytes 65568 | tf_op jit(solution)/shard_map/ppermute | solution.py:291
  19.9 1.4 %shard_map.49 = bf16[136,128]{1,0:T(8,128)(2,1)S(1)} custom-call(bf16[4,272,1024]{2,1,0:T(8,128)(2,1)S(1)} %shard_map.47.refs_0_, bf16[4,8,1024]{2,1,0:T(8,128)(2,1)S(1)} %get-tuple-element.8.w_ref.refs_1_, bf16[4,8,1024]{2,1,0:T(8,128)(2,1)S(1)} %collective-permute-done.refs_2_, bf16[4,8,1024]{2,1,0:T(8,128)(2,1)S(1)} %collective-permute-done.1.refs_3_, ...), custom_call_target="tpu_custom_call" | custom-call | flops 142606336 | bytes 2162688 | tf_op jit(solution)/shard_map/pallas_call | solution.py:351
  21.3 1.6 %collective-permute-start.15 = (bf16[136,128]{1,0:T(8,128)(2,1)S(1)}, bf16[136,128]{1,0:T(8,128)(2,1)S(1)}, u32[]{:S(2)}, u32[]{:S(2)}) collective-permute-start(bf16[136,128]{1,0:T(8,128)(2,1)S(1)} %shard_map.49), channel_id=1, source_target_pairs={{0,1},{1,0},{2,3},{3,2},{4,5},{5,4},{6,7},{7,6},{8,9},{9,8},{10,11... | collective-permute-start | bytes 104456 | tf_op jit(solution)/shard_map/ppermute | solution.py:365
  22.9 1.4 %shard_map.48.keep_ref = f32[136,128]{1,0:T(8,128)S(1)} custom-call(bf16[4,272,1024]{2,1,0:T(8,128)(2,1)S(1)} %shard_map.47.refs_0_, bf16[4,8,1024]{2,1,0:T(8,128)(2,1)S(1)} %get-tuple-element.8.w_ref.refs_1_, bf16[4,8,1024]{2,1,0:T(8,128)(2,1)S(1)} %collective-permute-done.refs_2_, bf16[4,8,1024]{2,1,0:T(8,128)(2,1)S(1)} %collective-permute-done.1.refs_3_, ...), custom_call_target="tpu_custom_call" | custom-call | flops 142606336 | bytes 2162688 | tf_op jit(solution)/shard_map/pallas_call | solution.py:351
  24.3 1.0 %collective-permute-done.15.got_ref = bf16[136,128]{1,0:T(8,128)(2,1)S(1)} collective-permute-done((bf16[136,128]{1,0:T(8,128)(2,1)S(1)}, bf16[136,128]{1,0:T(8,128)(2,1)S(1)}, u32[]{:S(2)}, u32[]{:S(2)}) %collective-permute-start.15) | collective-permute-done | bytes 34848 | tf_op jit(solution)/shard_map/ppermute | solution.py:365
  25.3 0.7 %shard_map.50 = f32[33,4,128]{2,1,0:T(4,128)} custom-call(s32[1]{0:T(128)} %bitcast.me_ref, f32[136,128]{1,0:T(8,128)S(1)} %shard_map.48.keep_ref, bf16[136,128]{1,0:T(8,128)(2,1)S(1)} %collective-permute-done.15.got_ref), custom_call_target="tpu_custom_call" | custom-call | tf_op jit(solution)/shard_map/pallas_call | solution.py:367
Async XLA Ops:
  1.3 9.9 %collective-permute-start.7 = (bf16[4,8,1024]{2,1,0:T(8,128)(2,1)S(1)}, bf16[4,8,1024]{2,1,0:T(8,128)(2,1)S(1)}, u32[]{:S(2)}, u32[]{:S(2)}) collective-permute-start(bf16[4,8,1024]{2,1,0:T(8,128)(2,1)S(1)} %get-tuple-element.8.w_ref.refs_1_), channel_id=1, source_target_pairs={{0,16},{2,18},{4,20},{6,22},{8,24},{10,26},{12,28},{14,30},{16,0},... | collective-permute-start | bytes 196616 | tf_op jit(solution)/shard_map/ppermute | solution.py:291
  5.4 7.4 %collective-permute-start.13 = (bf16[4,8,1024]{2,1,0:T(8,128)(2,1)S(1)}, bf16[4,8,1024]{2,1,0:T(8,128)(2,1)S(1)}, u32[]{:S(2)}, u32[]{:S(2)}) collective-permute-start(bf16[4,8,1024]{2,1,0:T(8,128)(2,1)S(1)} %get-tuple-element.8.w_ref.refs_1_), channel_id=1, source_target_pairs={{0,28},{2,30},{4,24},{6,26},{8,20},{10,22},{12,16},{14,18},{16,12}... | collective-permute-start | bytes 196616 | tf_op jit(solution)/shard_map/ppermute | solution.py:291
  7.7 6.0 %collective-permute-start.2 = (bf16[4,8,1024]{2,1,0:T(8,128)(2,1)S(1)}, bf16[4,8,1024]{2,1,0:T(8,128)(2,1)S(1)}, u32[]{:S(2)}, u32[]{:S(2)}) collective-permute-start(bf16[4,8,1024]{2,1,0:T(8,128)(2,1)S(1)} %get-tuple-element.8.w_ref.refs_1_), channel_id=1, source_target_pairs={{0,8},{2,6},{4,12},{6,2},{8,0},{10,14},{12,4},{14,10},{16,24},{18,... | collective-permute-start | bytes 196616 | tf_op jit(solution)/shard_map/ppermute | solution.py:291
  7.7 6.3 %collective-permute-start.1 = (bf16[4,8,1024]{2,1,0:T(8,128)(2,1)S(1)}, bf16[4,8,1024]{2,1,0:T(8,128)(2,1)S(1)}, u32[]{:S(2)}, u32[]{:S(2)}) collective-permute-start(bf16[4,8,1024]{2,1,0:T(8,128)(2,1)S(1)} %get-tuple-element.8.w_ref.refs_1_), channel_id=1, source_target_pairs={{0,4},{2,10},{4,0},{6,14},{8,12},{10,2},{12,8},{14,6},{16,20},{18,... | collective-permute-start | bytes 196616 | tf_op jit(solution)/shard_map/ppermute | solution.py:291
  8.5 6.1 %collective-permute-start.5 = (bf16[4,8,1024]{2,1,0:T(8,128)(2,1)S(1)}, bf16[4,8,1024]{2,1,0:T(8,128)(2,1)S(1)}, u32[]{:S(2)}, u32[]{:S(2)}) collective-permute-start(bf16[4,8,1024]{2,1,0:T(8,128)(2,1)S(1)} %get-tuple-element.8.w_ref.refs_1_), channel_id=1, source_target_pairs={{0,12},{2,14},{4,8},{6,10},{8,4},{10,6},{12,0},{14,2},{16,28},{18,... | collective-permute-start | bytes 196616 | tf_op jit(solution)/shard_map/ppermute | solution.py:291
  11.2 3.4 %collective-permute-start = (bf16[4,8,1024]{2,1,0:T(8,128)(2,1)S(1)}, bf16[4,8,1024]{2,1,0:T(8,128)(2,1)S(1)}, u32[]{:S(2)}, u32[]{:S(2)}) collective-permute-start(bf16[4,8,1024]{2,1,0:T(8,128)(2,1)S(1)} %get-tuple-element.8.w_ref.refs_1_), channel_id=1, source_target_pairs={{0,2},{2,0},{4,6},{6,4},{8,10},{10,8},{12,14},{14,12},{16,18},{18,... | collective-permute-start | bytes 196616 | tf_op jit(solution)/shard_map/ppermute | solution.py:291
  12.8 4.3 %collective-permute-start.10 = (bf16[4,8,1024]{2,1,0:T(8,128)(2,1)S(1)}, bf16[4,8,1024]{2,1,0:T(8,128)(2,1)S(1)}, u32[]{:S(2)}, u32[]{:S(2)}) collective-permute-start(bf16[4,8,1024]{2,1,0:T(8,128)(2,1)S(1)} %collective-permute-done.7.refs_9_), channel_id=1, source_target_pairs={{0,8},{2,6},{4,12},{6,2},{8,0},{10,14},{12,4},{14,10},{16,24},{18,... | collective-permute-start | bytes 196616 | tf_op jit(solution)/shard_map/ppermute | solution.py:291
  13.7 4.3 %collective-permute-start.9 = (bf16[4,8,1024]{2,1,0:T(8,128)(2,1)S(1)}, bf16[4,8,1024]{2,1,0:T(8,128)(2,1)S(1)}, u32[]{:S(2)}, u32[]{:S(2)}) collective-permute-start(bf16[4,8,1024]{2,1,0:T(8,128)(2,1)S(1)} %collective-permute-done.7.refs_9_), channel_id=1, source_target_pairs={{0,4},{2,10},{4,0},{6,14},{8,12},{10,2},{12,8},{14,6},{16,20},{18,... | collective-permute-start | bytes 196616 | tf_op jit(solution)/shard_map/ppermute | solution.py:291
  14.0 4.0 %collective-permute-start.8 = (bf16[4,8,1024]{2,1,0:T(8,128)(2,1)S(1)}, bf16[4,8,1024]{2,1,0:T(8,128)(2,1)S(1)}, u32[]{:S(2)}, u32[]{:S(2)}) collective-permute-start(bf16[4,8,1024]{2,1,0:T(8,128)(2,1)S(1)} %collective-permute-done.7.refs_9_), channel_id=1, source_target_pairs={{0,2},{2,0},{4,6},{6,4},{8,10},{10,8},{12,14},{14,12},{16,18},{18,... | collective-permute-start | bytes 196616 | tf_op jit(solution)/shard_map/ppermute | solution.py:291
  14.6 3.9 %collective-permute-start.14 = (bf16[4,8,1024]{2,1,0:T(8,128)(2,1)S(1)}, bf16[4,8,1024]{2,1,0:T(8,128)(2,1)S(1)}, u32[]{:S(2)}, u32[]{:S(2)}) collective-permute-start(bf16[4,8,1024]{2,1,0:T(8,128)(2,1)S(1)} %collective-permute-done.13.refs_15_), channel_id=1, source_target_pairs={{0,2},{2,0},{4,6},{6,4},{8,10},{10,8},{12,14},{14,12},{16,18},{18,... | collective-permute-start | bytes 196616 | tf_op jit(solution)/shard_map/ppermute | solution.py:291
  14.6 4.5 %collective-permute-start.3 = (bf16[4,8,1024]{2,1,0:T(8,128)(2,1)S(1)}, bf16[4,8,1024]{2,1,0:T(8,128)(2,1)}, u32[]{:S(2)}, u32[]{:S(2)}) collective-permute-start(bf16[4,8,1024]{2,1,0:T(8,128)(2,1)S(1)} %collective-permute-done.2.refs_5_), channel_id=1, source_target_pairs={{0,2},{2,0},{4,6},{6,4},{8,10},{10,8},{12,14},{14,12},{16,18},{18,... | collective-permute-start | bytes 196616 | tf_op jit(solution)/shard_map/ppermute | solution.py:291
  17.1 2.0 %collective-permute-start.4 = (bf16[4,8,1024]{2,1,0:T(8,128)(2,1)S(1)}, bf16[4,8,1024]{2,1,0:T(8,128)(2,1)}, u32[]{:S(2)}, u32[]{:S(2)}) collective-permute-start(bf16[4,8,1024]{2,1,0:T(8,128)(2,1)S(1)} %collective-permute-done.1.refs_3_), channel_id=1, source_target_pairs={{0,2},{2,0},{4,6},{6,4},{8,10},{10,8},{12,14},{14,12},{16,18},{18,... | collective-permute-start | bytes 196616 | tf_op jit(solution)/shard_map/ppermute | solution.py:291
  18.0 1.4 %collective-permute-start.6 = (bf16[4,8,1024]{2,1,0:T(8,128)(2,1)S(1)}, bf16[4,8,1024]{2,1,0:T(8,128)(2,1)}, u32[]{:S(2)}, u32[]{:S(2)}) collective-permute-start(bf16[4,8,1024]{2,1,0:T(8,128)(2,1)S(1)} %collective-permute-done.5.refs_7_), channel_id=1, source_target_pairs={{0,2},{2,0},{4,6},{6,4},{8,10},{10,8},{12,14},{14,12},{16,18},{18,... | collective-permute-start | bytes 196616 | tf_op jit(solution)/shard_map/ppermute | solution.py:291
  18.0 1.5 %collective-permute-start.11 = (bf16[4,8,1024]{2,1,0:T(8,128)(2,1)S(1)}, bf16[4,8,1024]{2,1,0:T(8,128)(2,1)}, u32[]{:S(2)}, u32[]{:S(2)}) collective-permute-start(bf16[4,8,1024]{2,1,0:T(8,128)(2,1)S(1)} %collective-permute-done.10.refs_13_), channel_id=1, source_target_pairs={{0,2},{2,0},{4,6},{6,4},{8,10},{10,8},{12,14},{14,12},{16,18},{18,... | collective-permute-start | bytes 196616 | tf_op jit(solution)/shard_map/ppermute | solution.py:291
  18.5 1.4 %collective-permute-start.12 = (bf16[4,8,1024]{2,1,0:T(8,128)(2,1)S(1)}, bf16[4,8,1024]{2,1,0:T(8,128)(2,1)}, u32[]{:S(2)}, u32[]{:S(2)}) collective-permute-start(bf16[4,8,1024]{2,1,0:T(8,128)(2,1)S(1)} %collective-permute-done.9.refs_11_), channel_id=1, source_target_pairs={{0,2},{2,0},{4,6},{6,4},{8,10},{10,8},{12,14},{14,12},{16,18},{18,... | collective-permute-start | bytes 196616 | tf_op jit(solution)/shard_map/ppermute | solution.py:291
  21.3 4.0 %collective-permute-start.15 = (bf16[136,128]{1,0:T(8,128)(2,1)S(1)}, bf16[136,128]{1,0:T(8,128)(2,1)S(1)}, u32[]{:S(2)}, u32[]{:S(2)}) collective-permute-start(bf16[136,128]{1,0:T(8,128)(2,1)S(1)} %shard_map.49), channel_id=1, source_target_pairs={{0,1},{1,0},{2,3},{3,2},{4,5},{5,4},{6,7},{7,6},{8,9},{9,8},{10,11... | collective-permute-start | bytes 104456 | tf_op jit(solution)/shard_map/ppermute | solution.py:365

commit v8 on v7

--- a/solution.py
+++ b/solution.py
@@ -256,7 +256,7 @@
     me = me_ref[0]
     block = (lane // own) ^ me
     crossed = (block & ~6) | ((block & 2) << 1) | ((block & 4) >> 1)
-    block = jnp.where((me & 1) != 0, crossed, block)
+    block = jnp.where(((me & 1) != 0) & (block > 7), crossed, block)
     index = block * own + lane % own
     value = jnp.take_along_axis(value, index, axis=1)
     for lag in range(lags):
@@ -277,7 +277,8 @@
     far = held[1:]
     plan += [(m | cross, 0, m | cross, m | cross) for m in held]
     for m in held:
-        plan += [(m | SIDE, m, SIDE, NEAR), (m | NEAR, m, NEAR, SIDE)]
+        a, b = (NEAR, SIDE) if m else (SIDE, NEAR)
+        plan += [(m | SIDE, m, SIDE, a), (m | NEAR, m, NEAR, b)]
     mates = [0, cross] + far + [SIDE, NEAR]
     for m in far:
         mates += [m | SIDE, m | cross, m | NEAR]
@@ -289,7 +290,7 @@
     for block, source, even, odd in gather_plan(col):
         pairs = [(i, i ^ (odd if i & 1 else even)) for i in range(col)]
         blocks[block] = lax.ppermute(blocks[source], "col", pairs)
-    order = [m ^ (6 if m & 1 and (m & 6) in (SIDE, NEAR) else 0) for m in range(col)]
+    order = [m ^ (6 if m & 1 and (m & 6) in (SIDE, NEAR) and m > 7 else 0) for m in range(col)]
     return [blocks[m] for m in order]
 
 

time: 26.3 us -> 26.3 us (level)
  starting transfers between devices: 13.7 us -> 14.4 us
  waiting for transfers between devices: 6.88 us -> 6.18 us
    ppermute x15, waiting for transfers between devices: 5.87 us -> 5.19 us  [gather(): blocks[block] = lax.ppermute(blocks[source], 'col', pairs)]
    ppermute x15, starting transfers between devices: 12.2 us -> 12.8 us  [gather(): blocks[block] = lax.ppermute(blocks[source], 'col', pairs)]
  transfers between devices with their start and end apart: 16 -> 16, of which waited for: 8 -> 7; matrix products, arithmetic and copies ran while one was open for 0% -> 0% of each run, Pallas kernels for 8% -> 8%
where the time goes in v8:
time: 26.3 us; the launch traced here: 26 us
  starting transfers between devices  14.4 us (55%)
  waiting for transfers between devices  6.18 us (23%)
  Pallas kernels  5.39 us (20%)
    ppermute x15, starting transfers between devices, gather(): blocks[block] = lax.ppermute(blocks[source], 'col', pairs)  12.8 us
    ppermute x15, waiting for transfers between devices, gather(): blocks[block] = lax.ppermute(blocks[source], 'col', pairs)  5.19 us
    pallas_call x2, Pallas kernels, multiply(): pl.pallas_call(kernel, out_shape=jax.ShapeDtypeStruct((rows, lanes), dtyp...  2.88 us
    ppermute x1, starting transfers between devices, fast_body(): got = lax.ppermute(send, 'seg', [(0, 1), (1, 0)])  1.56 us
    pallas_call x1, Pallas kernels, fast_body(): pl.pallas_call(whiten_kernel, out_shape=[jax.ShapeDtypeStruct(traces.shap...  1.25 us
    ppermute x1, waiting for transfers between devices, fast_body(): got = lax.ppermute(send, 'seg', [(0, 1), (1, 0)])  1 us
    pallas_call x1, Pallas kernels, fast_body(): pl.pallas_call(functools.partial(finish_kernel, scale, own), out_shape=ja...  0.73 us
    pallas_call x1, Pallas kernels, fast_body(): pl.pallas_call(rotate_kernel, out_shape=jax.ShapeDtypeStruct((segs, 2 * r...  0.53 us
  transfers between devices with their start and end apart: 16, of which 7 were waited for; matrix products, arithmetic and copies ran while one was open for 0% of the time, Pallas kernels for 8%

profile of v8, /device:TPU:0, one launch (start us, length us, event | category | flops | bytes accessed | tf_op | source)
XLA Modules:
  0.0 26.0 jit_solution(15619504616421264813)
XLA Ops:
  0.0 1.2 %shard_map.46 = (bf16[4,8,1024]{2,1,0:T(8,128)(2,1)S(1)}, f32[136,512]{1,0:T(8,128)S(1)}, f32[136,512]{1,0:T(8,128)S(1)}) custom-call(bf16[4,8,1024]{2,1,0:T(8,128)(2,1)} %x_in.1, s32[4,8]{1,0:T(4,128)} %v_in.1, f32[136,512]{1,0:T(8,128)} %constant.12.clone.c_in, f32[136,512]{1,0:T(8,128)} %constant.13.clone.s_in), custom_call_target="tpu_custom_call" | custom-call | tf_op jit(solution)/shard_map/pallas_call | solution.py:312
  1.3 4.1 %collective-permute-start.7 = (bf16[4,8,1024]{2,1,0:T(8,128)(2,1)S(1)}, bf16[4,8,1024]{2,1,0:T(8,128)(2,1)S(1)}, u32[]{:S(2)}, u32[]{:S(2)}) collective-permute-start(bf16[4,8,1024]{2,1,0:T(8,128)(2,1)S(1)} %get-tuple-element.8.w_ref.refs_1_), channel_id=1, source_target_pairs={{0,16},{2,18},{4,20},{6,22},{8,24},{10,26},{12,28},{14,30},{16,0},... | collective-permute-start | bytes 196616 | tf_op jit(solution)/shard_map/ppermute | solution.py:292
  5.4 2.3 %collective-permute-start.13 = (bf16[4,8,1024]{2,1,0:T(8,128)(2,1)S(1)}, bf16[4,8,1024]{2,1,0:T(8,128)(2,1)S(1)}, u32[]{:S(2)}, u32[]{:S(2)}) collective-permute-start(bf16[4,8,1024]{2,1,0:T(8,128)(2,1)S(1)} %get-tuple-element.8.w_ref.refs_1_), channel_id=1, source_target_pairs={{0,28},{2,30},{4,24},{6,26},{8,20},{10,22},{12,16},{14,18},{16,12}... | collective-permute-start | bytes 196616 | tf_op jit(solution)/shard_map/ppermute | solution.py:292
  7.7 0.5 %collective-permute-start.1 = (bf16[4,8,1024]{2,1,0:T(8,128)(2,1)S(1)}, bf16[4,8,1024]{2,1,0:T(8,128)(2,1)S(1)}, u32[]{:S(2)}, u32[]{:S(2)}) collective-permute-start(bf16[4,8,1024]{2,1,0:T(8,128)(2,1)S(1)} %get-tuple-element.8.w_ref.refs_1_), channel_id=1, source_target_pairs={{0,4},{2,6},{4,0},{6,2},{8,12},{10,14},{12,8},{14,10},{16,20},{18,... | collective-permute-start | bytes 196616 | tf_op jit(solution)/shard_map/ppermute | solution.py:292
  8.2 0.3 %collective-permute-start.3 = (bf16[4,8,1024]{2,1,0:T(8,128)(2,1)S(1)}, bf16[4,8,1024]{2,1,0:T(8,128)(2,1)S(1)}, u32[]{:S(2)}, u32[]{:S(2)}) collective-permute-start(bf16[4,8,1024]{2,1,0:T(8,128)(2,1)S(1)} %get-tuple-element.8.w_ref.refs_1_), channel_id=1, source_target_pairs={{0,8},{2,10},{4,12},{6,14},{8,0},{10,2},{12,4},{14,6},{16,24},{18,... | collective-permute-start | bytes 196616 | tf_op jit(solution)/shard_map/ppermute | solution.py:292
  8.5 2.7 %collective-permute-start.5 = (bf16[4,8,1024]{2,1,0:T(8,128)(2,1)S(1)}, bf16[4,8,1024]{2,1,0:T(8,128)(2,1)S(1)}, u32[]{:S(2)}, u32[]{:S(2)}) collective-permute-start(bf16[4,8,1024]{2,1,0:T(8,128)(2,1)S(1)} %get-tuple-element.8.w_ref.refs_1_), channel_id=1, source_target_pairs={{0,12},{2,14},{4,8},{6,10},{8,4},{10,6},{12,0},{14,2},{16,28},{18,... | collective-permute-start | bytes 196616 | tf_op jit(solution)/shard_map/ppermute | solution.py:292
  11.2 0.0 collective-permute-done.7.refs_9_
  11.2 0.0 collective-permute-start
  11.2 1.6 %collective-permute-done.13.refs_15_ = bf16[4,8,1024]{2,1,0:T(8,128)(2,1)S(1)} collective-permute-done((bf16[4,8,1024]{2,1,0:T(8,128)(2,1)S(1)}, bf16[4,8,1024]{2,1,0:T(8,128)(2,1)S(1)}, u32[]{:S(2)}, u32[]{:S(2)}) %collective-permute-start.13) | collective-permute-done | bytes 65568 | tf_op jit(solution)/shard_map/ppermute | solution.py:292
  12.8 0.8 %collective-permute-start.10 = (bf16[4,8,1024]{2,1,0:T(8,128)(2,1)S(1)}, bf16[4,8,1024]{2,1,0:T(8,128)(2,1)S(1)}, u32[]{:S(2)}, u32[]{:S(2)}) collective-permute-start(bf16[4,8,1024]{2,1,0:T(8,128)(2,1)S(1)} %collective-permute-done.7.refs_9_), channel_id=1, source_target_pairs={{0,8},{2,6},{4,12},{6,2},{8,0},{10,14},{12,4},{14,10},{16,24},{18,... | collective-permute-start | bytes 196616 | tf_op jit(solution)/shard_map/ppermute | solution.py:292
  13.7 0.0 collective-permute-done.1.refs_3_
  13.7 0.9 %collective-permute-start.9 = (bf16[4,8,1024]{2,1,0:T(8,128)(2,1)S(1)}, bf16[4,8,1024]{2,1,0:T(8,128)(2,1)S(1)}, u32[]{:S(2)}, u32[]{:S(2)}) collective-permute-start(bf16[4,8,1024]{2,1,0:T(8,128)(2,1)S(1)} %collective-permute-done.7.refs_9_), channel_id=1, source_target_pairs={{0,4},{2,10},{4,0},{6,14},{8,12},{10,2},{12,8},{14,6},{16,20},{18,... | collective-permute-start | bytes 196616 | tf_op jit(solution)/shard_map/ppermute | solution.py:292
  14.6 0.0 collective-permute-done.3.refs_5_
  14.6 0.0 collective-permute-start.8
  14.6 0.0 collective-permute-done.5.refs_7_
  14.6 0.5 %collective-permute-start.14 = (bf16[4,8,1024]{2,1,0:T(8,128)(2,1)S(1)}, bf16[4,8,1024]{2,1,0:T(8,128)(2,1)S(1)}, u32[]{:S(2)}, u32[]{:S(2)}) collective-permute-start(bf16[4,8,1024]{2,1,0:T(8,128)(2,1)S(1)} %collective-permute-done.13.refs_15_), channel_id=1, source_target_pairs={{0,2},{2,0},{4,6},{6,4},{8,10},{10,8},{12,14},{14,12},{16,18},{18,... | collective-permute-start | bytes 196616 | tf_op jit(solution)/shard_map/ppermute | solution.py:292
  15.1 0.0 collective-permute-done.refs_2_
  15.1 0.1 collective-permute-start.2
  15.2 1.9 %collective-permute-done.10.refs_13_ = bf16[4,8,1024]{2,1,0:T(8,128)(2,1)S(1)} collective-permute-done((bf16[4,8,1024]{2,1,0:T(8,128)(2,1)S(1)}, bf16[4,8,1024]{2,1,0:T(8,128)(2,1)S(1)}, u32[]{:S(2)}, u32[]{:S(2)}) %collective-permute-start.10) | collective-permute-done | bytes 65568 | tf_op jit(solution)/shard_map/ppermute | solution.py:292
  17.1 0.0 collective-permute-start.4
  17.1 0.8 %collective-permute-done.9.refs_11_ = bf16[4,8,1024]{2,1,0:T(8,128)(2,1)S(1)} collective-permute-done((bf16[4,8,1024]{2,1,0:T(8,128)(2,1)S(1)}, bf16[4,8,1024]{2,1,0:T(8,128)(2,1)S(1)}, u32[]{:S(2)}, u32[]{:S(2)}) %collective-permute-start.9) | collective-permute-done | bytes 65568 | tf_op jit(solution)/shard_map/ppermute | solution.py:292
  17.9 0.0 collective-permute-start.6
  17.9 0.0 collective-permute-done.8.refs_10_
  17.9 0.5 %collective-permute-start.11 = (bf16[4,8,1024]{2,1,0:T(8,128)(2,1)S(1)}, bf16[4,8,1024]{2,1,0:T(8,128)(2,1)}, u32[]{:S(2)}, u32[]{:S(2)}) collective-permute-start(bf16[4,8,1024]{2,1,0:T(8,128)(2,1)S(1)} %collective-permute-done.10.refs_13_), channel_id=1, source_target_pairs={{0,2},{2,0},{4,6},{6,4},{8,10},{10,8},{12,14},{14,12},{16,18},{18,... | collective-permute-start | bytes 196616 | tf_op jit(solution)/shard_map/ppermute | solution.py:292
  18.4 0.0 collective-permute-done.14.refs_16_
  18.5 0.1 collective-permute-start.12
  18.5 0.5 %shard_map.47.refs_0_ = bf16[4,272,1024]{2,1,0:T(8,128)(2,1)S(1)} custom-call(s32[1]{0:T(128)} %bitcast.1.seg_ref, bf16[4,8,1024]{2,1,0:T(8,128)(2,1)S(1)} %get-tuple-element.8.w_ref.refs_1_, f32[136,512]{1,0:T(8,128)S(1)} %get-tuple-element.9.c_ref, f32[136,512]{1,0:T(8,128)S(1)} %get-tuple-element.10.s_ref), custom_call_target="tpu_custom_call" | custom-call | flops 6684672 | bytes 2228224 | tf_op jit(solution)/shard_map/pallas_call | solution.py:338
  19.1 0.0 collective-permute-done.2.refs_4_
  19.1 0.0 collective-permute-done.4.refs_6_
  19.1 0.2 collective-permute-done.6.refs_8_
  19.3 0.2 collective-permute-done.11.refs_12_
  19.5 0.4 %collective-permute-done.12.refs_14_ = bf16[4,8,1024]{2,1,0:T(8,128)(2,1)} collective-permute-done((bf16[4,8,1024]{2,1,0:T(8,128)(2,1)S(1)}, bf16[4,8,1024]{2,1,0:T(8,128)(2,1)}, u32[]{:S(2)}, u32[]{:S(2)}) %collective-permute-start.12) | collective-permute-done | bytes 65568 | tf_op jit(solution)/shard_map/ppermute | solution.py:292
  19.8 1.4 %shard_map.49 = bf16[136,128]{1,0:T(8,128)(2,1)S(1)} custom-call(bf16[4,272,1024]{2,1,0:T(8,128)(2,1)S(1)} %shard_map.47.refs_0_, bf16[4,8,1024]{2,1,0:T(8,128)(2,1)S(1)} %get-tuple-element.8.w_ref.refs_1_, bf16[4,8,1024]{2,1,0:T(8,128)(2,1)S(1)} %collective-permute-done.refs_2_, bf16[4,8,1024]{2,1,0:T(8,128)(2,1)S(1)} %collective-permute-done.1.refs_3_, ...), custom_call_target="tpu_custom_call" | custom-call | flops 142606336 | bytes 2162688 | tf_op jit(solution)/shard_map/pallas_call | solution.py:352
  21.3 1.6 %collective-permute-start.15 = (bf16[136,128]{1,0:T(8,128)(2,1)S(1)}, bf16[136,128]{1,0:T(8,128)(2,1)S(1)}, u32[]{:S(2)}, u32[]{:S(2)}) collective-permute-start(bf16[136,128]{1,0:T(8,128)(2,1)S(1)} %shard_map.49), channel_id=1, source_target_pairs={{0,1},{1,0},{2,3},{3,2},{4,5},{5,4},{6,7},{7,6},{8,9},{9,8},{10,11... | collective-permute-start | bytes 104456 | tf_op jit(solution)/shard_map/ppermute | solution.py:366
  22.8 1.4 %shard_map.48.keep_ref = f32[136,128]{1,0:T(8,128)S(1)} custom-call(bf16[4,272,1024]{2,1,0:T(8,128)(2,1)S(1)} %shard_map.47.refs_0_, bf16[4,8,1024]{2,1,0:T(8,128)(2,1)S(1)} %get-tuple-element.8.w_ref.refs_1_, bf16[4,8,1024]{2,1,0:T(8,128)(2,1)S(1)} %collective-permute-done.refs_2_, bf16[4,8,1024]{2,1,0:T(8,128)(2,1)S(1)} %collective-permute-done.1.refs_3_, ...), custom_call_target="tpu_custom_call" | custom-call | flops 142606336 | bytes 2162688 | tf_op jit(solution)/shard_map/pallas_call | solution.py:352
  24.3 1.0 %collective-permute-done.15.got_ref = bf16[136,128]{1,0:T(8,128)(2,1)S(1)} collective-permute-done((bf16[136,128]{1,0:T(8,128)(2,1)S(1)}, bf16[136,128]{1,0:T(8,128)(2,1)S(1)}, u32[]{:S(2)}, u32[]{:S(2)}) %collective-permute-start.15) | collective-permute-done | bytes 34848 | tf_op jit(solution)/shard_map/ppermute | solution.py:366
  25.3 0.7 %shard_map.50 = f32[33,4,128]{2,1,0:T(4,128)} custom-call(s32[1]{0:T(128)} %bitcast.me_ref, f32[136,128]{1,0:T(8,128)S(1)} %shard_map.48.keep_ref, bf16[136,128]{1,0:T(8,128)(2,1)S(1)} %collective-permute-done.15.got_ref), custom_call_target="tpu_custom_call" | custom-call | tf_op jit(solution)/shard_map/pallas_call | solution.py:368
Async XLA Ops:
  1.3 9.9 %collective-permute-start.7 = (bf16[4,8,1024]{2,1,0:T(8,128)(2,1)S(1)}, bf16[4,8,1024]{2,1,0:T(8,128)(2,1)S(1)}, u32[]{:S(2)}, u32[]{:S(2)}) collective-permute-start(bf16[4,8,1024]{2,1,0:T(8,128)(2,1)S(1)} %get-tuple-element.8.w_ref.refs_1_), channel_id=1, source_target_pairs={{0,16},{2,18},{4,20},{6,22},{8,24},{10,26},{12,28},{14,30},{16,0},... | collective-permute-start | bytes 196616 | tf_op jit(solution)/shard_map/ppermute | solution.py:292
  5.4 7.4 %collective-permute-start.13 = (bf16[4,8,1024]{2,1,0:T(8,128)(2,1)S(1)}, bf16[4,8,1024]{2,1,0:T(8,128)(2,1)S(1)}, u32[]{:S(2)}, u32[]{:S(2)}) collective-permute-start(bf16[4,8,1024]{2,1,0:T(8,128)(2,1)S(1)} %get-tuple-element.8.w_ref.refs_1_), channel_id=1, source_target_pairs={{0,28},{2,30},{4,24},{6,26},{8,20},{10,22},{12,16},{14,18},{16,12}... | collective-permute-start | bytes 196616 | tf_op jit(solution)/shard_map/ppermute | solution.py:292
  7.7 6.0 %collective-permute-start.1 = (bf16[4,8,1024]{2,1,0:T(8,128)(2,1)S(1)}, bf16[4,8,1024]{2,1,0:T(8,128)(2,1)S(1)}, u32[]{:S(2)}, u32[]{:S(2)}) collective-permute-start(bf16[4,8,1024]{2,1,0:T(8,128)(2,1)S(1)} %get-tuple-element.8.w_ref.refs_1_), channel_id=1, source_target_pairs={{0,4},{2,6},{4,0},{6,2},{8,12},{10,14},{12,8},{14,10},{16,20},{18,... | collective-permute-start | bytes 196616 | tf_op jit(solution)/shard_map/ppermute | solution.py:292
  8.2 6.4 %collective-permute-start.3 = (bf16[4,8,1024]{2,1,0:T(8,128)(2,1)S(1)}, bf16[4,8,1024]{2,1,0:T(8,128)(2,1)S(1)}, u32[]{:S(2)}, u32[]{:S(2)}) collective-permute-start(bf16[4,8,1024]{2,1,0:T(8,128)(2,1)S(1)} %get-tuple-element.8.w_ref.refs_1_), channel_id=1, source_target_pairs={{0,8},{2,10},{4,12},{6,14},{8,0},{10,2},{12,4},{14,6},{16,24},{18,... | collective-permute-start | bytes 196616 | tf_op jit(solution)/shard_map/ppermute | solution.py:292
  8.5 6.1 %collective-permute-start.5 = (bf16[4,8,1024]{2,1,0:T(8,128)(2,1)S(1)}, bf16[4,8,1024]{2,1,0:T(8,128)(2,1)S(1)}, u32[]{:S(2)}, u32[]{:S(2)}) collective-permute-start(bf16[4,8,1024]{2,1,0:T(8,128)(2,1)S(1)} %get-tuple-element.8.w_ref.refs_1_), channel_id=1, source_target_pairs={{0,12},{2,14},{4,8},{6,10},{8,4},{10,6},{12,0},{14,2},{16,28},{18,... | collective-permute-start | bytes 196616 | tf_op jit(solution)/shard_map/ppermute | solution.py:292
  11.2 3.9 %collective-permute-start = (bf16[4,8,1024]{2,1,0:T(8,128)(2,1)S(1)}, bf16[4,8,1024]{2,1,0:T(8,128)(2,1)S(1)}, u32[]{:S(2)}, u32[]{:S(2)}) collective-permute-start(bf16[4,8,1024]{2,1,0:T(8,128)(2,1)S(1)} %get-tuple-element.8.w_ref.refs_1_), channel_id=1, source_target_pairs={{0,2},{2,0},{4,6},{6,4},{8,10},{10,8},{12,14},{14,12},{16,18},{18,... | collective-permute-start | bytes 196616 | tf_op jit(solution)/shard_map/ppermute | solution.py:292
  12.8 4.3 %collective-permute-start.10 = (bf16[4,8,1024]{2,1,0:T(8,128)(2,1)S(1)}, bf16[4,8,1024]{2,1,0:T(8,128)(2,1)S(1)}, u32[]{:S(2)}, u32[]{:S(2)}) collective-permute-start(bf16[4,8,1024]{2,1,0:T(8,128)(2,1)S(1)} %collective-permute-done.7.refs_9_), channel_id=1, source_target_pairs={{0,8},{2,6},{4,12},{6,2},{8,0},{10,14},{12,4},{14,10},{16,24},{18,... | collective-permute-start | bytes 196616 | tf_op jit(solution)/shard_map/ppermute | solution.py:292
  13.7 4.3 %collective-permute-start.9 = (bf16[4,8,1024]{2,1,0:T(8,128)(2,1)S(1)}, bf16[4,8,1024]{2,1,0:T(8,128)(2,1)S(1)}, u32[]{:S(2)}, u32[]{:S(2)}) collective-permute-start(bf16[4,8,1024]{2,1,0:T(8,128)(2,1)S(1)} %collective-permute-done.7.refs_9_), channel_id=1, source_target_pairs={{0,4},{2,10},{4,0},{6,14},{8,12},{10,2},{12,8},{14,6},{16,20},{18,... | collective-permute-start | bytes 196616 | tf_op jit(solution)/shard_map/ppermute | solution.py:292
  14.6 3.4 %collective-permute-start.8 = (bf16[4,8,1024]{2,1,0:T(8,128)(2,1)S(1)}, bf16[4,8,1024]{2,1,0:T(8,128)(2,1)S(1)}, u32[]{:S(2)}, u32[]{:S(2)}) collective-permute-start(bf16[4,8,1024]{2,1,0:T(8,128)(2,1)S(1)} %collective-permute-done.7.refs_9_), channel_id=1, source_target_pairs={{0,2},{2,0},{4,6},{6,4},{8,10},{10,8},{12,14},{14,12},{16,18},{18,... | collective-permute-start | bytes 196616 | tf_op jit(solution)/shard_map/ppermute | solution.py:292
  14.6 3.9 %collective-permute-start.14 = (bf16[4,8,1024]{2,1,0:T(8,128)(2,1)S(1)}, bf16[4,8,1024]{2,1,0:T(8,128)(2,1)S(1)}, u32[]{:S(2)}, u32[]{:S(2)}) collective-permute-start(bf16[4,8,1024]{2,1,0:T(8,128)(2,1)S(1)} %collective-permute-done.13.refs_15_), channel_id=1, source_target_pairs={{0,2},{2,0},{4,6},{6,4},{8,10},{10,8},{12,14},{14,12},{16,18},{18,... | collective-permute-start | bytes 196616 | tf_op jit(solution)/shard_map/ppermute | solution.py:292
  15.1 4.0 %collective-permute-start.2 = (bf16[4,8,1024]{2,1,0:T(8,128)(2,1)S(1)}, bf16[4,8,1024]{2,1,0:T(8,128)(2,1)}, u32[]{:S(2)}, u32[]{:S(2)}) collective-permute-start(bf16[4,8,1024]{2,1,0:T(8,128)(2,1)S(1)} %collective-permute-done.1.refs_3_), channel_id=1, source_target_pairs={{0,2},{2,0},{4,6},{6,4},{8,10},{10,8},{12,14},{14,12},{16,18},{18,... | collective-permute-start | bytes 196616 | tf_op jit(solution)/shard_map/ppermute | solution.py:292
  17.1 2.0 %collective-permute-start.4 = (bf16[4,8,1024]{2,1,0:T(8,128)(2,1)S(1)}, bf16[4,8,1024]{2,1,0:T(8,128)(2,1)}, u32[]{:S(2)}, u32[]{:S(2)}) collective-permute-start(bf16[4,8,1024]{2,1,0:T(8,128)(2,1)S(1)} %collective-permute-done.3.refs_5_), channel_id=1, source_target_pairs={{0,2},{2,0},{4,6},{6,4},{8,10},{10,8},{12,14},{14,12},{16,18},{18,... | collective-permute-start | bytes 196616 | tf_op jit(solution)/shard_map/ppermute | solution.py:292
  17.9 1.4 %collective-permute-start.6 = (bf16[4,8,1024]{2,1,0:T(8,128)(2,1)S(1)}, bf16[4,8,1024]{2,1,0:T(8,128)(2,1)}, u32[]{:S(2)}, u32[]{:S(2)}) collective-permute-start(bf16[4,8,1024]{2,1,0:T(8,128)(2,1)S(1)} %collective-permute-done.5.refs_7_), channel_id=1, source_target_pairs={{0,2},{2,0},{4,6},{6,4},{8,10},{10,8},{12,14},{14,12},{16,18},{18,... | collective-permute-start | bytes 196616 | tf_op jit(solution)/shard_map/ppermute | solution.py:292
  17.9 1.5 %collective-permute-start.11 = (bf16[4,8,1024]{2,1,0:T(8,128)(2,1)S(1)}, bf16[4,8,1024]{2,1,0:T(8,128)(2,1)}, u32[]{:S(2)}, u32[]{:S(2)}) collective-permute-start(bf16[4,8,1024]{2,1,0:T(8,128)(2,1)S(1)} %collective-permute-done.10.refs_13_), channel_id=1, source_target_pairs={{0,2},{2,0},{4,6},{6,4},{8,10},{10,8},{12,14},{14,12},{16,18},{18,... | collective-permute-start | bytes 196616 | tf_op jit(solution)/shard_map/ppermute | solution.py:292
  18.5 1.4 %collective-permute-start.12 = (bf16[4,8,1024]{2,1,0:T(8,128)(2,1)S(1)}, bf16[4,8,1024]{2,1,0:T(8,128)(2,1)}, u32[]{:S(2)}, u32[]{:S(2)}) collective-permute-start(bf16[4,8,1024]{2,1,0:T(8,128)(2,1)S(1)} %collective-permute-done.9.refs_11_), channel_id=1, source_target_pairs={{0,2},{2,0},{4,6},{6,4},{8,10},{10,8},{12,14},{14,12},{16,18},{18,... | collective-permute-start | bytes 196616 | tf_op jit(solution)/shard_map/ppermute | solution.py:292
  21.3 4.0 %collective-permute-start.15 = (bf16[136,128]{1,0:T(8,128)(2,1)S(1)}, bf16[136,128]{1,0:T(8,128)(2,1)S(1)}, u32[]{:S(2)}, u32[]{:S(2)}) collective-permute-start(bf16[136,128]{1,0:T(8,128)(2,1)S(1)} %shard_map.49), channel_id=1, source_target_pairs={{0,1},{1,0},{2,3},{3,2},{4,5},{5,4},{6,7},{7,6},{8,9},{9,8},{10,11... | collective-permute-start | bytes 104456 | tf_op jit(solution)/shard_map/ppermute | solution.py:366
